TPU v7x, 128 devices: a whole 4x4x4 slice. The times are simulated.
128 devices in a mesh: ctx: 32 (over x, z, core), own: 4 (over y).
Axes of the slice: x: 4, y: 4, z: 4, core: 2. Of those that a mesh axis runs over, the one named last changes fastest.
Arguments:
- query_proj: bfloat16 [16384, 8192], P(('ctx', 'own')), may hold values from -6 to 6
- key_proj: bfloat16 [16384, 8192], P(('ctx', 'own')), may hold values from -6 to 6
- value_proj: bfloat16 [16384, 8192], P(('ctx', 'own')), may hold values from -6 to 6
- short_taps: float32 [3, 7, 512], P(None, None, 'own'), may hold values from -2 to 2
- long_taps: float32 [128, 512], P(None, 'own'), may hold values from -0.5 to 0.5
- decay_rate: float32 [8, 8192], P(None, 'own'), may hold values from 3.0517579e-06 to 0.03
- residues: float32 [8, 8192], P(None, 'own'), may hold values from -2 to 2
- grad_out: bfloat16 [16384, 8192], P(('ctx', 'own')), may hold values from -6 to 6
Outputs:
- layer_out: bfloat16 [16384, 8192], P(('ctx', 'own'))
- grad_query: bfloat16 [16384, 8192], P(('ctx', 'own'))
- grad_key: bfloat16 [16384, 8192], P(('ctx', 'own'))
- grad_value: bfloat16 [16384, 8192], P(('ctx', 'own'))
- grad_long_taps: float32 [128, 512], P(None, 'own')
All inputs are finite; a program needn't handle non-finite values.
Results may differ from a plain program's by a relative error of at most 0.02.
Values may be sent and summed in bfloat16 or wider, within the bound.
No kernel may reach another device: no remote copies, remote signals or barrier semaphores. Data moves between devices by JAX's collectives and lax.ppermute only.
A program may use at most 256 MiB of HBM per device.

v0:
```python
import math

import jax
import jax.numpy as jnp
from jax import lax
from jax.sharding import PartitionSpec as P

CPG = 16


exact_mode = lax.Precision.HIGHEST


def from_behind(value, axis, steps):
    count = lax.axis_size(axis)
    leading, last = (max(0, -steps), min(count, count - steps))
    return lax.ppermute(value, axis, [(source, source + steps) for source in range(leading, last)])


def carried_in(x, axis, combine, identity, reverse):
    size, index = (lax.axis_size(axis), lax.axis_index(axis))
    everything = jax.tree.map(
        lambda part, kind: lax.all_gather(part.astype(kind), axis), x, (jnp.bfloat16, jnp.bfloat16)
    )
    start = jax.tree.map(
        lambda part, zero: jnp.broadcast_to(jnp.asarray(zero, part.dtype), part.shape), x, identity
    )

    def hop(k, before):
        at = size - 1 - k if reverse else k
        reached = at > index if reverse else at < index
        new = combine(
            before, jax.tree.map(lambda part, own: part[at].astype(own.dtype), everything, x)
        )
        return jax.tree.map(lambda a, b: jnp.where(reached, a, b), new, before)

    return lax.fori_loop(0, size, hop, start)


def tables(row_count):
    bin_count = row_count + 1
    freq_index = jnp.arange(bin_count, dtype=jnp.int32)[:, None]
    place_index = jnp.arange(row_count, dtype=jnp.int32)[None, :]
    phase_index = freq_index * place_index % (2 * row_count)
    angle_all = phase_index.astype(jnp.float32) * (math.pi / row_count)
    cos_fwd = jnp.cos(angle_all)
    sin_fwd = jnp.sin(angle_all)
    at_edge = jnp.logical_or(freq_index == 0, freq_index == row_count)
    weight_bin = jnp.where(at_edge, 1.0, 2.0).astype(jnp.float32) / (2.0 * row_count)
    cos_inv = jnp.transpose(cos_fwd * weight_bin)
    sin_inv = jnp.transpose(sin_fwd * weight_bin)
    parity = (1 - 2 * (freq_index % 2)).astype(jnp.float32)
    return (cos_fwd, sin_fwd, cos_inv, sin_inv, parity)


def transform(table_set, rows_in):
    values = rows_in.astype(jnp.float32)
    real_part = jnp.dot(
        table_set[0], values, precision=exact_mode, preferred_element_type=jnp.float32
    )
    imag_part = -jnp.dot(
        table_set[1], values, precision=exact_mode, preferred_element_type=jnp.float32
    )
    return (real_part, imag_part)


def restore(table_set, real_part, imag_part):
    first = jnp.dot(
        table_set[2], real_part, precision=exact_mode, preferred_element_type=jnp.float32
    )
    return first - jnp.dot(
        table_set[3], imag_part, precision=exact_mode, preferred_element_type=jnp.float32
    )


def featurize(rim_part, main_rows, taps_chan):
    joined = jnp.concatenate([rim_part, main_rows], axis=0).astype(jnp.float32)
    row_count = main_rows.shape[0]
    tap_count = taps_chan.shape[0]
    summed = jnp.zeros(main_rows.shape, jnp.float32)
    for offset in range(tap_count):
        first_row = tap_count - 1 - offset
        summed = summed + taps_chan[offset][None, :] * joined[first_row : first_row + row_count]
    return summed.astype(jnp.bfloat16)


def unfeaturize(main_rows, rim_part, taps_chan):
    joined = jnp.concatenate([main_rows, rim_part], axis=0).astype(jnp.float32)
    row_count = main_rows.shape[0]
    tap_count = taps_chan.shape[0]
    summed = jnp.zeros(main_rows.shape, jnp.float32)
    for offset in range(tap_count):
        summed = summed + taps_chan[offset][None, :] * joined[offset : offset + row_count]
    return summed.astype(jnp.bfloat16)


def spread(spectrum):
    bin_count, group_count = spectrum.shape
    return jnp.broadcast_to(spectrum[:, :, None], (bin_count, group_count, CPG)).reshape(
        bin_count, group_count * CPG
    )


def modal_weight(decay, resid):
    return resid * jnp.sqrt(-jnp.expm1(-2.0 * decay))


def pole_rows(coeff, decay, lag_rows, scaling):
    summed = jnp.zeros((lag_rows.shape[0], decay.shape[1]), jnp.float32)
    for pole in range(decay.shape[0]):
        summed = summed + (coeff[pole] * scaling[pole])[None, :] * jnp.exp(
            -decay[pole][None, :] * lag_rows[:, None]
        )
    return summed


def pole_states(decay, lag_rows, field):
    states = []
    for pole in range(decay.shape[0]):
        states.append(jnp.sum(jnp.exp(-decay[pole][None, :] * lag_rows[:, None]) * field, axis=0))
    return jnp.stack(states)


def shards(query_proj, key_proj, value_proj, short_taps, long_taps, decay_rate, residues, grad_out):
    row_count, chan_count = query_proj.shape
    rim_rows = short_taps.shape[1] - 1
    table_set = tables(row_count)
    parity = table_set[4]
    lag_index = jnp.arange(row_count, dtype=jnp.float32)
    weight = modal_weight(decay_rate, residues)
    head_rows = pole_rows(weight, decay_rate, lag_index, jnp.ones_like(weight))
    head_re, head_im = transform(table_set, head_rows)
    taps_re, taps_im = transform(table_set, long_taps)
    head_all, taps_all, decay_all, resid_all, short_all = (
        lax.all_gather(jnp.stack([head_re, head_im]), "own", axis=2, tiled=True),
        lax.all_gather(jnp.stack([taps_re, taps_im]), "own", axis=2, tiled=True),
        lax.all_gather(decay_rate, "own", axis=1, tiled=True),
        lax.all_gather(residues, "own", axis=1, tiled=True),
        lax.all_gather(short_taps, "own", axis=2, tiled=True),
    )
    head_re, head_im = (head_all[0], head_all[1])
    edge_re, edge_im = (spread(taps_all[0]), spread(taps_all[1]))
    tap_count = short_all.shape[1]
    group_count = short_all.shape[2]
    short_chan = jnp.broadcast_to(
        short_all[:, :, :, None], (3, tap_count, group_count, CPG)
    ).reshape(3, tap_count, group_count * CPG)
    weight_all = modal_weight(decay_all, resid_all)
    block_rate = decay_all * row_count

    def chain_pair(earlier_pair, later_pair):
        return (
            earlier_pair[0] + later_pair[0],
            jnp.exp(-block_rate * later_pair[0]) * earlier_pair[1] + later_pair[1],
        )

    identity = (jnp.zeros((), jnp.float32), jnp.zeros_like(block_rate))
    one_block = jnp.ones((), jnp.float32)
    rim_set = from_behind(
        (
            query_proj[row_count - rim_rows :],
            key_proj[row_count - rim_rows :],
            value_proj[row_count - rim_rows :],
        ),
        ("ctx", "own"),
        1,
    )
    query_feat = featurize(rim_set[0], query_proj, short_chan[0])
    key_feat = featurize(rim_set[1], key_proj, short_chan[1])
    value_feat = featurize(rim_set[2], value_proj, short_chan[2])
    product = (key_feat.astype(jnp.float32) * value_feat.astype(jnp.float32)).astype(jnp.bfloat16)
    earlier = from_behind(product, ("ctx", "own"), 1)
    product_float = product.astype(jnp.float32)
    block_state = pole_states(decay_all, row_count - 1 - lag_index, product_float)
    state_in = carried_in((one_block, block_state), ("ctx", "own"), chain_pair, identity, False)[1]
    prev_re, prev_im = transform(table_set, earlier)
    own_re, own_im = transform(table_set, product)
    own_re = parity * own_re
    own_im = parity * own_im
    win_re = prev_re + own_re
    win_im = prev_im + own_im
    out_re = win_re * edge_re - win_im * edge_im + own_re * head_re - own_im * head_im
    out_im = win_re * edge_im + win_im * edge_re + own_re * head_im + own_im * head_re
    near_part = restore(table_set, parity * out_re, parity * out_im)
    far_part = pole_rows(weight_all, decay_all, lag_index + 1.0, state_in)
    long_conv = near_part + far_part
    layer_out = (query_feat.astype(jnp.float32) * long_conv).astype(jnp.bfloat16)
    grad_float = grad_out.astype(jnp.float32)
    grad_conv = (grad_float * query_feat.astype(jnp.float32)).astype(jnp.bfloat16)
    grad_qfeat = (grad_float * long_conv).astype(jnp.bfloat16)
    next_grad = from_behind(grad_conv, ("ctx", "own"), -1)
    conv_float = grad_conv.astype(jnp.float32)
    back_state = pole_states(decay_all, lag_index, conv_float)
    state_after = carried_in((one_block, back_state), ("ctx", "own"), chain_pair, identity, True)[1]
    cur_re, cur_im = transform(table_set, grad_conv)
    nxt_re, nxt_im = transform(table_set, next_grad)
    gwin_re = cur_re + parity * nxt_re
    gwin_im = cur_im + parity * nxt_im
    back_re = gwin_re * edge_re + gwin_im * edge_im + cur_re * head_re + cur_im * head_im
    back_im = gwin_im * edge_re - gwin_re * edge_im + cur_im * head_re - cur_re * head_im
    near_back = restore(table_set, back_re, back_im)
    far_back = pole_rows(weight_all, decay_all, row_count - lag_index, state_after)
    grad_prod = near_back + far_back
    grad_kfeat = (grad_prod * value_feat.astype(jnp.float32)).astype(jnp.bfloat16)
    grad_vfeat = (grad_prod * key_feat.astype(jnp.float32)).astype(jnp.bfloat16)
    back_rims = from_behind(
        (grad_qfeat[:rim_rows], grad_kfeat[:rim_rows], grad_vfeat[:rim_rows]), ("ctx", "own"), -1
    )
    grad_query = unfeaturize(grad_qfeat, back_rims[0], short_chan[0])
    grad_key = unfeaturize(grad_kfeat, back_rims[1], short_chan[1])
    grad_value = unfeaturize(grad_vfeat, back_rims[2], short_chan[2])
    corr_re = parity * (cur_re * win_re + cur_im * win_im)
    corr_im = parity * (cur_im * win_re - cur_re * win_im)
    bin_count = corr_re.shape[0]
    all_groups = chan_count // CPG
    corr_re = corr_re.reshape(bin_count, all_groups, CPG).sum(axis=2)
    corr_im = corr_im.reshape(bin_count, all_groups, CPG).sum(axis=2)
    seq_total = row_count * lax.axis_size("ctx") * lax.axis_size("own")
    scale_taps = 1.0 / math.sqrt(seq_total * CPG)
    partial_taps = (
        jnp.dot(table_set[2], corr_re, precision=exact_mode, preferred_element_type=jnp.float32)
        - jnp.dot(table_set[3], corr_im, precision=exact_mode, preferred_element_type=jnp.float32)
    ) * scale_taps
    summed_taps = lax.psum(partial_taps, ("ctx", "own"))
    own_groups = all_groups // lax.axis_size("own")
    grad_taps = lax.dynamic_slice_in_dim(
        summed_taps, lax.axis_index("own") * own_groups, own_groups, 1
    )
    return (layer_out, grad_query, grad_key, grad_value, grad_taps)


def solution(mesh):
    placed = (
        P(("ctx", "own"), None),
        P(("ctx", "own"), None),
        P(("ctx", "own"), None),
        P(None, None, "own"),
        P(None, "own"),
        P(None, "own"),
        P(None, "own"),
        P(("ctx", "own"), None),
    )
    return jax.shard_map(
        shards,
        mesh=mesh,
        in_specs=placed,
        out_specs=(
            P(("ctx", "own"), None),
            P(("ctx", "own"), None),
            P(("ctx", "own"), None),
            P(("ctx", "own"), None),
            P(None, "own"),
        ),
        check_vma=False,
    )
```

profile of v0, /device:TPU:18, one launch (start us, length us, event | category | flops | bytes accessed | tf_op | source)
XLA Modules:
  0.0 1164.0 jit_solution(342298592889918397)
XLA Ops:
  8.1 1.6 slice.600
  9.7 3.2 collective-permute-start.2
  12.8 1.6 slice.578
  14.4 1.9 collective-permute-start.1
  16.4 1.6 slice.556
  18.0 2.8 collective-permute-start
  21.9 12.6 %all_gather.27 = f32[3,7,512]{2,1,0:T(8,128)S(1)} all-gather(f32[3,7,128]{2,1,0:T(8,128)} %param.15), channel_id=1, replica_groups=mesh['ctx'=32,'own'=4] {'own'}, dimensions={2}, use_global_device_ids=true | all-gather | bytes 53760 | tf_op jit(solution)/shard_map/all_gather | solution.py:139
  34.6 1.9 slice_negate_fusion.15
  36.5 12.5 %all_gather.31 = f32[8,8192]{1,0:T(8,128)S(1)} all-gather(f32[8,2048]{1,0:T(8,128)} %param.17), channel_id=1, replica_groups=mesh['ctx'=32,'own'=4] {'own'}, dimensions={1}, use_global_device_ids=true | all-gather | bytes 327680 | tf_op jit(solution)/shard_map/all_gather | solution.py:137
  56.3 1.8 maximum_convert_fusion
  58.1 1.6 maximum_convert_fusion.1
  59.8 1.6 maximum_convert_fusion.2
  61.8 24.6 %fusion.62 = (bf16[8192]{0:T(1024)(128)(2,1)}, bf16[8192]{0:T(1024)(128)(2,1)}, bf16[8192]{0:T(1024)(128)(2,1)}, bf16[8192]{0:T(1024)(128)(2,1)}, bf16[8192]{0:T...) fusion(f32[8192]{0:T(1024)S(1)} %bitcast.146, ...), kind=kLoop, calls=%fused_computation.101 | loop fusion | flops 104726528 | bytes 101876224 | tf_op jit(solution)/shard_map/reduce_sum | solution.py:120
  86.5 3.0 collective-permute-start.3
  89.6 3.7 convolution_bitcast_fusion
  93.3 3.6 fusion.105
  96.9 2.1 convolution_negate_fusion.1
  99.1 2.4 fusion.5
  101.4 2.2 convolution_multiply_fusion.1
  103.7 28.1 %collective-permute-done.3 = bf16[128,8192]{1,0:T(8,128)(2,1)S(1)} collective-permute-done((bf16[128,8192]{1,0:T(8,128)(2,1)S(1)}, bf16[128,8192]{1,0:T(8,128)(2,1)S(1)}, u32[]{:S(2)}, u32[]{:S(2)}) %collective-permute-start.3) | collective-permute-done | bytes 2097184 | tf_op jit(solution)/shard_map/ppermute | solution.py:17
  131.7 2.3 convolution_add_fusion
  134.1 2.5 fusion.6
  136.6 16.6 %subtract_multiply_fusion = (f32[129,8192]{1,0:T(8,128)}, f32[129,8192]{1,0:T(8,128)}, f32[129,8192]{1,0:T(8,128)}) fusion(f32[129,8192]{1,0:T(8,128)S(1)} %fusion.6, f32[129,8192]{1,0:T(8,128)S(1)} %convolution_negate_fusion.1, f32[129,8192]{1,0:T(8,128)S(1)} %convolution_add_fusion, f32[129]{0:T(256)S(1)} %copy-done.77, ...), kind=kOutput, calls=%fused_computation.46 | convolution fusion | flops 1631880960 | bytes 27460100 | tf_op jit(solution)/shard_map/dot_general | solution.py:58
  153.2 7.6 copy.36
  160.8 5.2 bitcast_reduce_fusion
  166.0 7.6 copy.35
  173.7 5.2 bitcast_reduce_fusion.1
  179.9 1.6 fusion.108
  181.6 3.2 pad_maximum_fusion
  187.4 12.7 %all_gather.28 = f32[2,129,512]{2,1,0:T(8,128)S(1)} all-gather(f32[2,129,128]{2,1,0:T(8,128)S(1)} %pad_maximum_fusion.1), channel_id=1, replica_groups=mesh['ctx'=32,'own'=4] {'own'}, dimensions={2}, use_global_device_ids=true | all-gather | bytes 660480 | tf_op jit(solution)/shard_map/all_gather | solution.py:136
  200.8 1.2 copy.25
  203.0 5.1 broadcast_in_dim.218
  208.1 8.0 copy.28
  216.1 4.0 broadcast_in_dim.216
  220.1 8.1 copy.26
  228.3 72.0 %all-reduce = bf16[128]{0:T(256)(128)(2,1)} all-reduce(bf16[128]{0:T(256)(128)(2,1)S(1)} %dynamic-update-slice), channel_id=1, replica_groups=mesh['ctx'=32,'own'=4] {'ctx','own'}, use_global_device_ids=true, to_apply=%add | all-reduce | flops 128 | bytes 512
  300.3 2.9 collective-permute-start.5
  303.3 69.3 %all_gather.30 = f32[8,8192]{1,0:T(8,128)S(1)} all-gather(f32[8,2048]{1,0:T(8,128)S(1)} %copy-done.52), channel_id=1, replica_groups=mesh['ctx'=32,'own'=4] {'own'}, dimensions={1}, use_global_device_ids=true | all-gather | bytes 327680 | tf_op jit(solution)/shard_map/all_gather | solution.py:138
  380.2 7.5 fusion.3
  387.8 6.0 fusion.4
  393.8 39.3 %all-reduce.3.cloned.1.call-done = f32[128,512]{1,0:T(8,128)} async-done(((f32[128,512]{1,0:T(8,128)}), f32[128,512]{1,0:T(8,128)}) %all-reduce.3.cloned.1.call-update) | async-done | bytes 262160 | tf_op jit(solution)/shard_map/psum | solution.py:224
  433.1 1.5 constant_dynamic-slice_fusion
  434.6 20.2 %fusion.32 = f32[128,8192]{1,0:T(8,128)} fusion(f32[129,8192]{1,0:T(8,128)} %copy-done.3, f32[129,8192]{1,0:T(8,128)} %copy-done.4, f32[129,8192]{1,0:T(8,128)} %copy-done.6, f32[129,8192]{1,0:T(8,128)} %copy.28, f32[129,8192]{1,0:T(8,128)} %copy-done.5, f32[129,8192]{1,0:T(8,128)} %copy.26, f32[2,129,8192]{2,1,0:T(8,128)} %all-gather.4.cloned.1.call-done, ...), kind=kOutput, calls=%fused_computation.71 | convolution fusion | flops 1631897472 | bytes 38011912 | tf_op jit(solution)/shard_map/dot_general | solution.py:68
  454.8 19.2 %fusion.16 = f32[128,8192]{1,0:T(8,128)} fusion(f32[129,8192]{1,0:T(8,128)} %copy-done.2, f32[129,8192]{1,0:T(8,128)} %get-tuple-element.478, f32[129,8192]{1,0:T(8,128)} %fusion.3, f32[129,8192]{1,0:T(8,128)} %copy.28, f32[129,8192]{1,0:T(8,128)S(1)} %copy-done.7, f32[129,8192]{1,0:T(8,128)} %copy.26, f32[2,129,8192]{2,1,0:T(8,128)} %all-gather.4.cloned.1.call-done, ...), kind=kOutput, calls=%fused_computation.55 | convolution fusion | flops 1630840704 | bytes 38011396 | tf_op jit(solution)/shard_map/dot_general | solution.py:68
  474.0 301.8 %while.33 = (s32[]{:T(128)}, f32[8,8192]{1,0:T(8,128)S(1)}, s32[]{:T(128)}, bf16[128]{0:T(256)(128)(2,1)S(1)}, f32[8,8192]{1,0:T(8,128)S(1)}, /*index=5*/bf16[12...) while((s32[]{:T(128)}, f32[8,8192]{1,0:T(8,128)S(1)}, s32[]{:T(128)}, ...), condition=%wide.region_19.20_spmd.clone, body=%wide.region_18.19_spmd.clone.sunk | while | flops 393225 | bytes 917701 | solution.py:37
  494.1 1.1 fusion.249
  496.5 1.1 fusion.249
  538.9 1.1 fusion.249
  541.3 1.1 fusion.249
  583.7 1.1 fusion.249
  586.1 1.1 fusion.249
  628.5 1.1 fusion.249
  630.9 1.1 fusion.249
  776.0 303.6 %while.32 = (s32[]{:T(128)}, f32[8,8192]{1,0:T(8,128)S(1)}, s32[]{:T(128)}, bf16[128]{0:T(256)(128)(2,1)S(1)}, f32[8,8192]{1,0:T(8,128)S(1)}, /*index=5*/bf16[128,8,8192]{2,1,0:T(8,128)(2,1)}, s32[]{:T(128)}, s32[]{:T(128)}) while((s32[]{:T(128)}, f32[8,8192]{1,0:T(8,128)S(1)}, s32[]{:T(128)}, bf16[128]{0:T(256)(128)(2,1)S(1)}, ...), condition=%wide.region_9.10_spmd.clone, body=%wide.region_8.9_spmd.clone.sunk | while | flops 393221 | bytes 917639 | solution.py:37
  1080.5 19.6 %fusion.8 = f32[128,8192]{1,0:T(8,128)} fusion(f32[128,8192]{1,0:T(8,128)} %fusion.32, f32[129,8192]{1,0:T(8,128)} %copy-done.3, f32[129,8192]{1,0:T(8,128)} %copy-done.4, f32[129,8192]{1,0:T(8,128)} %copy-done.6, f32[129,8192]{1,0:T(8,128)} %copy.26, f32[129,8192]{1,0:T(8,128)} %copy-done.5, f32[129,8192]{1,0:T(8,128)} %copy.28, ...), kind=kOutput, calls=%fused_computation.35 | convolution fusion | flops 1658111872 | bytes 42731016 | tf_op jit(solution)/shard_map/dot_general | solution.py:71
  1100.0 5.8 fusion.45
  1105.8 2.3 collective-permute-start.4
  1108.1 18.6 %fusion.7 = f32[128,8192]{1,0:T(8,128)} fusion(f32[128,8192]{1,0:T(8,128)} %fusion.16, f32[129,8192]{1,0:T(8,128)} %get-tuple-element.478, f32[129,8192]{1,0:T(8,128)S(1)} %bitcast.138, f32[129,8192]{1,0:T(8,128)} %fusion.4, f32[129,8192]{1,0:T(8,128)} %copy.28, f32[129,8192]{1,0:T(8,128)} %fusion.3, f32[129,8192]{1,0:T(8,128)} %copy.26, ...), kind=kOutput, calls=%fused_computation.33 | convolution fusion | flops 1657055104 | bytes 42730500 | tf_op jit(solution)/shard_map/dot_general | solution.py:71
  1126.7 4.5 fusion.42
  1131.3 3.5 collective-permute-start.6
  1134.8 5.6 collective-permute-start.7
  1141.0 4.5 fusion.78
  1146.3 4.4 fusion.64
  1151.6 4.4 fusion.71
  (805 shorter events, 449.8 us)
Async XLA Ops:
  8.0 178.3 %copy-start = (f32[128,128]{1,0:T(8,128)S(1)}, f32[128,128]{1,0:T(8,128)}, u32[]{:S(2)}) copy-start(f32[128,128]{1,0:T(8,128)} %param.16) | copy-start | bytes 196612
  8.0 425.1 %all-reduce.3.cloned.1.call-start = ((), (), s32[]{:S(2)}) async-start(), calls=%async_computation.3 | async-start | bytes 524288 | tf_op jit(solution)/shard_map/psum | solution.py:224
  9.7 50.1 %collective-permute-start.2 = (bf16[6,8192]{1,0:T(8,128)(2,1)}, bf16[6,8192]{1,0:T(8,128)(2,1)}, u32[]{:S(2)}, u32[]{:S(2)}) collective-permute-start(bf16[6,8192]{1,0:T(8,128)(2,1)} %slice.600), channel_id=1, source_target_pairs={{0,1},{1,2},{2,3},{3,4},{4,5},{5,6},{6,7},{7,8},{8,9},{9,10},{10,1... | collective-permute-start | bytes 294920 | tf_op jit(solution)/shard_map/ppermute | solution.py:17
  14.4 43.6 %collective-permute-start.1 = (bf16[6,8192]{1,0:T(8,128)(2,1)}, bf16[6,8192]{1,0:T(8,128)(2,1)}, u32[]{:S(2)}, u32[]{:S(2)}) collective-permute-start(bf16[6,8192]{1,0:T(8,128)(2,1)} %slice.578), channel_id=1, source_target_pairs={{0,1},{1,2},{2,3},{3,4},{4,5},{5,6},{6,7},{7,8},{8,9},{9,10},{10,1... | collective-permute-start | bytes 294920 | tf_op jit(solution)/shard_map/ppermute | solution.py:17
  18.0 38.3 %collective-permute-start = (bf16[6,8192]{1,0:T(8,128)(2,1)}, bf16[6,8192]{1,0:T(8,128)(2,1)}, u32[]{:S(2)}, u32[]{:S(2)}) collective-permute-start(bf16[6,8192]{1,0:T(8,128)(2,1)} %slice.556), channel_id=1, source_target_pairs={{0,1},{1,2},{2,3},{3,4},{4,5},{5,6},{6,7},{7,8},{8,9},{9,10},{10,1... | collective-permute-start | bytes 294920 | tf_op jit(solution)/shard_map/ppermute | solution.py:17
  50.3 11.1 copy-start.16
  50.6 10.9 copy-start.20
  51.4 10.1 copy-start.14
  51.7 9.8 copy-start.18
  52.0 9.5 copy-start.22
  52.2 9.2 copy-start.26
  52.5 9.0 copy-start.30
  52.8 8.7 copy-start.24
  53.1 8.4 copy-start.28
  53.4 8.2 copy-start.32
  53.6 7.9 copy-start.34
  53.9 7.6 copy-start.36
  61.7 27.8 %copy-start.81 = (f32[1,2048]{1,0:T(1,128)S(1)}, f32[1,2048]{1,0:T(1,128)}, u32[]{:S(2)}) copy-start(f32[1,2048]{1,0:T(1,128)} %get-tuple-element.449) | copy-start | bytes 24580
  61.7 27.8 %copy-start.82 = (f32[1,2048]{1,0:T(1,128)S(1)}, f32[1,2048]{1,0:T(1,128)}, u32[]{:S(2)}) copy-start(f32[1,2048]{1,0:T(1,128)} %get-tuple-element.450) | copy-start | bytes 24580
  61.7 27.8 %copy-start.83 = (f32[1,2048]{1,0:T(1,128)S(1)}, f32[1,2048]{1,0:T(1,128)}, u32[]{:S(2)}) copy-start(f32[1,2048]{1,0:T(1,128)} %get-tuple-element.451) | copy-start | bytes 24580
  61.8 27.8 %copy-start.84 = (f32[1,2048]{1,0:T(1,128)S(1)}, f32[1,2048]{1,0:T(1,128)}, u32[]{:S(2)}) copy-start(f32[1,2048]{1,0:T(1,128)} %get-tuple-element.452) | copy-start | bytes 24580
  61.8 27.8 %copy-start.85 = (f32[1,2048]{1,0:T(1,128)S(1)}, f32[1,2048]{1,0:T(1,128)}, u32[]{:S(2)}) copy-start(f32[1,2048]{1,0:T(1,128)} %get-tuple-element.453) | copy-start | bytes 24580
  61.8 27.8 %copy-start.86 = (f32[1,2048]{1,0:T(1,128)S(1)}, f32[1,2048]{1,0:T(1,128)}, u32[]{:S(2)}) copy-start(f32[1,2048]{1,0:T(1,128)} %get-tuple-element.454) | copy-start | bytes 24580
  61.8 27.8 %copy-start.87 = (f32[1,2048]{1,0:T(1,128)S(1)}, f32[1,2048]{1,0:T(1,128)}, u32[]{:S(2)}) copy-start(f32[1,2048]{1,0:T(1,128)} %get-tuple-element.455) | copy-start | bytes 24580
  61.8 27.8 %copy-start.88 = (f32[1,2048]{1,0:T(1,128)S(1)}, f32[1,2048]{1,0:T(1,128)}, u32[]{:S(2)}) copy-start(f32[1,2048]{1,0:T(1,128)} %get-tuple-element.456) | copy-start | bytes 24580
  86.5 45.3 %collective-permute-start.3 = (bf16[128,8192]{1,0:T(8,128)(2,1)S(1)}, bf16[128,8192]{1,0:T(8,128)(2,1)S(1)}, u32[]{:S(2)}, u32[]{:S(2)}) collective-permute-start(bf16[128,8192]{1,0:T(8,128)(2,1)S(1)} %get-tuple-element.404), channel_id=1, source_target_pairs={{0,1},{1,2},{2,3},{3,4},{4,5},{5,6},{6,7},{7,8},{8,9},{9,10},{10,1... | collective-permute-start | bytes 6291464 | tf_op jit(solution)/shard_map/ppermute | solution.py:17
  99.1 37.5 %copy-start.2 = (f32[129,8192]{1,0:T(8,128)}, f32[129,8192]{1,0:T(8,128)S(1)}, u32[]{:S(2)}) copy-start(f32[129,8192]{1,0:T(8,128)S(1)} %convolution_negate_fusion.1) | copy-start | bytes 12681220
  101.4 32.6 %copy-start.3 = (f32[129,8192]{1,0:T(8,128)}, f32[129,8192]{1,0:T(8,128)S(1)}, u32[]{:S(2)}) copy-start(f32[129,8192]{1,0:T(8,128)S(1)} %fusion.5) | copy-start | bytes 12681220
  103.6 30.4 %copy-start.4 = (f32[129,8192]{1,0:T(8,128)}, f32[129,8192]{1,0:T(8,128)S(1)}, u32[]{:S(2)}) copy-start(f32[129,8192]{1,0:T(8,128)S(1)} %convolution_multiply_fusion.1) | copy-start | bytes 12681220
  136.6 16.6 %copy-start.6 = (f32[129,8192]{1,0:T(8,128)}, f32[129,8192]{1,0:T(8,128)S(1)}, u32[]{:S(2)}) copy-start(f32[129,8192]{1,0:T(8,128)S(1)} %fusion.6) | copy-start | bytes 12681220
  181.5 253.1 %all-gather.4.cloned.1.call-start = ((), (), s32[]{:S(2)}) async-start(), calls=%async_computation | async-start | bytes 11141120 | tf_op jit(solution)/shard_map/all_gather | solution.py:135
  184.8 289.2 %all-gather.8.cloned.1.call-start = ((), (), s32[]{:S(2)}) async-start(), calls=%async_computation.2 | async-start | bytes 16908288 | tf_op jit(solution)/shard_map/all_gather | solution.py:23
  186.2 589.8 %all-gather.6.cloned.1.call-start = ((), (), s32[]{:S(2)}) async-start(), calls=%async_computation.1 | async-start | bytes 16908288 | tf_op jit(solution)/shard_map/all_gather | solution.py:23
  220.1 83.1 %copy-start.52 = (f32[8,2048]{1,0:T(8,128)S(1)}, f32[8,2048]{1,0:T(8,128)}, u32[]{:S(2)}) copy-start(f32[8,2048]{1,0:T(8,128)} %param.18) | copy-start | bytes 196612
  220.1 153.6 %copy-start.13 = (f32[8,8192]{1,0:T(8,128)S(1)}, f32[8,8192]{1,0:T(8,128)}, u32[]{:S(2)}) copy-start(f32[8,8192]{1,0:T(8,128)} %copy-done.12) | copy-start | bytes 786436
  220.1 159.0 %copy-start.69 = (bf16[8192]{0:T(1024)(128)(2,1)S(1)}, bf16[8192]{0:T(1024)(128)(2,1)}, u32[]{:S(2)}) copy-start(bf16[8192]{0:T(1024)(128)(2,1)} %get-tuple-element.377) | copy-start | bytes 49156
  300.3 79.9 %collective-permute-start.5 = (bf16[128,8192]{1,0:T(8,128)(2,1)S(1)}, bf16[128,8192]{1,0:T(8,128)(2,1)}, u32[]{:S(2)}, u32[]{:S(2)}) collective-permute-start(bf16[128,8192]{1,0:T(8,128)(2,1)S(1)} %get-tuple-element.402), channel_id=1, source_target_pairs={{1,0},{2,1},{3,2},{4,3},{5,4},{6,5},{7,6},{8,7},{9,8},{10,9},{11,1... | collective-permute-start | bytes 6291464 | tf_op jit(solution)/shard_map/ppermute | solution.py:17
  380.2 7.6 slice-start.2
  380.2 7.6 slice-start.3
  387.8 46.8 %copy-start.80 = (f32[129]{0:T(256)S(1)}, f32[129]{0:T(256)}, u32[]{:S(2)}) copy-start(f32[129]{0:T(256)} %fusion.150) | copy-start | bytes 1552
  434.6 20.2 %copy-start.7 = (f32[129,8192]{1,0:T(8,128)S(1)}, f32[129,8192]{1,0:T(8,128)}, u32[]{:S(2)}) copy-start(f32[129,8192]{1,0:T(8,128)} %fusion.4) | copy-start | bytes 12681220
  454.8 19.2 %copy-start.89 = (bf16[128]{0:T(256)(128)(2,1)S(1)}, bf16[128]{0:T(256)(128)(2,1)}, u32[]{:S(2)}) copy-start(bf16[128]{0:T(256)(128)(2,1)} %all-reduce) | copy-start | bytes 772
  775.9 304.5 %copy-start.54 = (f32[1,8192]{1,0:T(1,128)S(1)}, f32[1,8192]{1,0:T(1,128)}, u32[]{:S(2)}) copy-start(f32[1,8192]{1,0:T(1,128)} %copy-done.53) | copy-start | bytes 98308
  775.9 304.5 %copy-start.56 = (f32[1,8192]{1,0:T(1,128)S(1)}, f32[1,8192]{1,0:T(1,128)}, u32[]{:S(2)}) copy-start(f32[1,8192]{1,0:T(1,128)} %copy-done.55) | copy-start | bytes 98308
  775.9 304.5 %copy-start.58 = (f32[1,8192]{1,0:T(1,128)S(1)}, f32[1,8192]{1,0:T(1,128)}, u32[]{:S(2)}) copy-start(f32[1,8192]{1,0:T(1,128)} %copy-done.57) | copy-start | bytes 98308
  775.9 304.5 %copy-start.60 = (f32[1,8192]{1,0:T(1,128)S(1)}, f32[1,8192]{1,0:T(1,128)}, u32[]{:S(2)}) copy-start(f32[1,8192]{1,0:T(1,128)} %copy-done.59) | copy-start | bytes 98308
  775.9 304.5 %copy-start.62 = (f32[1,8192]{1,0:T(1,128)S(1)}, f32[1,8192]{1,0:T(1,128)}, u32[]{:S(2)}) copy-start(f32[1,8192]{1,0:T(1,128)} %copy-done.61) | copy-start | bytes 98308
  775.9 304.5 %copy-start.64 = (f32[1,8192]{1,0:T(1,128)S(1)}, f32[1,8192]{1,0:T(1,128)}, u32[]{:S(2)}) copy-start(f32[1,8192]{1,0:T(1,128)} %copy-done.63) | copy-start | bytes 98308
  775.9 304.5 %copy-start.66 = (f32[1,8192]{1,0:T(1,128)S(1)}, f32[1,8192]{1,0:T(1,128)}, u32[]{:S(2)}) copy-start(f32[1,8192]{1,0:T(1,128)} %copy-done.65) | copy-start | bytes 98308
  776.0 304.5 %copy-start.68 = (f32[1,8192]{1,0:T(1,128)S(1)}, f32[1,8192]{1,0:T(1,128)}, u32[]{:S(2)}) copy-start(f32[1,8192]{1,0:T(1,128)} %copy-done.67) | copy-start | bytes 98308
  776.0 304.5 %copy-start.91 = (f32[128]{0:T(128)S(1)}, f32[128]{0:T(128)}, u32[]{:S(2)}) copy-start(f32[128]{0:T(128)} %iota_add_fusion) | copy-start | bytes 1540
  776.0 332.1 %slice-start = ((s8[4456448]{0:T(1024)(128)(4,1)}), s8[262144]{0:T(1024)(128)(4,1)S(1)}, s32[]{:S(2)}) async-start(s8[4456448]{0:T(1024)(128)(4,1)} %bitcast.137), calls=%async_computation.4 | async-start | bytes 524288
  1080.4 27.7 %slice-start.1 = ((s8[4456448]{0:T(1024)(128)(4,1)}), s8[4194304]{0:T(1024)(128)(4,1)S(1)}, s32[]{:S(2)}) async-start(s8[4456448]{0:T(1024)(128)(4,1)} %bitcast.137), calls=%async_computation.5 | async-start | bytes 8388608
  1100.0 8.1 copy-start.90
  1105.8 34.6 %collective-permute-start.4 = (bf16[6,8192]{1,0:T(8,128)(2,1)S(1)}, bf16[6,8192]{1,0:T(8,128)(2,1)S(1)}, u32[]{:S(2)}, u32[]{:S(2)}) collective-permute-start(bf16[6,8192]{1,0:T(8,128)(2,1)S(1)} %slice.766), channel_id=1, source_target_pairs={{1,0},{2,1},{3,2},{4,3},{5,4},{6,5},{7,6},{8,7},{9,8},{10,9},{11,1... | collective-permute-start | bytes 294920 | tf_op jit(solution)/shard_map/ppermute | solution.py:17
  1131.2 9.7 copy-start.17
  1131.2 9.7 copy-start.21
  1131.2 9.7 copy-start.43
  1131.2 9.7 copy-start.45
  1131.2 9.7 copy-start.47
  1131.2 9.7 copy-start.49
  1131.2 9.7 copy-start.51
  1131.3 19.5 %collective-permute-start.6 = (bf16[6,8192]{1,0:T(8,128)(2,1)S(1)}, bf16[6,8192]{1,0:T(8,128)(2,1)S(1)}, u32[]{:S(2)}, u32[]{:S(2)}) collective-permute-start(bf16[6,8192]{1,0:T(8,128)(2,1)S(1)} %slice.774), channel_id=1, source_target_pairs={{1,0},{2,1},{3,2},{4,3},{5,4},{6,5},{7,6},{8,7},{9,8},{10,9},{11,1... | collective-permute-start | bytes 294920 | tf_op jit(solution)/shard_map/ppermute | solution.py:17
  1134.8 10.6 collective-permute-start.7
  (44 other events, 174.2 us)
Sparse Core Ops, SparseCore 0:
  181.6 251.4 all-reduce.2
Sparse Core Ops, SparseCore 1:
  184.9 93.0 all-gather.3
  281.0 99.9 all-gather.7
  384.6 83.4 all-gather.5
where the time goes:
time: 1180 us; the launch traced here: 1160 us
  other arithmetic  358 us (30%)
  local copies, waits for them, and re-layouts  215 us (18%)
  blocking collectives  179 us (15%)
  loops' own time  171 us (14%)
  matrix products  130 us (11%)
  waiting for transfers between devices  67.5 us (6%)
  starting transfers between devices  25.5 us (2%)
  between operations  18.2 us (2%)
    select_n x256, other arithmetic, hop(): return jax.tree.map(lambda a, b: jnp.where(reached, a, b), new, before)  283 us
    another operation x2, loops' own time, carried_in(): return lax.fori_loop(0, size, hop, start)  171 us
    dynamic_slice x256, local copies, waits for them, and re-layouts, hop(): part[at].astype(own.dtype)  152 us
    unnamed x1, blocking collectives  72 us
    all_gather x1, blocking collectives, shards(): lax.all_gather(residues, 'own', axis=1, tiled=True)  69.3 us
    dot_general x2, matrix products, restore(): jnp.dot(table_set[2], real_part, precision=exact_mode, preferred_element_...  39.4 us
    psum x1, waiting for transfers between devices, shards(): summed_taps = lax.psum(partial_taps, ('ctx', 'own'))  39.3 us
    dot_general x2, matrix products, restore(): jnp.dot(table_set[3], imag_part, precision=exact_mode, preferred_element_...  38.1 us
  transfers between devices with their start and end apart: 12, of which 2 were waited for; matrix products, arithmetic and copies ran while one was open for 32% of the time, Pallas kernels for 0%

commit v1 on v0

v1 whole, which is shorter than its diff:
```python
import math

import jax
import jax.numpy as jnp
import numpy as np
from jax import lax
from jax.experimental import pallas as pl
from jax.experimental.pallas import tpu as pltpu
from jax.sharding import PartitionSpec as P

CPG = 16
BLOCK = 512
TERMS = 16
RATE_TOP = 0.03
AXES = ("ctx", "own")
F32, BF16 = jnp.float32, jnp.bfloat16


def split_np(table):
    high = table.astype(np.float32).astype(jnp.bfloat16)
    low = (table - high.astype(np.float64)).astype(np.float32).astype(jnp.bfloat16)
    return high, low


def series(lags):
    nodes = np.cos(np.pi * (np.arange(64) + 0.5) / 64)
    values = np.exp(-np.outer(np.asarray(lags, np.float64), RATE_TOP / 2 * (1 + nodes)))
    basis = np.cos(np.outer(np.arange(TERMS), np.pi * (np.arange(64) + 0.5) / 64))
    coeff = values @ basis.T * (2.0 / 64)
    coeff[:, 0] *= 0.5
    return coeff


def tables(rows):
    angle = np.pi * (2 * np.arange(rows) + 1) / (2 * rows)

    def forward(places):
        phase = np.outer(angle, places)
        return np.concatenate([np.cos(phase), -np.sin(phase)])

    here = np.arange(rows)
    own, before, after = forward(here), forward(here - rows), forward(here + rows)
    phase = np.outer(here, angle)
    inverse = np.concatenate([np.cos(phase), -np.sin(phase)], axis=1) / rows
    cat = np.concatenate
    pair = lambda m: cat(split_np(m), axis=1)

    def triple(m):
        high, low = split_np(m)
        return cat([high, low, high], axis=1)

    return dict(
        own=pair(own),
        before=pair(before),
        after=pair(after),
        taps=triple(own),
        head=triple(own @ series(here)),
        inverse=split_np(inverse)[0],
        inverse3=triple(inverse),
        ahead=triple(series(here + 1)),
        behind=triple(series(rows - here)),
        moment=cat(
            [
                pair(series(rows - 1 - here).T),
                pair(series(here).T),
            ],
            axis=0,
        ),
    )


def dot(a, b):
    return jnp.dot(a, b, preferred_element_type=F32)


def halves(x):
    high = x.astype(BF16)
    return high, (x - high.astype(F32)).astype(BF16)


def stack3(x):
    high, low = halves(x)
    return jnp.concatenate([high, high, low], axis=0)


def spread_matrix(groups, quarter, copies=1):
    row = lax.broadcasted_iota(jnp.int32, (copies * groups, BLOCK), 0) % groups
    col = lax.broadcasted_iota(jnp.int32, (copies * groups, BLOCK), 1)
    return (row == col // CPG + quarter * (BLOCK // CPG)).astype(F32).astype(BF16)


def spread_taps(short, quarter, out):
    high, rest = halves(short)
    rest = short - high.astype(F32)
    mid, rest2 = halves(rest)
    low = rest2
    lhs = jnp.concatenate([high, mid, low], axis=1)
    out[...] = dot(lhs, spread_matrix(128, quarter, 3))


def chebyshev(rate):
    z = rate * (2.0 / RATE_TOP) - 1.0
    terms = [jnp.ones_like(z), z]
    while len(terms) < TERMS:
        terms.append(2.0 * z * terms[-1] - terms[-2])
    return terms


def front_kernel(
    me, q, k, v, g, rim, short, rates, moment,
    qf, kf, vf, prod, gconv, sf, sb, xq, xk, xv, taps,
):
    rows = q.shape[0]
    quarter = pl.program_id(0)
    spread_taps(short[0], quarter, taps)
    for at, (src, dst) in enumerate(((q, xq), (k, xk), (v, xv))):
        dst[0:8] = rim[8 * at : 8 * at + 8].astype(F32)
        dst[8:] = src[...].astype(F32)

    def step(r, _):
        base = pl.multiple_of(r * 16, 16)
        feats = []
        for at, src in enumerate((xq, xk, xv)):
            window = src[pl.ds(base, 24), :]
            total = taps[7 * at : 7 * at + 1, :] * window[8:24]
            for j in range(1, 7):
                total = total + taps[7 * at + j : 7 * at + j + 1, :] * window[8 - j : 24 - j]
            feats.append(total.astype(BF16))
        here = pl.ds(base, 16)
        qf[here, :] = feats[0]
        kf[here, :] = feats[1]
        vf[here, :] = feats[2]
        prod[here, :] = (feats[1].astype(F32) * feats[2].astype(F32)).astype(BF16)
        gconv[here, :] = (g[here, :].astype(F32) * feats[0].astype(F32)).astype(BF16)
        return 0

    lax.fori_loop(0, rows // 16, step, 0)
    p, c = prod[...], gconv[...]
    mf = dot(moment[0:16, :], jnp.concatenate([p, p], axis=0))
    mb = dot(moment[16:32, :], jnp.concatenate([c, c], axis=0))
    for lane in range(BLOCK // 128):
        cols = slice(128 * lane, 128 * lane + 128)
        terms = chebyshev(rates[0, 8 * lane : 8 * lane + 8, :])
        ahead = jnp.zeros((8, 128), F32)
        back = jnp.zeros((8, 128), F32)
        for n, term in enumerate(terms):
            ahead = ahead + term * mf[n : n + 1, cols]
            back = back + term * mb[n : n + 1, cols]
        sf[lane] = ahead.astype(BF16)
        sb[lane] = back.astype(BF16)


def scan_kernel(me, states, rates, out):
    count = states.shape[0]
    backward = me[1]
    factor = jnp.exp(rates[0] * -128.0)

    def hop(n, carry):
        at = jnp.where(backward == 1, count - 1 - n, n)
        out[at] = carry.astype(BF16)
        return factor * carry + states[at].astype(F32)

    lax.fori_loop(0, count, hop, jnp.zeros((8, 128), F32), unroll=4)


def back_kernel(
    me, qf, kf, vf, g, prod, gconv, before, after, sf, sb, short, rates, weights, ltaps,
    t_own, t_before, t_after, t_taps, t_head, t_inv, t_inv3, t_ahead, t_behind, *rest,
):
    outs = rest[-27:]
    (layer, gq, gk, gv, rim, last, tgrad) = outs[:7]
    (xx, own, prv, cur, nxt, tre, hre, ys, zs, cs, tsp, acc, taps, eq, ek, ev, coef, lg, gp, _unused) = outs[7:]
    rows = qf.shape[0]
    quarter = pl.program_id(0)
    spread_taps(short[0], quarter, taps)

    @pl.when(quarter == 0)
    def _():
        spec = dot(t_taps[...], stack3(ltaps[0]))
        high, low = halves(spec)
        tsp[:, 0:128] = high
        tsp[:, 128:256] = low
        acc[...] = jnp.zeros_like(acc)

    tre[...] = dot(tsp[...], spread_matrix(128, quarter, 2))
    for src, table, dst in (
        (prod, t_own, own), (before, t_before, prv), (gconv, t_own, cur), (after, t_after, nxt),
    ):
        value = src[...]
        xx[0:rows] = value
        xx[rows:] = value
        dst[...] = dot(table[...], xx[...])
    for lane in range(BLOCK // 128):
        cols = slice(128 * lane, 128 * lane + 128)
        eight = slice(8 * lane, 8 * lane + 8)
        weight = weights[0, eight, :]
        sets = (weight, weight * sf[lane].astype(F32), weight * sb[lane].astype(F32))
        for n, term in enumerate(chebyshev(rates[0, eight, :])):
            for at, field in enumerate(sets):
                coef[16 * at + n : 16 * at + n + 1, cols] = jnp.sum(
                    term * field, axis=0, keepdims=True
                )
    hre[...] = dot(t_head[...], stack3(coef[0:16]))

    def bins(r, _):
        base = pl.multiple_of(r * 16, 16)
        re = pl.ds(base, 16)
        im = pl.ds(rows + base, 16)
        for lane in range(BLOCK // 128):
            cols = slice(128 * lane, 128 * lane + 128)
            tr, ti, hr, hi = tre[re, cols], tre[im, cols], hre[re, cols], hre[im, cols]
            pr, pi, cr, ci = own[re, cols], own[im, cols], cur[re, cols], cur[im, cols]
            wr, wi = pr + prv[re, cols], pi + prv[im, cols]
            ar, ai = cr + nxt[re, cols], ci + nxt[im, cols]
            ys[re, cols] = (wr * tr - wi * ti + (pr * hr - pi * hi)).astype(BF16)
            ys[im, cols] = (wr * ti + wi * tr + (pr * hi + pi * hr)).astype(BF16)
            zs[re, cols] = (ar * tr + ai * ti + (cr * hr + ci * hi)).astype(BF16)
            zs[im, cols] = (ai * tr - ar * ti + (ci * hr - cr * hi)).astype(BF16)
            cs[re, cols] = (cr * wr + ci * wi).astype(BF16)
            cs[im, cols] = (ci * wr - cr * wi).astype(BF16)
        return 0

    lax.fori_loop(0, rows // 16, bins, 0)
    lg[...] = dot(t_inv[...], ys[...]) + dot(t_ahead[...], stack3(coef[16:32]))
    gp[...] = dot(t_inv[...], zs[...]) + dot(t_behind[...], stack3(coef[32:48]))
    chan = lax.broadcasted_iota(jnp.int32, (BLOCK, 128), 0)
    group = lax.broadcasted_iota(jnp.int32, (BLOCK, 128), 1)
    gather = (chan // CPG + quarter * (BLOCK // CPG) == group).astype(F32).astype(BF16)
    acc[...] += dot(cs[...], gather)

    @pl.when(quarter == pl.num_programs(0) - 1)
    def _():
        tgrad[...] = dot(t_inv3[...], stack3(acc[...]))

    def rows_out(r, _):
        here = pl.ds(pl.multiple_of(r * 16, 16), 16)
        conv, grad = lg[here, :], gp[here, :]
        layer[here, :] = (qf[here, :].astype(F32) * conv).astype(BF16)
        eq[here, :] = (g[here, :].astype(F32) * conv).astype(BF16).astype(F32)
        ek[here, :] = (grad * vf[here, :].astype(F32)).astype(BF16).astype(F32)
        ev[here, :] = (grad * kf[here, :].astype(F32)).astype(BF16).astype(F32)
        return 0

    lax.fori_loop(0, rows // 16, rows_out, 0)
    for at, src in enumerate((eq, ek, ev)):
        src[rows:] = jnp.zeros((8, BLOCK), F32)
        rim[8 * at : 8 * at + 8] = src[0:8].astype(BF16)

    def unfeature(r):
        base = r * 16 if isinstance(r, int) else pl.multiple_of(r * 16, 16)
        sums = []
        for at, src in enumerate((eq, ek, ev)):
            window = src[pl.ds(base, 24), :]
            total = taps[7 * at : 7 * at + 1, :] * window[0:16]
            for j in range(1, 7):
                total = total + taps[7 * at + j : 7 * at + j + 1, :] * window[j : 16 + j]
            sums.append(total)
        return sums

    def finish(r, _):
        here = pl.ds(pl.multiple_of(r * 16, 16), 16)
        for dst, total in zip((gq, gk, gv), unfeature(r)):
            dst[here, :] = total.astype(BF16)
        return 0

    lax.fori_loop(0, rows // 16, finish, 0)
    for at, total in enumerate(unfeature(rows // 16 - 1)):
        last[16 * at : 16 * at + 16] = total


def tail_kernel(me, last, rim, short, gq_in, gk_in, gv_in, gq, gk, gv, taps):
    quarter = pl.program_id(0) % 4
    spread_taps(short[0], quarter, taps)
    for at, dst in enumerate((gq, gk, gv)):
        window = jnp.concatenate(
            [jnp.zeros((16, BLOCK), F32), rim[8 * at : 8 * at + 8].astype(F32)], axis=0
        )
        total = last[16 * at : 16 * at + 16]
        for j in range(1, 7):
            total = total + taps[7 * at + j : 7 * at + j + 1, :] * window[j : 16 + j]
        dst[...] = total.astype(BF16)


def shift(value, steps):
    count = lax.axis_size(AXES)
    first, last = max(0, -steps), min(count, count - steps)
    return lax.ppermute(value, AXES, [(at, at + steps) for at in range(first, last)])


def gather_own(value):
    count = lax.axis_size("own")
    parts = [value]
    for hop in range(1, count):
        parts.append(lax.ppermute(value, "own", [(at, (at + hop) % count) for at in range(count)]))
    return jnp.stack(parts)


def tiles(x):
    rows, width = x.shape
    return x.reshape(rows, width // 128, 128).transpose(1, 0, 2).reshape(-1, 128)


def params_of(vmem):
    return pltpu.CompilerParams(
        dimension_semantics=("arbitrary",), vmem_limit_bytes=vmem
    )


def shards(query, key, value, short_taps, long_taps, decay_rate, residues, grad_out):
    rows, width = query.shape
    owners = lax.axis_size("own")
    per_own = width // owners
    steps = per_own // BLOCK
    ctx, own = lax.axis_index("ctx"), lax.axis_index("own")
    flat = ctx * owners + own
    half = width // 128
    me = jnp.stack([own, flat // half, flat % half]).astype(jnp.int32)
    table = tables(rows)

    short = jnp.pad(short_taps.reshape(-1, short_taps.shape[2]), ((0, 3), (0, 0)))
    short_all = gather_own(short)
    rims = shift(jnp.concatenate([query[rows - 8 :], key[rows - 8 :], value[rows - 8 :]]), 1)
    weight = residues * jnp.sqrt(-jnp.expm1(-2.0 * decay_rate))
    poles_all = gather_own(jnp.concatenate([tiles(decay_rate), tiles(weight), long_taps]))

    def slot(me_ref, chunk):
        return (me_ref[0] - chunk) % owners

    tab = lambda name: (jnp.asarray(table[name]), pl.BlockSpec(table[name].shape, lambda i, m: (0, 0)))
    full = jax.ShapeDtypeStruct((rows, width), BF16)
    part = jax.ShapeDtypeStruct((rows, per_own), BF16)
    state = jax.ShapeDtypeStruct((per_own // 128, 8, 128), BF16)
    group = BLOCK // 128

    def front(chunk):
        wide = pl.BlockSpec((rows, BLOCK), lambda i, m: (0, chunk * steps + i))
        here = pl.BlockSpec((rows, BLOCK), lambda i, m: (0, i))
        sspec = pl.BlockSpec((group, 8, 128), lambda i, m: (i, 0, 0))
        moment, moment_spec = tab("moment")
        return pl.pallas_call(
            front_kernel,
            out_shape=(part,) * 5 + (state,) * 2,
            grid_spec=pltpu.PrefetchScalarGridSpec(
                num_scalar_prefetch=1,
                grid=(steps,),
                in_specs=[wide] * 4
                + [
                    pl.BlockSpec((24, BLOCK), lambda i, m: (0, chunk * steps + i)),
                    pl.BlockSpec((1, 24, 128), lambda i, m: (slot(m, chunk), 0, 0)),
                    pl.BlockSpec((1, 8 * group, 128), lambda i, m: (slot(m, chunk), i, 0)),
                    moment_spec,
                ],
                out_specs=(here,) * 5 + (sspec,) * 2,
                scratch_shapes=[pltpu.VMEM((rows + 8, BLOCK), F32)] * 3
                + [pltpu.VMEM((24, BLOCK), F32)],
            ),
            compiler_params=params_of(32 << 20),
            cost_estimate=pl.CostEstimate(
                flops=2_000_000_000, transcendentals=0, bytes_accessed=10_000_000
            ),
            name=f"front{chunk}",
        )(me, query, key, value, grad_out, rims, short_all, poles_all, moment)

    fronts, behinds, aheads = [], [], []
    for chunk in range(owners):
        made = front(chunk)
        fronts.append(made)
        behinds.append(shift(made[3], 1))
        aheads.append(shift(made[4], -1))

    states = jnp.concatenate([f[5] for f in fronts] + [f[6] for f in fronts])
    arrived = lax.all_to_all(states, AXES, 0, 0, tiled=True)
    scanned = pl.pallas_call(
        scan_kernel,
        out_shape=jax.ShapeDtypeStruct(arrived.shape, BF16),
        grid_spec=pltpu.PrefetchScalarGridSpec(
            num_scalar_prefetch=1,
            grid=(1,),
            in_specs=[
                pl.BlockSpec(arrived.shape, lambda i, m: (0, 0, 0)),
                pl.BlockSpec(
                    (1, 8, 128),
                    lambda i, m: ((m[0] - m[2] // (half // owners)) % owners, m[2] % (half // owners), 0),
                ),
            ],
            out_specs=pl.BlockSpec(arrived.shape, lambda i, m: (0, 0, 0)),
        ),
        compiler_params=params_of(16 << 20),
        name="scan",
    )(me, arrived, poles_all)
    carried = lax.all_to_all(scanned, AXES, 0, 0, tiled=True)

    names = ("own", "before", "after", "taps", "head", "inverse", "inverse3", "ahead", "behind")

    def back(chunk, outs):
        wide = pl.BlockSpec((rows, BLOCK), lambda i, m: (0, chunk * steps + i))
        here = pl.BlockSpec((rows, BLOCK), lambda i, m: (0, i))
        quarter = per_own // 128
        consts = [tab(name) for name in names]
        made = fronts[chunk]
        operands = [
            me, made[0], made[1], made[2], grad_out, made[3], made[4],
            behinds[chunk], aheads[chunk], carried, carried, short_all,
            poles_all, poles_all, poles_all,
        ] + [c for c, _ in consts]
        blocks = quarter // group
        in_specs = [
            here, here, here, wide, here, here, here, here,
            pl.BlockSpec((group, 8, 128), lambda i, m: (chunk * blocks + i, 0, 0)),
            pl.BlockSpec((group, 8, 128), lambda i, m: ((owners + chunk) * blocks + i, 0, 0)),
            pl.BlockSpec((1, 24, 128), lambda i, m: (slot(m, chunk), 0, 0)),
            pl.BlockSpec((1, 8 * group, 128), lambda i, m: (slot(m, chunk), i, 0)),
            pl.BlockSpec((1, 8 * group, 128), lambda i, m: (slot(m, chunk), blocks + i, 0)),
            pl.BlockSpec((1, 128, 128), lambda i, m: (slot(m, chunk), 2, 0)),
        ] + [s for _, s in consts]
        aliases = {}
        for at, out in enumerate(outs):
            aliases[len(operands)] = at
            operands.append(out)
            in_specs.append(pl.BlockSpec(memory_space=pl.ANY))
        spectrum = pltpu.VMEM((2 * rows, BLOCK), F32)
        packed = pltpu.VMEM((2 * rows, BLOCK), BF16)
        ext = pltpu.VMEM((rows + 8, BLOCK), F32)
        plain = pltpu.VMEM((rows, BLOCK), F32)
        return pl.pallas_call(
            back_kernel,
            out_shape=(full,) * 4
            + (
                jax.ShapeDtypeStruct((24, per_own), BF16),
                jax.ShapeDtypeStruct((48, per_own), F32),
                jax.ShapeDtypeStruct((128, 128), F32),
            ),
            grid_spec=pltpu.PrefetchScalarGridSpec(
                num_scalar_prefetch=1,
                grid=(steps,),
                in_specs=in_specs,
                out_specs=(wide,) * 4
                + (
                    pl.BlockSpec((24, BLOCK), lambda i, m: (0, i)),
                    pl.BlockSpec((48, BLOCK), lambda i, m: (0, i)),
                    pl.BlockSpec((128, 128), lambda i, m: (0, 0)),
                ),
                scratch_shapes=[packed]
                + [spectrum] * 6
                + [packed] * 3
                + [
                    pltpu.VMEM((2 * rows, 256), BF16),
                    pltpu.VMEM((2 * rows, 128), F32),
                    pltpu.VMEM((24, BLOCK), F32),
                    ext, ext, ext,
                    pltpu.VMEM((48, BLOCK), F32),
                    plain, plain,
                    pltpu.VMEM((8, 128), F32),
                ],
            ),
            input_output_aliases=aliases,
            compiler_params=params_of(48 << 20),
            cost_estimate=pl.CostEstimate(
                flops=4_000_000_000, transcendentals=0, bytes_accessed=16_000_000
            ),
            name=f"back{chunk}",
        )(*operands)

    outs, edges, lasts, partial = (), [], [], []
    for chunk in range(owners):
        made = back(chunk, outs)
        outs = made[:4]
        edges.append(shift(made[4], -1))
        lasts.append(made[5])
        partial.append(made[6])

    def tail(chunk, outs):
        strip = pl.BlockSpec((16, BLOCK), lambda i, m: (rows // 16 - 1, chunk * steps + i))
        anyspec = pl.BlockSpec(memory_space=pl.ANY)
        thin = jax.ShapeDtypeStruct((rows, width), BF16)
        return pl.pallas_call(
            tail_kernel,
            out_shape=(thin,) * 3,
            grid_spec=pltpu.PrefetchScalarGridSpec(
                num_scalar_prefetch=1,
                grid=(steps,),
                in_specs=[
                    pl.BlockSpec((48, BLOCK), lambda i, m: (0, i)),
                    pl.BlockSpec((24, BLOCK), lambda i, m: (0, i)),
                    pl.BlockSpec((1, 24, 128), lambda i, m: (slot(m, chunk), 0, 0)),
                    anyspec, anyspec, anyspec,
                ],
                out_specs=(strip,) * 3,
                scratch_shapes=[pltpu.VMEM((24, BLOCK), F32)],
            ),
            input_output_aliases={4: 0, 5: 1, 6: 2},
            compiler_params=params_of(16 << 20),
            name=f"tail{chunk}",
        )(me, lasts[chunk], edges[chunk], short_all, *outs)

    grads = outs[1:4]
    for chunk in range(owners):
        grads = tail(chunk, grads)

    ctxs = lax.axis_size("ctx")
    share = rows // ctxs
    pieces = jnp.stack([p.reshape(ctxs, share, 128) for p in partial], axis=1)
    landed = lax.all_to_all(pieces.reshape(ctxs * owners, share, 128), AXES, 0, 0, tiled=True)
    tokens = rows * ctxs * owners
    total = landed.sum(axis=0) * (1.0 / math.sqrt(tokens * CPG))
    every = lax.all_to_all(
        jnp.broadcast_to(total[None], (ctxs, share, 128)), "ctx", 0, 0, tiled=True
    )
    return (outs[0],) + tuple(grads) + (every.reshape(rows, 128),)


def solution(mesh):
    placed = (
        P(AXES, None),
        P(AXES, None),
        P(AXES, None),
        P(None, None, "own"),
        P(None, "own"),
        P(None, "own"),
        P(None, "own"),
        P(AXES, None),
    )
    return jax.shard_map(
        shards,
        mesh=mesh,
        in_specs=placed,
        out_specs=(P(AXES, None),) * 4 + (P(None, "own"),),
        check_vma=False,
    )
```

time: 1180 us -> 241 us (0.20); the launches traced: 1160 us -> 238 us
  other arithmetic: 358 us -> 3.08 us
  local copies, waits for them, and re-layouts: 215 us -> 30 us
  loops' own time: 171 us -> 0 us
  blocking collectives: 179 us -> 20.6 us
  matrix products: 130 us -> 0 us
  Pallas kernels: 0 us -> 98.5 us
  waiting for transfers between devices: 67.5 us -> 11.2 us
  starting transfers between devices: 25.5 us -> 73.5 us
  between operations: 18.2 us -> 1.41 us
    select_n x256 -> x0, other arithmetic: 283 us -> none  [hop(): return jax.tree.map(lambda a, b: jnp.where(reached, a, b), new, before)]
    another operation x2 -> x0, loops' own time: 171 us -> none  [carried_in(): return lax.fori_loop(0, size, hop, start)]
    dynamic_slice x257 -> x0, local copies, waits for them, and re-layouts: 153 us -> none  [the longest x256 152 us: hop(): part[at].astype(own.dtype)]
    dot_general x18 -> x0, matrix products: 130 us -> none  [the longest x2 39.4 us: restore(): jnp.dot(table_set[2], real_part, precision=exact_mode, preferred_element_...]
    all_gather x4 -> x0, blocking collectives: 107 us -> none  [the longest x1 69.3 us: shards(): lax.all_gather(residues, 'own', axis=1, tiled=True)]
    pallas_call x0 -> x13, Pallas kernels: none -> 98.5 us  [the longest x4 58.9 us: back(): pl.pallas_call(back_kernel, out_shape=(full,) * 4 + (jax.ShapeDtypeStruct...]
    unnamed x1 -> x0, blocking collectives: 72 us -> none
    psum x1 -> x0, waiting for transfers between devices: 39.3 us -> none  [shards(): summed_taps = lax.psum(partial_taps, ('ctx', 'own'))]
  transfers between devices with their start and end apart: 12 -> 22, of which waited for: 2 -> 2; matrix products, arithmetic and copies ran while one was open for 32% -> 3% of each run, Pallas kernels for 0% -> 32%
where the time goes in v1:
time: 241 us; the launch traced here: 238 us
  Pallas kernels  98.5 us (41%)
  starting transfers between devices  73.5 us (30%)
  local copies, waits for them, and re-layouts  30 us (12%)
  blocking collectives  20.6 us (9%)
  waiting for transfers between devices  11.2 us (5%)
  other arithmetic  3.08 us (1%)
    pallas_call x4, Pallas kernels, back(): pl.pallas_call(back_kernel, out_shape=(full,) * 4 + (jax.ShapeDtypeStruct...  58.9 us
    ppermute x13, starting transfers between devices, shift(): lax.ppermute(value, AXES, [(at, at + steps) for at in range(first, last)])  42.2 us
    pallas_call x4, Pallas kernels, front(): pl.pallas_call(front_kernel, out_shape=(part,) * 5 + (state,) * 2, grid_s...  27.4 us
    unnamed x128, local copies, waits for them, and re-layouts  24.6 us
    all_to_all x1, blocking collectives, shards(): arrived = lax.all_to_all(states, AXES, 0, 0, tiled=True)  20.6 us
    all_to_all x1, starting transfers between devices, shards(): lax.all_to_all(pieces.reshape(ctxs * owners, share, 128), AXES, 0, 0, til...  11.3 us
    ppermute x6, waiting for transfers between devices, gather_own(): lax.ppermute(value, 'own', [(at, (at + hop) % count) for at in range(coun...  11.2 us
    pallas_call x4, Pallas kernels, tail(): pl.pallas_call(tail_kernel, out_shape=(thin,) * 3, grid_spec=pltpu.Prefet...  10.6 us
  transfers between devices with their start and end apart: 22, of which 2 were waited for; matrix products, arithmetic and copies ran while one was open for 3% of the time, Pallas kernels for 32%

profile of v1, /device:TPU:18, one launch (start us, length us, event | category | flops | bytes accessed | tf_op | source)
XLA Modules:
  0.0 238.4 jit_solution(17682174316840703158)
XLA Ops:
  0.7 0.9 reshape.34
  1.5 1.3 collective-permute-start.1
  3.4 1.1 collective-permute-start.3
  4.5 0.9 slice.10
  5.4 0.9 slice.11
  6.3 0.9 slice.9
  7.3 3.0 %collective-permute-start = (bf16[24,8192]{1,0:T(8,128)(2,1)S(1)}, bf16[24,8192]{1,0:T(8,128)(2,1)S(1)}, u32[]{:S(2)}, u32[]{:S(2)}) collective-permute-start(bf16[24,8192]{1,0:T(8,128)(2,1)S(1)} %pad_maximum_fusion.1), channel_id=1, source_target_pairs={{0,1},{1,2},{2,3},{3,4},{4,5},{5,6},{6,7},{7,8},{8,9},{9,10},{10,1... | collective-permute-start | bytes 1179656 | tf_op jit(solution)/shard_map/ppermute | solution.py:287
  10.3 0.9 multiply_bitcast_fusion
  11.3 1.6 fusion
  12.8 1.8 collective-permute-start.4
  14.7 0.9 collective-permute-start.5
  15.6 2.6 %collective-permute-start.6 = (f32[384,128]{1,0:T(8,128)}, f32[384,128]{1,0:T(8,128)S(1)}, u32[]{:S(2)}, u32[]{:S(2)}) collective-permute-start(f32[384,128]{1,0:T(8,128)} %get-tuple-element.142), channel_id=1, source_target_pairs={{0,3},{1,0},{2,1},{3,2},{4,7},{5,4},{6,5},{7,6},{8,11},{9,8},{10,9... | collective-permute-start | bytes 589832 | tf_op jit(solution)/shard_map/ppermute | solution.py:294
  18.3 6.6 %collective-permute-done.4 = f32[384,128]{1,0:T(8,128)S(1)} collective-permute-done((f32[384,128]{1,0:T(8,128)}, f32[384,128]{1,0:T(8,128)S(1)}, u32[]{:S(2)}, u32[]{:S(2)}) %collective-permute-start.4) | collective-permute-done | bytes 196640 | tf_op jit(solution)/shard_map/ppermute | solution.py:294
  24.9 4.6 %collective-permute-done.5 = f32[384,128]{1,0:T(8,128)S(1)} collective-permute-done((f32[384,128]{1,0:T(8,128)}, f32[384,128]{1,0:T(8,128)S(1)}, u32[]{:S(2)}, u32[]{:S(2)}) %collective-permute-start.5) | collective-permute-done | bytes 196640 | tf_op jit(solution)/shard_map/ppermute | solution.py:294
  29.6 1.8 copy-done.2
  31.4 1.6 copy-done.3
  33.0 1.6 copy-done.4
  34.6 7.2 %front0.1 = (bf16[128,2048]{1,0:T(8,128)(2,1)S(1)}, bf16[128,2048]{1,0:T(8,128)(2,1)S(1)}, bf16[128,2048]{1,0:T(8,128)(2,1)S(1)}, bf16[128,2048]{1,0:T(8,128)(2,...) custom-call(s32[3]{0:T(128)S(1)} %pad_add_fusion.me, ...), custom_call_target="tpu_custom_call" | custom-call | flops 2000000000 | bytes 10000000 | tf_op jit(solution)/shard_map/front0/pallas_call | solution.py:340
  41.8 0.8 copy-done.48
  42.6 0.8 copy-done.50
  44.2 2.6 %collective-permute-start.13 = (bf16[128,2048]{1,0:T(8,128)(2,1)}, bf16[128,2048]{1,0:T(8,128)(2,1)}, u32[]{:S(2)}, u32[]{:S(2)}) collective-permute-start(bf16[128,2048]{1,0:T(8,128)(2,1)} %get-tuple-element.99.prod), channel_id=1, source_target_pairs={{0,1},{1,2},{2,3},{3,4},{4,5},{5,6},{6,7},{7,8},{8,9},{9,10},{10,1... | collective-permute-start | bytes 1572872 | tf_op jit(solution)/shard_map/ppermute | solution.py:287
  46.8 3.2 %collective-permute-start.14 = (bf16[128,2048]{1,0:T(8,128)(2,1)}, bf16[128,2048]{1,0:T(8,128)(2,1)}, u32[]{:S(2)}, u32[]{:S(2)}) collective-permute-start(bf16[128,2048]{1,0:T(8,128)(2,1)} %get-tuple-element.100.gconv), channel_id=1, source_target_pairs={{1,0},{2,1},{3,2},{4,3},{5,4},{6,5},{7,6},{8,7},{9,8},{10,9},{11,1... | collective-permute-start | bytes 1572872 | tf_op jit(solution)/shard_map/ppermute | solution.py:287
  50.0 6.5 %front1.1 = (bf16[128,2048]{1,0:T(8,128)(2,1)S(1)}, bf16[128,2048]{1,0:T(8,128)(2,1)S(1)}, bf16[128,2048]{1,0:T(8,128)(2,1)S(1)}, bf16[128,2048]{1,0:T(8,128)(2,...) custom-call(s32[3]{0:T(128)S(1)} %pad_add_fusion.me, ...), custom_call_target="tpu_custom_call" | custom-call | flops 2000000000 | bytes 10000000 | tf_op jit(solution)/shard_map/front1/pallas_call | solution.py:340
  57.4 0.8 copy-done.31
  58.2 0.8 copy-done.33
  59.0 0.8 copy-done.35
  59.9 0.8 copy-done.37
  60.7 6.5 %front2.1 = (bf16[128,2048]{1,0:T(8,128)(2,1)S(1)}, bf16[128,2048]{1,0:T(8,128)(2,1)S(1)}, bf16[128,2048]{1,0:T(8,128)(2,1)S(1)}, bf16[128,2048]{1,0:T(8,128)(2,...) custom-call(s32[3]{0:T(128)S(1)} %pad_add_fusion.me, ...), custom_call_target="tpu_custom_call" | custom-call | flops 2000000000 | bytes 10000000 | tf_op jit(solution)/shard_map/front2/pallas_call | solution.py:340
  67.2 0.8 copy-done.18
  68.0 0.8 copy-done.20
  68.8 0.8 copy-done.22
  69.6 0.8 copy-done.24
  70.5 0.8 copy-done.27
  71.3 7.2 %front3.1 = (bf16[128,2048]{1,0:T(8,128)(2,1)S(1)}, bf16[128,2048]{1,0:T(8,128)(2,1)S(1)}, bf16[128,2048]{1,0:T(8,128)(2,1)S(1)}, bf16[128,2048]{1,0:T(8,128)(2,...) custom-call(s32[3]{0:T(128)S(1)} %pad_add_fusion.me, ...), custom_call_target="tpu_custom_call" | custom-call | flops 2000000000 | bytes 10000000 | tf_op jit(solution)/shard_map/front3/pallas_call | solution.py:340
  78.4 0.8 copy-done.12
  79.3 0.8 copy-done.14
  80.1 0.8 copy-done.16
  81.0 20.6 %all_to_all.20.states = bf16[128,8,128]{2,1,0:T(8,128)(2,1)S(1)} all-to-all(bf16[128,8,128]{2,1,0:T(8,128)(2,1)S(1)} %constant_dynamic-update-slice_fusion), channel_id=1, replica_groups=mesh['ctx'=32,'own'=4] {'ctx','own'}, dimensions={0} | all-to-all | bytes 524288 | tf_op jit(solution)/shard_map/all_to_all | solution.py:372
  101.6 1.6 scan.1
  103.3 6.7 %all-to-all-start.1 = ((bf16[128,8,128]{2,1,0:T(8,128)(2,1)}), bf16[128,8,128]{2,1,0:T(8,128)(2,1)S(1)}, u32[]{:S(2)}, u32[]{:S(2)}) async-start(bf16[128,8,128]{2,1,0:T(8,128)(2,1)} %scan.1), calls=%async_computation.1 | async-start | bytes 524288 | tf_op jit(solution)/shard_map/all_to_all | solution.py:391
  110.0 3.1 %collective-permute-start.11 = (bf16[128,2048]{1,0:T(8,128)(2,1)}, bf16[128,2048]{1,0:T(8,128)(2,1)}, u32[]{:S(2)}, u32[]{:S(2)}) collective-permute-start(bf16[128,2048]{1,0:T(8,128)(2,1)} %copy-done.35), channel_id=1, source_target_pairs={{0,1},{1,2},{2,3},{3,4},{4,5},{5,6},{6,7},{7,8},{8,9},{9,10},{10,1... | collective-permute-start | bytes 1572872 | tf_op jit(solution)/shard_map/ppermute | solution.py:287
  113.1 2.7 %collective-permute-start.12 = (bf16[128,2048]{1,0:T(8,128)(2,1)}, bf16[128,2048]{1,0:T(8,128)(2,1)}, u32[]{:S(2)}, u32[]{:S(2)}) collective-permute-start(bf16[128,2048]{1,0:T(8,128)(2,1)} %copy-done.37), channel_id=1, source_target_pairs={{1,0},{2,1},{3,2},{4,3},{5,4},{6,5},{7,6},{8,7},{9,8},{10,9},{11,1... | collective-permute-start | bytes 1572872 | tf_op jit(solution)/shard_map/ppermute | solution.py:287
  115.8 2.5 %collective-permute-start.10 = (bf16[128,2048]{1,0:T(8,128)(2,1)}, bf16[128,2048]{1,0:T(8,128)(2,1)}, u32[]{:S(2)}, u32[]{:S(2)}) collective-permute-start(bf16[128,2048]{1,0:T(8,128)(2,1)} %copy-done.27), channel_id=1, source_target_pairs={{1,0},{2,1},{3,2},{4,3},{5,4},{6,5},{7,6},{8,7},{9,8},{10,9},{11,1... | collective-permute-start | bytes 1572872 | tf_op jit(solution)/shard_map/ppermute | solution.py:287
  118.3 3.4 %collective-permute-start.9 = (bf16[128,2048]{1,0:T(8,128)(2,1)S(1)}, bf16[128,2048]{1,0:T(8,128)(2,1)}, u32[]{:S(2)}, u32[]{:S(2)}) collective-permute-start(bf16[128,2048]{1,0:T(8,128)(2,1)S(1)} %copy-done.25), channel_id=1, source_target_pairs={{0,1},{1,2},{2,3},{3,4},{4,5},{5,6},{6,7},{7,8},{8,9},{9,10},{10,1... | collective-permute-start | bytes 1572872 | tf_op jit(solution)/shard_map/ppermute | solution.py:287
  121.7 4.1 %collective-permute-start.7 = (bf16[128,2048]{1,0:T(8,128)(2,1)}, bf16[128,2048]{1,0:T(8,128)(2,1)}, u32[]{:S(2)}, u32[]{:S(2)}) collective-permute-start(bf16[128,2048]{1,0:T(8,128)(2,1)} %get-tuple-element.76.prod), channel_id=1, source_target_pairs={{0,1},{1,2},{2,3},{3,4},{4,5},{5,6},{6,7},{7,8},{8,9},{9,10},{10,1... | collective-permute-start | bytes 1572872 | tf_op jit(solution)/shard_map/ppermute | solution.py:287
  125.9 1.0 copy-done.49
  126.9 1.0 copy-done.51
  128.0 1.0 copy-done.53
  129.1 14.9 %back0.1 = (bf16[128,8192]{1,0:T(8,128)(2,1)}, bf16[128,8192]{1,0:T(8,128)(2,1)}, bf16[128,8192]{1,0:T(8,128)(2,1)}, bf16[128,8192]{1,0:T(8,128)(2,1)}, bf16[24,...) custom-call(s32[3]{0:T(128)S(1)} %pad_add_fusion.me, bf16[128,2048]{1,0:T(8,128)(2,1)S(1)} %copy-done.49, ...), custom_call_target="tpu_custom_call" | custom-call | flops 4000000000 | bytes 16000000 | tf_op jit(solution)/shard_map/back0/pallas_call | solution.py:425
  144.6 3.0 %collective-permute-start.8 = (bf16[128,2048]{1,0:T(8,128)(2,1)S(1)}, bf16[128,2048]{1,0:T(8,128)(2,1)S(1)}, u32[]{:S(2)}, u32[]{:S(2)}) collective-permute-start(bf16[128,2048]{1,0:T(8,128)(2,1)S(1)} %copy-done.17), channel_id=1, source_target_pairs={{1,0},{2,1},{3,2},{4,3},{5,4},{6,5},{7,6},{8,7},{9,8},{10,9},{11,1... | collective-permute-start | bytes 1572872 | tf_op jit(solution)/shard_map/ppermute | solution.py:287
  147.7 14.7 %back1.1 = (bf16[128,8192]{1,0:T(8,128)(2,1)}, bf16[128,8192]{1,0:T(8,128)(2,1)}, bf16[128,8192]{1,0:T(8,128)(2,1)}, bf16[128,8192]{1,0:T(8,128)(2,1)}, bf16[24,...) custom-call(s32[3]{0:T(128)S(1)} %pad_add_fusion.me, ...), custom_call_target="tpu_custom_call", output_to_operand_aliasing={{0}: (24, {}), {1}: (25, {}), {2}: (26, {}), {3}: (27, {})} | custom-call | flops 4000000000 | bytes 16000000 | tf_op jit(solution)/shard_map/back1/pallas_call | solution.py:425
  163.1 14.6 %back2.1 = (bf16[128,8192]{1,0:T(8,128)(2,1)}, bf16[128,8192]{1,0:T(8,128)(2,1)}, bf16[128,8192]{1,0:T(8,128)(2,1)}, bf16[128,8192]{1,0:T(8,128)(2,1)}, bf16[24,...) custom-call(s32[3]{0:T(128)S(1)} %pad_add_fusion.me, ...), custom_call_target="tpu_custom_call", output_to_operand_aliasing={{0}: (24, {}), {1}: (25, {}), {2}: (26, {}), {3}: (27, {})} | custom-call | flops 4000000000 | bytes 16000000 | tf_op jit(solution)/shard_map/back2/pallas_call | solution.py:425
  178.5 14.6 %back3.1 = (bf16[128,8192]{1,0:T(8,128)(2,1)}, bf16[128,8192]{1,0:T(8,128)(2,1)}, bf16[128,8192]{1,0:T(8,128)(2,1)}, bf16[128,8192]{1,0:T(8,128)(2,1)}, bf16[24,...) custom-call(s32[3]{0:T(128)S(1)} %pad_add_fusion.me, ...), custom_call_target="tpu_custom_call", output_to_operand_aliasing={{0}: (24, {}), {1}: (25, {}), {2}: (26, {}), {3}: (27, {})} | custom-call | flops 4000000000 | bytes 16000000 | tf_op jit(solution)/shard_map/back3/pallas_call | solution.py:425
  194.4 0.9 copy.55
  195.3 11.3 %all-to-all-start.2 = ((f32[128,4,128]{2,1,0:T(4,128)}), f32[128,4,128]{2,1,0:T(4,128)S(1)}, u32[]{:S(2)}, u32[]{:S(2)}) async-start(f32[128,4,128]{2,1,0:T(4,128)} %copy.55), calls=%async_computation.2 | async-start | bytes 524288 | tf_op jit(solution)/shard_map/all_to_all | solution.py:503
  206.6 2.5 %collective-permute-start.18 = (bf16[24,2048]{1,0:T(8,128)(2,1)S(1)}, bf16[24,2048]{1,0:T(8,128)(2,1)S(1)}, u32[]{:S(2)}, u32[]{:S(2)}) collective-permute-start(bf16[24,2048]{1,0:T(8,128)(2,1)S(1)} %copy-done.55), channel_id=1, source_target_pairs={{1,0},{2,1},{3,2},{4,3},{5,4},{6,5},{7,6},{8,7},{9,8},{10,9},{11,1... | collective-permute-start | bytes 294920 | tf_op jit(solution)/shard_map/ppermute | solution.py:287
  209.1 2.5 %collective-permute-start.17 = (bf16[24,2048]{1,0:T(8,128)(2,1)S(1)}, bf16[24,2048]{1,0:T(8,128)(2,1)S(1)}, u32[]{:S(2)}, u32[]{:S(2)}) collective-permute-start(bf16[24,2048]{1,0:T(8,128)(2,1)S(1)} %copy-done.57), channel_id=1, source_target_pairs={{1,0},{2,1},{3,2},{4,3},{5,4},{6,5},{7,6},{8,7},{9,8},{10,9},{11,1... | collective-permute-start | bytes 294920 | tf_op jit(solution)/shard_map/ppermute | solution.py:287
  211.6 7.3 %collective-permute-start.16 = (bf16[24,2048]{1,0:T(8,128)(2,1)S(1)}, bf16[24,2048]{1,0:T(8,128)(2,1)S(1)}, u32[]{:S(2)}, u32[]{:S(2)}) collective-permute-start(bf16[24,2048]{1,0:T(8,128)(2,1)S(1)} %copy-done.59), channel_id=1, source_target_pairs={{1,0},{2,1},{3,2},{4,3},{5,4},{6,5},{7,6},{8,7},{9,8},{10,9},{11,1... | collective-permute-start | bytes 294920 | tf_op jit(solution)/shard_map/ppermute | solution.py:287
  218.9 2.4 %collective-permute-start.15 = (bf16[24,2048]{1,0:T(8,128)(2,1)S(1)}, bf16[24,2048]{1,0:T(8,128)(2,1)S(1)}, u32[]{:S(2)}, u32[]{:S(2)}) collective-permute-start(bf16[24,2048]{1,0:T(8,128)(2,1)S(1)} %get-tuple-element.115), channel_id=1, source_target_pairs={{1,0},{2,1},{3,2},{4,3},{5,4},{6,5},{7,6},{8,7},{9,8},{10,9},{11,1... | collective-permute-start | bytes 294920 | tf_op jit(solution)/shard_map/ppermute | solution.py:287
  222.1 5.0 %all-to-all-start.3 = ((f32[32,4,128]{2,1,0:T(4,128)}), f32[32,4,128]{2,1,0:T(4,128)S(1)}, u32[]{:S(2)}, u32[]{:S(2)}) async-start(f32[32,4,128]{2,1,0:T(4,128)} %broadcast_in_dim.2), calls=%async_computation.3 | async-start | bytes 131072 | tf_op jit(solution)/shard_map/all_to_all | solution.py:506
  227.1 2.6 %tail0.1 = (bf16[128,8192]{1,0:T(8,128)(2,1)}, bf16[128,8192]{1,0:T(8,128)(2,1)}, bf16[128,8192]{1,0:T(8,128)(2,1)}) custom-call(s32[3]{0:T(128)S(1)} %pad_add_fusion.me, f32[48,2048]{1,0:T(8,128)S(1)} %get-tuple-element.120.last, bf16[24,2048]{1,0:T(8,128)(2,1)S(1)} %collective-permute-done.18.rim, ...), custom_call_target="tpu_custom_call", output_to_operand_aliasing={{0}: (4, {}), {1}: (5, {}), {2}: (6, {})} | custom-call | tf_op jit(solution)/shard_map/tail0/pallas_call | solution.py:476
  229.8 2.6 %tail1.1 = (bf16[128,8192]{1,0:T(8,128)(2,1)}, bf16[128,8192]{1,0:T(8,128)(2,1)}, bf16[128,8192]{1,0:T(8,128)(2,1)}) custom-call(s32[3]{0:T(128)S(1)} %pad_add_fusion.me, f32[48,2048]{1,0:T(8,128)S(1)} %copy-done.40, bf16[24,2048]{1,0:T(8,128)(2,1)S(1)} %collective-permute-done.17.rim, ...), custom_call_target="tpu_custom_call", output_to_operand_aliasing={{0}: (4, {}), {1}: (5, {}), {2}: (6, {})} | custom-call | tf_op jit(solution)/shard_map/tail1/pallas_call | solution.py:476
  232.4 2.6 %tail2.1 = (bf16[128,8192]{1,0:T(8,128)(2,1)}, bf16[128,8192]{1,0:T(8,128)(2,1)}, bf16[128,8192]{1,0:T(8,128)(2,1)}) custom-call(s32[3]{0:T(128)S(1)} %pad_add_fusion.me, f32[48,2048]{1,0:T(8,128)S(1)} %copy-done.42, bf16[24,2048]{1,0:T(8,128)(2,1)S(1)} %collective-permute-done.16.rim, ...), custom_call_target="tpu_custom_call", output_to_operand_aliasing={{0}: (4, {}), {1}: (5, {}), {2}: (6, {})} | custom-call | tf_op jit(solution)/shard_map/tail2/pallas_call | solution.py:476
  235.1 2.6 %tail3.1 = (bf16[128,8192]{1,0:T(8,128)(2,1)}, bf16[128,8192]{1,0:T(8,128)(2,1)}, bf16[128,8192]{1,0:T(8,128)(2,1)}) custom-call(s32[3]{0:T(128)S(1)} %pad_add_fusion.me, f32[48,2048]{1,0:T(8,128)S(1)} %copy-done.44, bf16[24,2048]{1,0:T(8,128)(2,1)S(1)} %collective-permute-done.15.rim, ...), custom_call_target="tpu_custom_call", output_to_operand_aliasing={{0}: (4, {}), {1}: (5, {}), {2}: (6, {})} | custom-call | tf_op jit(solution)/shard_map/tail3/pallas_call | solution.py:476
  (143 shorter events, 7.4 us)
Async XLA Ops:
  0.6 28.9 %copy-start.47 = (bf16[32,256]{1,0:T(8,128)(2,1)S(1)}, bf16[32,256]{1,0:T(8,128)(2,1)}, u32[]{:S(2)}) copy-start(bf16[32,256]{1,0:T(8,128)(2,1)} %constant.65.clone.moment) | copy-start | bytes 49156
  0.6 28.9 %copy-start.1 = (bf16[128,8192]{1,0:T(8,128)(2,1)S(1)}, bf16[128,8192]{1,0:T(8,128)(2,1)}, u32[]{:S(2)}) copy-start(bf16[128,8192]{1,0:T(8,128)(2,1)} %g.15) | copy-start | bytes 6291460
  1.5 13.1 %collective-permute-start.1 = (f32[24,128]{1,0:T(8,128)S(1)}, f32[24,128]{1,0:T(8,128)S(1)}, u32[]{:S(2)}, u32[]{:S(2)}) collective-permute-start(f32[24,128]{1,0:T(8,128)S(1)} %get-tuple-element.144), channel_id=1, source_target_pairs={{0,1},{1,2},{2,3},{3,0},{4,5},{5,6},{6,7},{7,4},{8,9},{9,10},{10,1... | collective-permute-start | bytes 36872 | tf_op jit(solution)/shard_map/ppermute | solution.py:294
  2.8 12.8 %collective-permute-start.2 = (f32[24,128]{1,0:T(8,128)S(1)}, f32[24,128]{1,0:T(8,128)S(1)}, u32[]{:S(2)}, u32[]{:S(2)}) collective-permute-start(f32[24,128]{1,0:T(8,128)S(1)} %get-tuple-element.144), channel_id=1, source_target_pairs={{0,2},{1,3},{2,0},{3,1},{4,6},{5,7},{6,4},{7,5},{8,10},{9,11},{10,... | collective-permute-start | bytes 36872 | tf_op jit(solution)/shard_map/ppermute | solution.py:294
  3.4 14.9 %collective-permute-start.3 = (f32[24,128]{1,0:T(8,128)S(1)}, f32[24,128]{1,0:T(8,128)S(1)}, u32[]{:S(2)}, u32[]{:S(2)}) collective-permute-start(f32[24,128]{1,0:T(8,128)S(1)} %get-tuple-element.144), channel_id=1, source_target_pairs={{0,3},{1,0},{2,1},{3,2},{4,7},{5,4},{6,5},{7,6},{8,11},{9,8},{10,9... | collective-permute-start | bytes 36872 | tf_op jit(solution)/shard_map/ppermute | solution.py:294
  7.3 22.3 %collective-permute-start = (bf16[24,8192]{1,0:T(8,128)(2,1)S(1)}, bf16[24,8192]{1,0:T(8,128)(2,1)S(1)}, u32[]{:S(2)}, u32[]{:S(2)}) collective-permute-start(bf16[24,8192]{1,0:T(8,128)(2,1)S(1)} %pad_maximum_fusion.1), channel_id=1, source_target_pairs={{0,1},{1,2},{2,3},{3,4},{4,5},{5,6},{6,7},{7,8},{8,9},{9,10},{10,1... | collective-permute-start | bytes 1179656 | tf_op jit(solution)/shard_map/ppermute | solution.py:287
  12.8 12.1 %collective-permute-start.4 = (f32[384,128]{1,0:T(8,128)}, f32[384,128]{1,0:T(8,128)S(1)}, u32[]{:S(2)}, u32[]{:S(2)}) collective-permute-start(f32[384,128]{1,0:T(8,128)} %get-tuple-element.142), channel_id=1, source_target_pairs={{0,1},{1,2},{2,3},{3,0},{4,5},{5,6},{6,7},{7,4},{8,9},{9,10},{10,1... | collective-permute-start | bytes 589832 | tf_op jit(solution)/shard_map/ppermute | solution.py:294
  14.7 14.8 %collective-permute-start.5 = (f32[384,128]{1,0:T(8,128)}, f32[384,128]{1,0:T(8,128)S(1)}, u32[]{:S(2)}, u32[]{:S(2)}) collective-permute-start(f32[384,128]{1,0:T(8,128)} %get-tuple-element.142), channel_id=1, source_target_pairs={{0,2},{1,3},{2,0},{3,1},{4,6},{5,7},{6,4},{7,5},{8,10},{9,11},{10,... | collective-permute-start | bytes 589832 | tf_op jit(solution)/shard_map/ppermute | solution.py:294
  15.6 13.9 %collective-permute-start.6 = (f32[384,128]{1,0:T(8,128)}, f32[384,128]{1,0:T(8,128)S(1)}, u32[]{:S(2)}, u32[]{:S(2)}) collective-permute-start(f32[384,128]{1,0:T(8,128)} %get-tuple-element.142), channel_id=1, source_target_pairs={{0,3},{1,0},{2,1},{3,2},{4,7},{5,4},{6,5},{7,6},{8,11},{9,8},{10,9... | collective-permute-start | bytes 589832 | tf_op jit(solution)/shard_map/ppermute | solution.py:294
  29.5 72.1 %copy-start = (f32[4,384,128]{2,1,0:T(8,128)}, f32[4,384,128]{2,1,0:T(8,128)S(1)}, u32[]{:S(2)}) copy-start(f32[4,384,128]{2,1,0:T(8,128)S(1)} %pad_maximum_fusion.rates.weights.ltaps) | copy-start | bytes 2359300
  29.6 1.9 copy-start.2
  31.4 1.6 copy-start.3
  33.0 1.6 copy-start.4
  44.2 74.1 %collective-permute-start.13 = (bf16[128,2048]{1,0:T(8,128)(2,1)}, bf16[128,2048]{1,0:T(8,128)(2,1)}, u32[]{:S(2)}, u32[]{:S(2)}) collective-permute-start(bf16[128,2048]{1,0:T(8,128)(2,1)} %get-tuple-element.99.prod), channel_id=1, source_target_pairs={{0,1},{1,2},{2,3},{3,4},{4,5},{5,6},{6,7},{7,8},{8,9},{9,10},{10,1... | collective-permute-start | bytes 1572872 | tf_op jit(solution)/shard_map/ppermute | solution.py:287
  46.8 74.9 %collective-permute-start.14 = (bf16[128,2048]{1,0:T(8,128)(2,1)}, bf16[128,2048]{1,0:T(8,128)(2,1)}, u32[]{:S(2)}, u32[]{:S(2)}) collective-permute-start(bf16[128,2048]{1,0:T(8,128)(2,1)} %get-tuple-element.100.gconv), channel_id=1, source_target_pairs={{1,0},{2,1},{3,2},{4,3},{5,4},{6,5},{7,6},{8,7},{9,8},{10,9},{11,1... | collective-permute-start | bytes 1572872 | tf_op jit(solution)/shard_map/ppermute | solution.py:287
  58.2 0.9 copy-start.33
  59.0 0.8 copy-start.35
  80.8 37.5 %copy-start.25 = (bf16[128,2048]{1,0:T(8,128)(2,1)S(1)}, bf16[128,2048]{1,0:T(8,128)(2,1)}, u32[]{:S(2)}) copy-start(bf16[128,2048]{1,0:T(8,128)(2,1)} %copy-done.24) | copy-start | bytes 1572868
  80.9 45.0 %copy-start.5 = (bf16[256,384]{1,0:T(8,128)(2,1)S(1)}, bf16[256,384]{1,0:T(8,128)(2,1)}, u32[]{:S(2)}) copy-start(bf16[256,384]{1,0:T(8,128)(2,1)} %constant.69.clone.t_taps) | copy-start | bytes 589828
  80.9 45.0 %copy-start.6 = (bf16[128,768]{1,0:T(8,128)(2,1)S(1)}, bf16[128,768]{1,0:T(8,128)(2,1)}, u32[]{:S(2)}) copy-start(bf16[128,768]{1,0:T(8,128)(2,1)} %constant.72.clone.t_inv3) | copy-start | bytes 589828
  80.9 45.0 %copy-start.7 = (bf16[256,256]{1,0:T(8,128)(2,1)S(1)}, bf16[256,256]{1,0:T(8,128)(2,1)}, u32[]{:S(2)}) copy-start(bf16[256,256]{1,0:T(8,128)(2,1)} %constant.66.clone.t_own) | copy-start | bytes 393220
  80.9 45.0 %copy-start.8 = (bf16[256,256]{1,0:T(8,128)(2,1)S(1)}, bf16[256,256]{1,0:T(8,128)(2,1)}, u32[]{:S(2)}) copy-start(bf16[256,256]{1,0:T(8,128)(2,1)} %constant.67.clone.t_before) | copy-start | bytes 393220
  80.9 45.0 %copy-start.9 = (bf16[256,256]{1,0:T(8,128)(2,1)S(1)}, bf16[256,256]{1,0:T(8,128)(2,1)}, u32[]{:S(2)}) copy-start(bf16[256,256]{1,0:T(8,128)(2,1)} %constant.68.clone.t_after) | copy-start | bytes 393220
  80.9 45.0 %copy-start.10 = (bf16[256,48]{1,0:T(8,128)(2,1)S(1)}, bf16[256,48]{1,0:T(8,128)(2,1)}, u32[]{:S(2)}) copy-start(bf16[256,48]{1,0:T(8,128)(2,1)} %constant.70.clone.t_head) | copy-start | bytes 73732
  80.9 45.0 %copy-start.11 = (bf16[128,256]{1,0:T(8,128)(2,1)S(1)}, bf16[128,256]{1,0:T(8,128)(2,1)}, u32[]{:S(2)}) copy-start(bf16[128,256]{1,0:T(8,128)(2,1)} %constant.71.clone.t_inv) | copy-start | bytes 196612
  80.9 45.0 %copy-start.45 = (bf16[128,48]{1,0:T(8,128)(2,1)S(1)}, bf16[128,48]{1,0:T(8,128)(2,1)}, u32[]{:S(2)}) copy-start(bf16[128,48]{1,0:T(8,128)(2,1)} %constant.73.clone.t_ahead) | copy-start | bytes 36868
  80.9 45.0 %copy-start.46 = (bf16[128,48]{1,0:T(8,128)(2,1)S(1)}, bf16[128,48]{1,0:T(8,128)(2,1)}, u32[]{:S(2)}) copy-start(bf16[128,48]{1,0:T(8,128)(2,1)} %constant.74.clone.t_behind) | copy-start | bytes 36868
  103.3 22.5 %all-to-all-start.1 = ((bf16[128,8,128]{2,1,0:T(8,128)(2,1)}), bf16[128,8,128]{2,1,0:T(8,128)(2,1)S(1)}, u32[]{:S(2)}, u32[]{:S(2)}) async-start(bf16[128,8,128]{2,1,0:T(8,128)(2,1)} %scan.1), calls=%async_computation.1 | async-start | bytes 524288 | tf_op jit(solution)/shard_map/all_to_all | solution.py:391
  110.0 34.7 %collective-permute-start.11 = (bf16[128,2048]{1,0:T(8,128)(2,1)}, bf16[128,2048]{1,0:T(8,128)(2,1)}, u32[]{:S(2)}, u32[]{:S(2)}) collective-permute-start(bf16[128,2048]{1,0:T(8,128)(2,1)} %copy-done.35), channel_id=1, source_target_pairs={{0,1},{1,2},{2,3},{3,4},{4,5},{5,6},{6,7},{7,8},{8,9},{9,10},{10,1... | collective-permute-start | bytes 1572872 | tf_op jit(solution)/shard_map/ppermute | solution.py:287
  113.1 34.5 %collective-permute-start.12 = (bf16[128,2048]{1,0:T(8,128)(2,1)}, bf16[128,2048]{1,0:T(8,128)(2,1)}, u32[]{:S(2)}, u32[]{:S(2)}) collective-permute-start(bf16[128,2048]{1,0:T(8,128)(2,1)} %copy-done.37), channel_id=1, source_target_pairs={{1,0},{2,1},{3,2},{4,3},{5,4},{6,5},{7,6},{8,7},{9,8},{10,9},{11,1... | collective-permute-start | bytes 1572872 | tf_op jit(solution)/shard_map/ppermute | solution.py:287
  115.8 47.2 %collective-permute-start.10 = (bf16[128,2048]{1,0:T(8,128)(2,1)}, bf16[128,2048]{1,0:T(8,128)(2,1)}, u32[]{:S(2)}, u32[]{:S(2)}) collective-permute-start(bf16[128,2048]{1,0:T(8,128)(2,1)} %copy-done.27), channel_id=1, source_target_pairs={{1,0},{2,1},{3,2},{4,3},{5,4},{6,5},{7,6},{8,7},{9,8},{10,9},{11,1... | collective-permute-start | bytes 1572872 | tf_op jit(solution)/shard_map/ppermute | solution.py:287
  118.3 44.7 %collective-permute-start.9 = (bf16[128,2048]{1,0:T(8,128)(2,1)S(1)}, bf16[128,2048]{1,0:T(8,128)(2,1)}, u32[]{:S(2)}, u32[]{:S(2)}) collective-permute-start(bf16[128,2048]{1,0:T(8,128)(2,1)S(1)} %copy-done.25), channel_id=1, source_target_pairs={{0,1},{1,2},{2,3},{3,4},{4,5},{5,6},{6,7},{7,8},{8,9},{9,10},{10,1... | collective-permute-start | bytes 1572872 | tf_op jit(solution)/shard_map/ppermute | solution.py:287
  121.7 56.7 %collective-permute-start.7 = (bf16[128,2048]{1,0:T(8,128)(2,1)}, bf16[128,2048]{1,0:T(8,128)(2,1)}, u32[]{:S(2)}, u32[]{:S(2)}) collective-permute-start(bf16[128,2048]{1,0:T(8,128)(2,1)} %get-tuple-element.76.prod), channel_id=1, source_target_pairs={{0,1},{1,2},{2,3},{3,4},{4,5},{5,6},{6,7},{7,8},{8,9},{9,10},{10,1... | collective-permute-start | bytes 1572872 | tf_op jit(solution)/shard_map/ppermute | solution.py:287
  125.9 1.0 copy-start.49
  126.9 1.0 copy-start.51
  128.0 1.0 copy-start.53
  129.0 15.6 %copy-start.17 = (bf16[128,2048]{1,0:T(8,128)(2,1)S(1)}, bf16[128,2048]{1,0:T(8,128)(2,1)}, u32[]{:S(2)}) copy-start(bf16[128,2048]{1,0:T(8,128)(2,1)} %copy-done.16) | copy-start | bytes 1572868
  129.0 18.6 %copy-start.30 = (bf16[128,2048]{1,0:T(8,128)(2,1)S(1)}, bf16[128,2048]{1,0:T(8,128)(2,1)}, u32[]{:S(2)}) copy-start(bf16[128,2048]{1,0:T(8,128)(2,1)} %copy-done.29) | copy-start | bytes 1572868
  129.0 18.6 %copy-start.32 = (bf16[128,2048]{1,0:T(8,128)(2,1)S(1)}, bf16[128,2048]{1,0:T(8,128)(2,1)}, u32[]{:S(2)}) copy-start(bf16[128,2048]{1,0:T(8,128)(2,1)} %copy-done.31) | copy-start | bytes 1572868
  129.0 18.6 %copy-start.34 = (bf16[128,2048]{1,0:T(8,128)(2,1)S(1)}, bf16[128,2048]{1,0:T(8,128)(2,1)}, u32[]{:S(2)}) copy-start(bf16[128,2048]{1,0:T(8,128)(2,1)} %copy-done.33) | copy-start | bytes 1572868
  129.0 18.6 %copy-start.36 = (bf16[128,2048]{1,0:T(8,128)(2,1)S(1)}, bf16[128,2048]{1,0:T(8,128)(2,1)}, u32[]{:S(2)}) copy-start(bf16[128,2048]{1,0:T(8,128)(2,1)} %copy-done.35) | copy-start | bytes 1572868
  129.0 18.6 %copy-start.38 = (bf16[128,2048]{1,0:T(8,128)(2,1)S(1)}, bf16[128,2048]{1,0:T(8,128)(2,1)}, u32[]{:S(2)}) copy-start(bf16[128,2048]{1,0:T(8,128)(2,1)} %copy-done.37) | copy-start | bytes 1572868
  144.6 33.8 %collective-permute-start.8 = (bf16[128,2048]{1,0:T(8,128)(2,1)S(1)}, bf16[128,2048]{1,0:T(8,128)(2,1)S(1)}, u32[]{:S(2)}, u32[]{:S(2)}) collective-permute-start(bf16[128,2048]{1,0:T(8,128)(2,1)S(1)} %copy-done.17), channel_id=1, source_target_pairs={{1,0},{2,1},{3,2},{4,3},{5,4},{6,5},{7,6},{8,7},{9,8},{10,9},{11,1... | collective-permute-start | bytes 1572872 | tf_op jit(solution)/shard_map/ppermute | solution.py:287
  147.7 15.4 %copy-start.19 = (bf16[128,2048]{1,0:T(8,128)(2,1)S(1)}, bf16[128,2048]{1,0:T(8,128)(2,1)}, u32[]{:S(2)}) copy-start(bf16[128,2048]{1,0:T(8,128)(2,1)} %copy-done.18) | copy-start | bytes 1572868
  147.7 15.4 %copy-start.21 = (bf16[128,2048]{1,0:T(8,128)(2,1)S(1)}, bf16[128,2048]{1,0:T(8,128)(2,1)}, u32[]{:S(2)}) copy-start(bf16[128,2048]{1,0:T(8,128)(2,1)} %copy-done.20) | copy-start | bytes 1572868
  147.7 15.4 %copy-start.23 = (bf16[128,2048]{1,0:T(8,128)(2,1)S(1)}, bf16[128,2048]{1,0:T(8,128)(2,1)}, u32[]{:S(2)}) copy-start(bf16[128,2048]{1,0:T(8,128)(2,1)} %copy-done.22) | copy-start | bytes 1572868
  147.7 15.4 %copy-start.26 = (bf16[128,2048]{1,0:T(8,128)(2,1)S(1)}, bf16[128,2048]{1,0:T(8,128)(2,1)}, u32[]{:S(2)}) copy-start(bf16[128,2048]{1,0:T(8,128)(2,1)} %copy-done.24) | copy-start | bytes 1572868
  147.7 15.4 %copy-start.28 = (bf16[128,2048]{1,0:T(8,128)(2,1)S(1)}, bf16[128,2048]{1,0:T(8,128)(2,1)}, u32[]{:S(2)}) copy-start(bf16[128,2048]{1,0:T(8,128)(2,1)} %copy-done.27) | copy-start | bytes 1572868
  163.0 14.7 %copy-start.39 = (f32[48,2048]{1,0:T(8,128)}, f32[48,2048]{1,0:T(8,128)S(1)}, u32[]{:S(2)}) copy-start(f32[48,2048]{1,0:T(8,128)S(1)} %get-tuple-element.118.last) | copy-start | bytes 1179652
  163.1 15.3 %copy-start.13 = (bf16[128,2048]{1,0:T(8,128)(2,1)S(1)}, bf16[128,2048]{1,0:T(8,128)(2,1)}, u32[]{:S(2)}) copy-start(bf16[128,2048]{1,0:T(8,128)(2,1)} %copy-done.12) | copy-start | bytes 1572868
  163.1 15.3 %copy-start.15 = (bf16[128,2048]{1,0:T(8,128)(2,1)S(1)}, bf16[128,2048]{1,0:T(8,128)(2,1)}, u32[]{:S(2)}) copy-start(bf16[128,2048]{1,0:T(8,128)(2,1)} %copy-done.14) | copy-start | bytes 1572868
  178.4 14.7 %copy-start.41 = (f32[48,2048]{1,0:T(8,128)}, f32[48,2048]{1,0:T(8,128)S(1)}, u32[]{:S(2)}) copy-start(f32[48,2048]{1,0:T(8,128)S(1)} %get-tuple-element.116.last) | copy-start | bytes 1179652
  193.9 12.7 %copy-start.55 = (bf16[24,2048]{1,0:T(8,128)(2,1)S(1)}, bf16[24,2048]{1,0:T(8,128)(2,1)}, u32[]{:S(2)}) copy-start(bf16[24,2048]{1,0:T(8,128)(2,1)} %copy-done.54) | copy-start | bytes 294916
  193.9 15.2 %copy-start.57 = (bf16[24,2048]{1,0:T(8,128)(2,1)S(1)}, bf16[24,2048]{1,0:T(8,128)(2,1)}, u32[]{:S(2)}) copy-start(bf16[24,2048]{1,0:T(8,128)(2,1)} %copy-done.56) | copy-start | bytes 294916
  193.9 17.7 %copy-start.59 = (bf16[24,2048]{1,0:T(8,128)(2,1)S(1)}, bf16[24,2048]{1,0:T(8,128)(2,1)}, u32[]{:S(2)}) copy-start(bf16[24,2048]{1,0:T(8,128)(2,1)} %copy-done.58) | copy-start | bytes 294916
  195.3 26.0 %all-to-all-start.2 = ((f32[128,4,128]{2,1,0:T(4,128)}), f32[128,4,128]{2,1,0:T(4,128)S(1)}, u32[]{:S(2)}, u32[]{:S(2)}) async-start(f32[128,4,128]{2,1,0:T(4,128)} %copy.55), calls=%async_computation.2 | async-start | bytes 524288 | tf_op jit(solution)/shard_map/all_to_all | solution.py:503
  206.6 20.5 %collective-permute-start.18 = (bf16[24,2048]{1,0:T(8,128)(2,1)S(1)}, bf16[24,2048]{1,0:T(8,128)(2,1)S(1)}, u32[]{:S(2)}, u32[]{:S(2)}) collective-permute-start(bf16[24,2048]{1,0:T(8,128)(2,1)S(1)} %copy-done.55), channel_id=1, source_target_pairs={{1,0},{2,1},{3,2},{4,3},{5,4},{6,5},{7,6},{8,7},{9,8},{10,9},{11,1... | collective-permute-start | bytes 294920 | tf_op jit(solution)/shard_map/ppermute | solution.py:287
  209.1 20.7 %collective-permute-start.17 = (bf16[24,2048]{1,0:T(8,128)(2,1)S(1)}, bf16[24,2048]{1,0:T(8,128)(2,1)S(1)}, u32[]{:S(2)}, u32[]{:S(2)}) collective-permute-start(bf16[24,2048]{1,0:T(8,128)(2,1)S(1)} %copy-done.57), channel_id=1, source_target_pairs={{1,0},{2,1},{3,2},{4,3},{5,4},{6,5},{7,6},{8,7},{9,8},{10,9},{11,1... | collective-permute-start | bytes 294920 | tf_op jit(solution)/shard_map/ppermute | solution.py:287
  211.6 20.9 %collective-permute-start.16 = (bf16[24,2048]{1,0:T(8,128)(2,1)S(1)}, bf16[24,2048]{1,0:T(8,128)(2,1)S(1)}, u32[]{:S(2)}, u32[]{:S(2)}) collective-permute-start(bf16[24,2048]{1,0:T(8,128)(2,1)S(1)} %copy-done.59), channel_id=1, source_target_pairs={{1,0},{2,1},{3,2},{4,3},{5,4},{6,5},{7,6},{8,7},{9,8},{10,9},{11,1... | collective-permute-start | bytes 294920 | tf_op jit(solution)/shard_map/ppermute | solution.py:287
  218.9 16.2 %collective-permute-start.15 = (bf16[24,2048]{1,0:T(8,128)(2,1)S(1)}, bf16[24,2048]{1,0:T(8,128)(2,1)S(1)}, u32[]{:S(2)}, u32[]{:S(2)}) collective-permute-start(bf16[24,2048]{1,0:T(8,128)(2,1)S(1)} %get-tuple-element.115), channel_id=1, source_target_pairs={{1,0},{2,1},{3,2},{4,3},{5,4},{6,5},{7,6},{8,7},{9,8},{10,9},{11,1... | collective-permute-start | bytes 294920 | tf_op jit(solution)/shard_map/ppermute | solution.py:287
  222.1 15.6 %all-to-all-start.3 = ((f32[32,4,128]{2,1,0:T(4,128)}), f32[32,4,128]{2,1,0:T(4,128)S(1)}, u32[]{:S(2)}, u32[]{:S(2)}) async-start(f32[32,4,128]{2,1,0:T(4,128)} %broadcast_in_dim.2), calls=%async_computation.3 | async-start | bytes 131072 | tf_op jit(solution)/shard_map/all_to_all | solution.py:506
  227.1 2.6 %copy-start.40 = (f32[48,2048]{1,0:T(8,128)S(1)}, f32[48,2048]{1,0:T(8,128)}, u32[]{:S(2)}) copy-start(f32[48,2048]{1,0:T(8,128)} %copy-done.39) | copy-start | bytes 1179652
  229.8 2.7 %copy-start.42 = (f32[48,2048]{1,0:T(8,128)S(1)}, f32[48,2048]{1,0:T(8,128)}, u32[]{:S(2)}) copy-start(f32[48,2048]{1,0:T(8,128)} %copy-done.41) | copy-start | bytes 1179652
  232.4 2.7 %copy-start.44 = (f32[48,2048]{1,0:T(8,128)S(1)}, f32[48,2048]{1,0:T(8,128)}, u32[]{:S(2)}) copy-start(f32[48,2048]{1,0:T(8,128)} %copy-done.43) | copy-start | bytes 1179652
  (18 other events, 14.0 us)

commit v2 on v1

v2 whole, which is shorter than its diff:
```python
import math

import jax
import jax.numpy as jnp
import numpy as np
from jax import lax
from jax.experimental import pallas as pl
from jax.experimental.pallas import tpu as pltpu
from jax.sharding import PartitionSpec as P

CPG = 16
BLOCK = 512
CHUNKS = 2
TERMS = 16
RATE_TOP = 0.03
AXES = ("ctx", "own")
F32, BF16 = jnp.float32, jnp.bfloat16


def split_np(table):
    high = table.astype(np.float32).astype(jnp.bfloat16)
    low = (table - high.astype(np.float64)).astype(np.float32).astype(jnp.bfloat16)
    return high, low


def series(lags):
    nodes = np.cos(np.pi * (np.arange(64) + 0.5) / 64)
    values = np.exp(-np.outer(np.asarray(lags, np.float64), RATE_TOP / 2 * (1 + nodes)))
    basis = np.cos(np.outer(np.arange(TERMS), np.pi * (np.arange(64) + 0.5) / 64))
    coeff = values @ basis.T * (2.0 / 64)
    coeff[:, 0] *= 0.5
    return coeff


def tables(rows):
    angle = np.pi * (2 * np.arange(rows) + 1) / (2 * rows)

    def forward(places):
        phase = np.outer(angle, places)
        return np.concatenate([np.cos(phase), -np.sin(phase)])

    here = np.arange(rows)
    own, before, after = forward(here), forward(here - rows), forward(here + rows)
    phase = np.outer(here, angle)
    inverse = np.concatenate([np.cos(phase), -np.sin(phase)], axis=1) / rows
    cat = np.concatenate
    pair = lambda m: cat(split_np(m), axis=1)

    def triple(m):
        high, low = split_np(m)
        return cat([high, low, high], axis=1)

    return dict(
        own=pair(own),
        before=pair(before),
        after=pair(after),
        taps=triple(own),
        head=triple(own @ series(here)),
        inverse=split_np(inverse)[0],
        inverse3=triple(inverse),
        ahead=triple(series(here + 1)),
        behind=triple(series(rows - here)),
        spread=(np.arange(16 * rows)[None, :] // CPG == here[:, None]).astype(jnp.bfloat16),
        moment=cat(
            [
                pair(series(rows - 1 - here).T),
                pair(series(here).T),
            ],
            axis=0,
        ),
    )


def dot(a, b):
    return jnp.dot(a, b, preferred_element_type=F32)


def halves(x):
    high = x.astype(BF16)
    return high, (x - high.astype(F32)).astype(BF16)


def stack3(x):
    high, low = halves(x)
    return jnp.concatenate([high, high, low], axis=0)


def spread_taps(short, spread):
    high, _ = halves(short)
    rest = short - high.astype(F32)
    mid, low = halves(rest)
    made = dot(jnp.concatenate([high, mid, low], axis=0), spread)
    return made[0:24] + made[24:48] + made[48:72]


def chebyshev(rate):
    z = rate * (2.0 / RATE_TOP) - 1.0
    terms = [jnp.ones_like(z), z]
    while len(terms) < TERMS:
        terms.append(2.0 * z * terms[-1] - terms[-2])
    return terms


def pack_kernel(q, k, v, short, rate, resid, ltaps, rim, small, big):
    for at, src in enumerate((q, k, v)):
        rim[8 * at : 8 * at + 8] = src[...]
    small[...] = jnp.zeros_like(small)
    for at in range(3):
        small[7 * at : 7 * at + 7] = short[at]
    for tile in range(rate.shape[1] // 128):
        cols = slice(128 * tile, 128 * tile + 128)
        big[8 * tile : 8 * tile + 8] = rate[:, cols]
        big[128 + 8 * tile : 136 + 8 * tile] = resid[:, cols]
    big[256:] = ltaps[...]


def front_kernel(
    me, q, k, v, g, rim, short, moment, spread,
    qf, kf, vf, prod, gconv, mom, taps, xq, xk, xv,
):
    rows = q.shape[0]
    taps[...] = spread_taps(short[0], spread[...])
    lanes = range(BLOCK // 128)
    for at, (src, dst) in enumerate(((q, xq), (k, xk), (v, xv))):
        for lane in lanes:
            cols = slice(128 * lane, 128 * lane + 128)
            dst[lane, 0:8] = rim[8 * at : 8 * at + 8, cols].astype(F32)
            dst[lane, 8:] = src[:, cols].astype(F32)

    def step(r, _):
        base = pl.multiple_of(r * 32, 32)
        here = pl.ds(base, 32)
        for lane in lanes:
            cols = slice(128 * lane, 128 * lane + 128)
            feats = []
            for at, src in enumerate((xq, xk, xv)):
                total = taps[7 * at : 7 * at + 1, cols] * src[lane, pl.ds(base + 8, 32), :]
                for j in range(1, 7):
                    tap = taps[7 * at + j : 7 * at + j + 1, cols]
                    total = total + tap * src[lane, pl.ds(base + 8 - j, 32), :]
                feats.append(total.astype(BF16))
            qf[here, cols] = feats[0]
            kf[here, cols] = feats[1]
            vf[here, cols] = feats[2]
            prod[here, cols] = (feats[1].astype(F32) * feats[2].astype(F32)).astype(BF16)
            gconv[here, cols] = (g[here, cols].astype(F32) * feats[0].astype(F32)).astype(BF16)
        return 0

    lax.fori_loop(0, rows // 32, step, 0)
    p, c = prod[...], gconv[...]
    mom[0:16] = dot(moment[0:16, :], jnp.concatenate([p, p], axis=0))
    mom[16:32] = dot(moment[16:32, :], jnp.concatenate([c, c], axis=0))


def state_kernel(me, *refs):
    moms, rates, out = refs[:CHUNKS], refs[CHUNKS], refs[CHUNKS + 1]
    owners = rates.shape[0]
    per = out.shape[0] // (2 * owners)
    for own in range(owners):
        chunk, part = divmod(own, owners // CHUNKS)
        mom = moms[chunk]
        slot = (me[0] - own + owners) % owners

        def tile(n, _):
            eight = pl.ds(pl.multiple_of(n * 8, 8), 8)
            cols = pl.ds(pl.multiple_of((part * per + n) * 128, 128), 128)
            terms = chebyshev(rates[slot, eight, :])
            mine = mom[:, cols]
            ahead = terms[0] * mine[0:1]
            back = terms[0] * mine[16:17]
            for at in range(1, TERMS):
                ahead = ahead + terms[at] * mine[at : at + 1]
                back = back + terms[at] * mine[16 + at : 17 + at]
            out[own * per + n] = ahead.astype(BF16)
            out[(owners + own) * per + n] = back.astype(BF16)
            return 0

        lax.fori_loop(0, per, tile, 0, unroll=4)


def scan_kernel(me, states, rates, out):
    count = states.shape[0]
    backward = me[1]
    factor = jnp.exp(rates[0] * -128.0)

    def hop(n, carry):
        at = jnp.where(backward == 1, count - 1 - n, n)
        out[at] = carry.astype(BF16)
        return factor * carry + states[at].astype(F32)

    lax.fori_loop(0, count, hop, jnp.zeros((8, 128), F32), unroll=8)


def modal_weight(rate, resid):
    x = 2.0 * rate
    return resid * jnp.sqrt(x * modal_series(x))


def modal_series(x):
    total = 1.0 - x * (1.0 / 8)
    for n in (7, 6, 5, 4, 3, 2):
        total = 1.0 - x * (1.0 / n) * total
    return total


def mid_kernel(
    me, prod, gconv, before, after, rates, resids, ltaps,
    t_own, t_before, t_after, t_taps, t_head, t_inv3, spread,
    yout, zout, tgrad, xx, own, prv, cur, nxt, tre, hre, cs, tsp, acc, coef,
):
    rows = prod.shape[0]
    quarter = pl.program_id(0) % (128 * CPG // BLOCK)

    @pl.when(quarter == 0)
    def _():
        spec = dot(t_taps[...], stack3(ltaps[0]))
        high, low = halves(spec)
        tsp[:, 0:128] = high
        tsp[:, 128:256] = low
        acc[...] = jnp.zeros_like(acc)

    one_hot = spread[...]
    xx[0:128] = one_hot
    xx[128:256] = one_hot
    tre[...] = dot(tsp[...], xx[...])
    for src, table, dst in (
        (prod, t_own, own), (before, t_before, prv), (gconv, t_own, cur), (after, t_after, nxt),
    ):
        value = src[...]
        xx[0:rows] = value
        xx[rows:] = value
        dst[...] = dot(table[...], xx[...])
    for lane in range(BLOCK // 128):
        cols = slice(128 * lane, 128 * lane + 128)
        eight = slice(8 * lane, 8 * lane + 8)
        weight = modal_weight(rates[0, eight, :], resids[0, eight, :])
        for n, term in enumerate(chebyshev(rates[0, eight, :])):
            coef[n : n + 1, cols] = jnp.sum(term * weight, axis=0, keepdims=True)
    hre[...] = dot(t_head[...], stack3(coef[...]))

    def bins(r, _):
        base = pl.multiple_of(r * 16, 16)
        re = pl.ds(base, 16)
        im = pl.ds(rows + base, 16)
        for lane in range(BLOCK // 128):
            cols = slice(128 * lane, 128 * lane + 128)
            tr, ti, hr, hi = tre[re, cols], tre[im, cols], hre[re, cols], hre[im, cols]
            pr, pi, cr, ci = own[re, cols], own[im, cols], cur[re, cols], cur[im, cols]
            wr, wi = pr + prv[re, cols], pi + prv[im, cols]
            ar, ai = cr + nxt[re, cols], ci + nxt[im, cols]
            yout[re, cols] = (wr * tr - wi * ti + (pr * hr - pi * hi)).astype(BF16)
            yout[im, cols] = (wr * ti + wi * tr + (pr * hi + pi * hr)).astype(BF16)
            zout[re, cols] = (ar * tr + ai * ti + (cr * hr + ci * hi)).astype(BF16)
            zout[im, cols] = (ai * tr - ar * ti + (ci * hr - cr * hi)).astype(BF16)
            cs[re, cols] = (cr * wr + ci * wi).astype(BF16)
            cs[im, cols] = (ci * wr - cr * wi).astype(BF16)
        return 0

    lax.fori_loop(0, rows // 16, bins, 0)
    acc[...] += lax.dot_general(
        cs[...], spread[...], (((1,), (1,)), ((), ())), preferred_element_type=F32
    )

    @pl.when(quarter == 128 * CPG // BLOCK - 1)
    def _():
        tgrad[...] = dot(t_inv3[...], stack3(acc[...]))


def back_kernel(
    me, qf, kf, vf, g, ys, zs, sf, sb, taps, rates, resids,
    t_inv, t_ahead, t_behind, *rest,
):
    (layer, gq, gk, gv, rim, last, eq, ek, ev, coef, lg, gp) = rest[-12:]
    rows = qf.shape[0]
    lanes = range(BLOCK // 128)
    for lane in lanes:
        cols = slice(128 * lane, 128 * lane + 128)
        eight = slice(8 * lane, 8 * lane + 8)
        weight = modal_weight(rates[0, eight, :], resids[0, eight, :])
        sets = (weight * sf[lane].astype(F32), weight * sb[lane].astype(F32))
        for n, term in enumerate(chebyshev(rates[0, eight, :])):
            for at, field in enumerate(sets):
                coef[16 * at + n : 16 * at + n + 1, cols] = jnp.sum(
                    term * field, axis=0, keepdims=True
                )
    lg[...] = dot(t_inv[...], ys[...]) + dot(t_ahead[...], stack3(coef[0:16]))
    gp[...] = dot(t_inv[...], zs[...]) + dot(t_behind[...], stack3(coef[16:32]))

    def rows_out(r, _):
        here = pl.ds(pl.multiple_of(r * 16, 16), 16)
        for lane in lanes:
            cols = slice(128 * lane, 128 * lane + 128)
            conv, grad = lg[here, cols], gp[here, cols]
            layer[here, cols] = (qf[here, cols].astype(F32) * conv).astype(BF16)
            eq[lane, here] = (g[here, cols].astype(F32) * conv).astype(BF16).astype(F32)
            ek[lane, here] = (grad * vf[here, cols].astype(F32)).astype(BF16).astype(F32)
            ev[lane, here] = (grad * kf[here, cols].astype(F32)).astype(BF16).astype(F32)
        return 0

    lax.fori_loop(0, rows // 16, rows_out, 0)
    for at, src in enumerate((eq, ek, ev)):
        for lane in lanes:
            cols = slice(128 * lane, 128 * lane + 128)
            src[lane, rows:] = jnp.zeros((8, 128), F32)
            rim[8 * at : 8 * at + 8, cols] = src[lane, 0:8].astype(BF16)

    def finish(r, _):
        base = pl.multiple_of(r * 32, 32)
        here = pl.ds(base, 32)
        for lane in lanes:
            cols = slice(128 * lane, 128 * lane + 128)
            for at, (src, dst) in enumerate(((eq, gq), (ek, gk), (ev, gv))):
                total = taps[7 * at : 7 * at + 1, cols] * src[lane, here, :]
                for j in range(1, 7):
                    tap = taps[7 * at + j : 7 * at + j + 1, cols]
                    total = total + tap * src[lane, pl.ds(base + j, 32), :]
                dst[here, cols] = total.astype(BF16)
                last[8 * at : 8 * at + 8, cols] = total[24:32]
        return 0

    lax.fori_loop(0, rows // 32, finish, 0)


def tail_kernel(me, *refs):
    lasts, rims, taps = refs[:CHUNKS], refs[CHUNKS : 2 * CHUNKS], refs[2 * CHUNKS : 3 * CHUNKS]
    gq, gk, gv, ext = refs[3 * CHUNKS + 3 :]
    pid = pl.program_id(0)
    ext[:, 0:8] = jnp.zeros((3, 8, 128), F32)
    for chunk in range(CHUNKS):
        last, rim, tap = lasts[chunk], rims[chunk], taps[chunk]

        @pl.when(pid == chunk)
        def _():
            def tile(n, _):
                cols = pl.ds(pl.multiple_of(n * 128, 128), 128)
                for at, dst in enumerate((gq, gk, gv)):
                    ext[at, 8:16] = rim[8 * at : 8 * at + 8, cols].astype(F32)
                    total = last[8 * at : 8 * at + 8, cols]
                    for j in range(1, 7):
                        total = total + tap[7 * at + j : 7 * at + j + 1, cols] * ext[at, j : 8 + j]
                    dst[:, cols] = total.astype(BF16)
                return 0

            lax.fori_loop(0, last.shape[1] // 128, tile, 0)


def fold_kernel(me, *refs):
    out = refs[-1]
    share = out.shape[1]
    owners = sum(part.shape[1] for part in refs[:-1]) // 128
    for at in range(refs[0].shape[0] // share):
        for own in range(owners):
            chunk, part = divmod(own, owners // CHUNKS)
            out[owners * at + own] = refs[chunk][
                share * at : share * at + share, 128 * part : 128 * part + 128
            ]


def shift(value, steps):
    count = lax.axis_size(AXES)
    first, last = max(0, -steps), min(count, count - steps)
    return lax.ppermute(value, AXES, [(at, at + steps) for at in range(first, last)])


def gather_own(value):
    return jnp.stack(ring_own(value))


def ring_own(value):
    count = lax.axis_size("own")
    parts = [value]
    for hop in range(1, count):
        parts.append(lax.ppermute(value, "own", [(at, (at + hop) % count) for at in range(count)]))
    return parts


def params_of(vmem):
    return pltpu.CompilerParams(
        dimension_semantics=("arbitrary",), vmem_limit_bytes=vmem
    )


def shards(query, key, value, short_taps, long_taps, decay_rate, residues, grad_out):
    rows, width = query.shape
    owners = lax.axis_size("own")
    per = width // CHUNKS
    steps = per // BLOCK
    quarters = width // owners // BLOCK
    ctx, own = lax.axis_index("ctx"), lax.axis_index("own")
    flat = ctx * owners + own
    half = width // 128
    me = jnp.stack([own, flat // half, flat % half]).astype(jnp.int32)
    table = tables(rows)
    group = BLOCK // 128
    whole = lambda shape: pl.BlockSpec(shape, lambda i, *m: (0,) * len(shape))
    edge = pl.BlockSpec((8, width), lambda i: (rows // 8 - 1, 0))

    rims, short, poles = pl.pallas_call(
        pack_kernel,
        out_shape=(
            jax.ShapeDtypeStruct((24, width), BF16),
            jax.ShapeDtypeStruct((24, 128), F32),
            jax.ShapeDtypeStruct((384, 128), F32),
        ),
        grid=(1,),
        in_specs=[edge] * 3
        + [whole(short_taps.shape), whole(decay_rate.shape), whole(residues.shape), whole(long_taps.shape)],
        out_specs=(
            whole((24, width)),
            whole((24, 128)),
            whole((384, 128)),
        ),
        compiler_params=params_of(60 << 20),
        name="pack",
    )(query, key, value, short_taps, decay_rate, residues, long_taps)
    short_all = gather_own(short)
    rims = shift(rims, 1)
    poles_parts = ring_own(poles)

    def slot(me_ref, chunk):
        return (me_ref[0] - chunk + owners) % owners

    tab = lambda name: (jnp.asarray(table[name]), whole(table[name].shape))
    full = jax.ShapeDtypeStruct((rows, width), BF16)
    part = jax.ShapeDtypeStruct((rows, per), BF16)
    spectrum = jax.ShapeDtypeStruct((2 * rows, per), BF16)
    here = pl.BlockSpec((rows, BLOCK), lambda i, m: (0, i))
    bins = pl.BlockSpec((2 * rows, BLOCK), lambda i, m: (0, i))

    def wide(chunk):
        return pl.BlockSpec((rows, BLOCK), lambda i, m: (0, chunk * steps + i))

    def owned(chunk, i, me_ref):
        return slot(me_ref, chunk * (owners // CHUNKS) + i // quarters)

    def shorts(chunk):
        return pl.BlockSpec((1, 24, 128), lambda i, m: (owned(chunk, i, m), 0, 0))

    def poles_at(chunk, first):
        return pl.BlockSpec(
            (1, 8 * group, 128), lambda i, m: (owned(chunk, i, m), first + i % quarters, 0)
        )

    def call(
        kernel, cost, grid, in_specs, operands, out_shape, out_specs, scratch,
        aliases={}, after=(),
    ):
        known = 1 + len(operands)

        def body(*refs):
            kernel(*refs[:known], *refs[known + len(after) :])

        in_specs = list(in_specs) + [pl.BlockSpec(memory_space=pl.ANY)] * len(after)
        operands = list(operands) + list(after)
        return pl.pallas_call(
            body,
            out_shape=out_shape,
            grid_spec=pltpu.PrefetchScalarGridSpec(
                num_scalar_prefetch=1,
                grid=grid,
                in_specs=in_specs,
                out_specs=out_specs,
                scratch_shapes=scratch,
            ),
            input_output_aliases=aliases,
            compiler_params=params_of(60 << 20),
            cost_estimate=pl.CostEstimate(flops=cost, transcendentals=0, bytes_accessed=cost // 200),
        )(me, *operands)

    spread = jnp.asarray(table["spread"])
    spread_spec = pl.BlockSpec((128, BLOCK), lambda i, m: (0, i % quarters))

    def front(chunk, after):
        moment, moment_spec = tab("moment")
        return call(
            front_kernel, 2_000_000_000, (steps,),
            [wide(chunk)] * 4
            + [pl.BlockSpec((24, BLOCK), lambda i, m: (0, chunk * steps + i)), shorts(chunk), moment_spec, spread_spec],
            (query, key, value, grad_out, rims, short_all, moment, spread),
            (part,) * 5
            + (jax.ShapeDtypeStruct((32, per), F32), jax.ShapeDtypeStruct((24, per), F32)),
            (here,) * 5
            + (
                pl.BlockSpec((32, BLOCK), lambda i, m: (0, i)),
                pl.BlockSpec((24, BLOCK), lambda i, m: (0, i)),
            ),
            [pltpu.VMEM((group, rows + 8, 128), F32)] * 3,
            after=after,
        )

    fronts, behinds, aheads = [], [], []
    for chunk in range(CHUNKS):
        made = front(chunk, [fronts[-1][5]] if fronts else [])
        fronts.append(made)

    def exchange(chunk, after):
        prod, gconv, after = lax.optimization_barrier((fronts[chunk][3], fronts[chunk][4], after))
        behinds.append(shift(prod, 1))
        aheads.append(shift(gconv, -1))
        return after

    poles_all = jnp.stack(exchange(0, tuple(poles_parts)))
    states = call(
        state_kernel, 200_000_000, (1,),
        [whole((32, per))] * CHUNKS + [pl.BlockSpec((owners, 128, 128), lambda i, m: (0, 0, 0))],
        [f[5] for f in fronts] + [poles_all],
        jax.ShapeDtypeStruct((2 * half, 8, 128), BF16),
        whole((2 * half, 8, 128)),
        [],
    )
    arrived = lax.all_to_all(states, AXES, 0, 0, tiled=True)
    for chunk in range(1, CHUNKS):
        exchange(chunk, arrived)

    def mid(chunk, after):
        consts = [tab(name) for name in ("own", "before", "after", "taps", "head", "inverse3")]
        spec32 = pltpu.VMEM((2 * rows, BLOCK), F32)
        spec16 = pltpu.VMEM((2 * rows, BLOCK), BF16)
        return call(
            mid_kernel, 2_000_000_000, (steps,),
            [here] * 4
            + [
                poles_at(chunk, 0),
                poles_at(chunk, quarters),
                pl.BlockSpec((1, 128, 128), lambda i, m: (owned(chunk, i, m), 2, 0)),
            ]
            + [spec for _, spec in consts]
            + [spread_spec],
            [fronts[chunk][3], fronts[chunk][4], behinds[chunk], aheads[chunk]]
            + [poles_all] * 3
            + [c for c, _ in consts]
            + [spread],
            (spectrum,) * 2 + (jax.ShapeDtypeStruct((128, per // CPG), F32),),
            (bins,) * 2 + (pl.BlockSpec((128, 128), lambda i, m: (0, i // quarters)),),
            [spec16]
            + [spec32] * 6
            + [
                spec16,
                pltpu.VMEM((2 * rows, 256), BF16),
                pltpu.VMEM((2 * rows, 128), F32),
                pltpu.VMEM((16, BLOCK), F32),
            ],
            after=after,
        )

    def back(chunk, ys, zs, outs, after):
        consts = [tab(name) for name in ("inverse", "ahead", "behind")]
        made = fronts[chunk]
        operands = [
            made[0], made[1], made[2], grad_out, ys, zs, carried, carried,
            made[6], poles_all, poles_all,
        ] + [c for c, _ in consts]
        in_specs = [
            here, here, here, wide(chunk), bins, bins,
            pl.BlockSpec((group, 8, 128), lambda i, m: (chunk * steps + i, 0, 0)),
            pl.BlockSpec((group, 8, 128), lambda i, m: ((CHUNKS + chunk) * steps + i, 0, 0)),
            pl.BlockSpec((24, BLOCK), lambda i, m: (0, i)),
            poles_at(chunk, 0),
            poles_at(chunk, quarters),
        ] + [spec for _, spec in consts]
        aliases = {}
        for at, out in enumerate(outs):
            aliases[1 + len(operands)] = at
            operands.append(out)
            in_specs.append(pl.BlockSpec(memory_space=pl.ANY))
        ext = pltpu.VMEM((group, rows + 8, 128), F32)
        plain = pltpu.VMEM((rows, BLOCK), F32)
        return call(
            back_kernel, 2_000_000_000, (steps,), in_specs, operands,
            (full,) * 4
            + (jax.ShapeDtypeStruct((24, per), BF16), jax.ShapeDtypeStruct((24, per), F32)),
            (wide(chunk),) * 4
            + (
                pl.BlockSpec((24, BLOCK), lambda i, m: (0, i)),
                pl.BlockSpec((24, BLOCK), lambda i, m: (0, i)),
            ),
            [ext, ext, ext, pltpu.VMEM((32, BLOCK), F32), plain, plain],
            aliases,
            after,
        )

    scanned = call(
        scan_kernel, 200_000_000, (1,),
        [
            whole(arrived.shape),
            pl.BlockSpec(
                (1, 8, 128),
                lambda i, m: (
                    (m[0] - m[2] // (half // owners) + owners) % owners, m[2] % (half // owners), 0
                ),
            ),
        ],
        (arrived, poles_all),
        jax.ShapeDtypeStruct(arrived.shape, BF16),
        whole(arrived.shape),
        [],
    )
    carried = lax.all_to_all(scanned, AXES, 0, 0, tiled=True)

    outs, edges, lasts = (), [], []

    def finish(chunk, after):
        made = back(chunk, mids[chunk][0], mids[chunk][1], outs, after)
        edges.append(shift(made[4], -1))
        lasts.append(made[5])
        return made[:4]

    mids = []
    for chunk in range(CHUNKS):
        mids.append(mid(chunk, [lasts[-1]] if lasts else [scanned]))
        if chunk < CHUNKS - 1:
            outs = finish(chunk, [])
    ctxs = lax.axis_size("ctx")
    share = rows // ctxs
    pieces = call(
        fold_kernel, 100_000_000, (1,),
        [whole((rows, per // CPG))] * CHUNKS,
        [m[2] for m in mids],
        jax.ShapeDtypeStruct((ctxs * owners, share, 128), F32),
        whole((ctxs * owners, share, 128)),
        [],
    )
    landed = lax.all_to_all(pieces, AXES, 0, 0, tiled=True)
    outs = finish(CHUNKS - 1, [landed])
    tokens = rows * ctxs * owners
    total = landed.sum(axis=0) * (1.0 / math.sqrt(tokens * CPG))
    every = lax.all_to_all(
        jnp.broadcast_to(total[None], (ctxs, share, 128)), "ctx", 0, 0, tiled=True
    )

    strip = pl.BlockSpec((8, per), lambda i, m: (rows // 8 - 1, i))
    anyspec = pl.BlockSpec(memory_space=pl.ANY)
    grads = call(
        tail_kernel, 200_000_000, (CHUNKS,),
        [whole((24, per))] * (3 * CHUNKS) + [anyspec] * 3,
        (*lasts, *edges, *[f[6] for f in fronts], *outs[1:4]),
        (full,) * 3,
        (strip,) * 3,
        [pltpu.VMEM((3, 16, 128), F32)],
        {3 * CHUNKS + 1: 0, 3 * CHUNKS + 2: 1, 3 * CHUNKS + 3: 2},
    )
    return (outs[0],) + tuple(grads) + (every.reshape(rows, 128),)


def solution(mesh):
    placed = (
        P(AXES, None),
        P(AXES, None),
        P(AXES, None),
        P(None, None, "own"),
        P(None, "own"),
        P(None, "own"),
        P(None, "own"),
        P(AXES, None),
    )
    return jax.shard_map(
        shards,
        mesh=mesh,
        in_specs=placed,
        out_specs=(P(AXES, None),) * 4 + (P(None, "own"),),
        check_vma=False,
    )
```

time: 241 us -> 196 us (0.81)
  the two profiles are of different devices: /device:TPU:18 before, /device:TPU:1 now
where the time goes in v2:
time: 196 us; the launch traced here: 194 us
  Pallas kernels  91.6 us (47%)
  starting transfers between devices  47.9 us (24%)
  blocking collectives  32.2 us (16%)
  waiting for transfers between devices  13.3 us (7%)
  local copies, waits for them, and re-layouts  4.56 us (2%)
  other arithmetic  4.04 us (2%)
    pallas_call x10, Pallas kernels, call(): pl.pallas_call(body, out_shape=out_shape, grid_spec=pltpu.PrefetchScalarG...  89.6 us
    ppermute x7, starting transfers between devices, shift(): lax.ppermute(value, AXES, [(at, at + steps) for at in range(first, last)])  26.9 us
    all_to_all x1, blocking collectives, shards(): arrived = lax.all_to_all(states, AXES, 0, 0, tiled=True)  20.9 us
    all_to_all x1, blocking collectives, shards(): lax.all_to_all(jnp.broadcast_to(total[None], (ctxs, share, 128)), 'ctx',...  11.3 us
    ppermute x6, starting transfers between devices, ring_own(): lax.ppermute(value, 'own', [(at, (at + hop) % count) for at in range(coun...  7.8 us
    all_to_all x1, starting transfers between devices, shards(): landed = lax.all_to_all(pieces, AXES, 0, 0, tiled=True)  7.66 us
    all_to_all x1, waiting for transfers between devices, shards(): landed = lax.all_to_all(pieces, AXES, 0, 0, tiled=True)  6.48 us
    all_to_all x1, starting transfers between devices, shards(): carried = lax.all_to_all(scanned, AXES, 0, 0, tiled=True)  5.55 us
  transfers between devices with their start and end apart: 15, of which 4 were waited for; matrix products, arithmetic and copies ran while one was open for 2% of the time, Pallas kernels for 35%

profile of v2, /device:TPU:1, one launch (start us, length us, event | category | flops | bytes accessed | tf_op | source)
XLA Modules:
  0.0 194.3 jit_solution(7170287362250682946)
XLA Ops:
  0.6 2.0 %pack.1 = (bf16[24,8192]{1,0:T(8,128)(2,1)}, f32[24,128]{1,0:T(8,128)}, f32[384,128]{1,0:T(8,128)}) custom-call(bf16[128,8192]{1,0:T(8,128)(2,1)} %refs_1_.3, bf16[128,8192]{1,0:T(8,128)(2,1)} %refs_2_.3, bf16[128,8192]{1,0:T(8,128)(2,1)} %refs_3_.3, f32[3,7,128]{2,1,0:T(8,128)} %short.1, f32[8,2048]{1,0:T(8,128)} %rate.1, f32[8,2048]{1,0:T(8,128)} %resid.1, ...), custom_call_target="tpu_custom_call" | custom-call | tf_op jit(solution)/shard_map/pack/pallas_call | solution.py:398
  2.6 4.0 %collective-permute-start = (bf16[24,8192]{1,0:T(8,128)(2,1)}, bf16[24,8192]{1,0:T(8,128)(2,1)S(1)}, u32[]{:S(2)}, u32[]{:S(2)}) collective-permute-start(bf16[24,8192]{1,0:T(8,128)(2,1)} %get-tuple-element.51), channel_id=1, source_target_pairs={{0,1},{1,2},{2,3},{3,4},{4,5},{5,6},{6,7},{7,8},{8,9},{9,10},{10,1... | collective-permute-start | bytes 1179656 | tf_op jit(solution)/shard_map/ppermute | solution.py:362
  6.6 3.4 %collective-permute-start.3 = (f32[24,128]{1,0:T(8,128)}, f32[24,128]{1,0:T(8,128)S(1)}, u32[]{:S(2)}, u32[]{:S(2)}) collective-permute-start(f32[24,128]{1,0:T(8,128)} %get-tuple-element.52), channel_id=1, source_target_pairs={{0,3},{1,0},{2,1},{3,2},{4,7},{5,4},{6,5},{7,6},{8,11},{9,8},{10,9... | collective-permute-start | bytes 36872 | tf_op jit(solution)/shard_map/ppermute | solution.py:373
  10.0 0.0 collective-permute-start.2
  10.0 0.7 collective-permute-start.1
  10.6 2.0 %collective-permute-start.6 = (f32[384,128]{1,0:T(8,128)}, f32[384,128]{1,0:T(8,128)S(1)}, u32[]{:S(2)}, u32[]{:S(2)}) collective-permute-start(f32[384,128]{1,0:T(8,128)} %get-tuple-element.63), channel_id=1, source_target_pairs={{0,3},{1,0},{2,1},{3,2},{4,7},{5,4},{6,5},{7,6},{8,11},{9,8},{10,9... | collective-permute-start | bytes 589832 | tf_op jit(solution)/shard_map/ppermute | solution.py:373
  12.6 0.6 pad_add_fusion.refs_0_
  13.3 0.0 collective-permute-done.3
  13.3 1.8 collective-permute-start.5
  15.0 2.9 %collective-permute-done.2 = f32[24,128]{1,0:T(8,128)S(1)} collective-permute-done((f32[24,128]{1,0:T(8,128)}, f32[24,128]{1,0:T(8,128)S(1)}, u32[]{:S(2)}, u32[]{:S(2)}) %collective-permute-start.2) | collective-permute-done | bytes 12320 | tf_op jit(solution)/shard_map/ppermute | solution.py:373
  17.9 0.0 collective-permute-start.4
  17.9 1.6 collective-permute-done.1
  19.5 1.3 pad_maximum_fusion.1.refs_6_
  20.9 0.0 collective-permute-done.refs_5_
  20.9 0.0 copy-start.2
  20.9 0.7 copy-done.2
  21.6 10.7 %shard_map.218 = (bf16[128,4096]{1,0:T(8,128)(2,1)}, bf16[128,4096]{1,0:T(8,128)(2,1)}, bf16[128,4096]{1,0:T(8,128)(2,1)}, bf16[128,4096]{1,0:T(8,128)(2,1)}, bf...) custom-call(s32[3]{0:T(128)} %pad_add_fusion.refs_0_, bf16[128,8192]{1,0:T(8,128)(2,1)} %refs_1_.3, ...), custom_call_target="tpu_custom_call" | custom-call | flops 2000000000 | bytes 10000000 | tf_op jit(solution)/shard_map/pallas_call | solution.py:455
  32.3 0.0 collective-permute-done.6
  32.3 0.0 collective-permute-done.5
  32.3 0.0 collective-permute-done.4
  32.3 1.9 collective-permute-start.9
  34.3 6.1 %collective-permute-start.10 = (bf16[128,4096]{1,0:T(8,128)(2,1)}, bf16[128,4096]{1,0:T(8,128)(2,1)}, u32[]{:S(2)}, u32[]{:S(2)}) collective-permute-start(bf16[128,4096]{1,0:T(8,128)(2,1)} %get-tuple-element.73.refs_2_), channel_id=1, source_target_pairs={{1,0},{2,1},{3,2},{4,3},{5,4},{6,5},{7,6},{8,7},{9,8},{10,9},{11,1... | collective-permute-start | bytes 3145736 | tf_op jit(solution)/shard_map/ppermute | solution.py:362
  40.3 0.0 copy-start.6
  40.4 10.9 %shard_map.219 = (bf16[128,4096]{1,0:T(8,128)(2,1)}, bf16[128,4096]{1,0:T(8,128)(2,1)}, bf16[128,4096]{1,0:T(8,128)(2,1)}, bf16[128,4096]{1,0:T(8,128)(2,1)}, bf...) custom-call(s32[3]{0:T(128)} %pad_add_fusion.refs_0_, bf16[128,8192]{1,0:T(8,128)(2,1)} %refs_1_.3, ...), custom_call_target="tpu_custom_call" | custom-call | flops 2000000000 | bytes 10000000 | tf_op jit(solution)/shard_map/pallas_call | solution.py:455
  51.2 0.0 copy-done.6
  51.2 0.0 copy-start.3
  51.2 0.0 copy-start.4
  51.3 1.0 pad_maximum_fusion.refs_3_.refs_2_.refs_5_.refs_6_.refs_7_.refs_10_.refs_11_
  52.2 3.8 %shard_map.220 = bf16[128,8,128]{2,1,0:T(8,128)(2,1)} custom-call(s32[3]{0:T(128)} %pad_add_fusion.refs_0_, f32[32,4096]{1,0:T(8,128)} %get-tuple-element.53.refs_9_.refs_1_, f32[32,4096]{1,0:T(8,128)} %get-tuple-element.59.refs_2_, f32[4,384,128]{2,1,0:T(8,128)} %pad_maximum_fusion.refs_3_.refs_2_.refs_5_.refs_6_.refs_7_.refs_10_.refs_11_), custom_call_target="tpu_custom_call" | custom-call | flops 200000000 | bytes 1000000 | tf_op jit(solution)/shard_map/pallas_call | solution.py:455
  56.0 20.9 %all_to_all.20.refs_1_ = bf16[128,8,128]{2,1,0:T(8,128)(2,1)} all-to-all(bf16[128,8,128]{2,1,0:T(8,128)(2,1)} %shard_map.220), channel_id=1, replica_groups=mesh['ctx'=32,'own'=4] {'ctx','own'}, dimensions={0} | all-to-all | bytes 524288 | tf_op jit(solution)/shard_map/all_to_all | solution.py:511
  76.8 0.0 copy-done.3
  76.8 2.2 %collective-permute-start.7 = (bf16[128,4096]{1,0:T(8,128)(2,1)S(1)}, bf16[128,4096]{1,0:T(8,128)(2,1)S(1)}, u32[]{:S(2)}, u32[]{:S(2)}) collective-permute-start(bf16[128,4096]{1,0:T(8,128)(2,1)S(1)} %copy-done.3), channel_id=1, source_target_pairs={{0,1},{1,2},{2,3},{3,4},{4,5},{5,6},{6,7},{7,8},{8,9},{9,10},{10,1... | collective-permute-start | bytes 3145736 | tf_op jit(solution)/shard_map/ppermute | solution.py:362
  79.1 0.0 copy-done.4
  79.1 4.5 %collective-permute-start.8 = (bf16[128,4096]{1,0:T(8,128)(2,1)S(1)}, bf16[128,4096]{1,0:T(8,128)(2,1)}, u32[]{:S(2)}, u32[]{:S(2)}) collective-permute-start(bf16[128,4096]{1,0:T(8,128)(2,1)S(1)} %copy-done.4), channel_id=1, source_target_pairs={{1,0},{2,1},{3,2},{4,3},{5,4},{6,5},{7,6},{8,7},{9,8},{10,9},{11,1... | collective-permute-start | bytes 3145736 | tf_op jit(solution)/shard_map/ppermute | solution.py:362
  83.6 2.6 %shard_map.221.refs_15_ = bf16[128,8,128]{2,1,0:T(8,128)(2,1)} custom-call(s32[3]{0:T(128)} %pad_add_fusion.refs_0_, bf16[128,8,128]{2,1,0:T(8,128)(2,1)} %all_to_all.20.refs_1_, f32[4,384,128]{2,1,0:T(8,128)} %pad_maximum_fusion.refs_3_.refs_2_.refs_5_.refs_6_.refs_7_.refs_10_.refs_11_), custom_call_target="tpu_custom_call" | custom-call | flops 200000000 | bytes 1000000 | tf_op jit(solution)/shard_map/pallas_call | solution.py:455
  86.3 5.6 %all-to-all-start.1 = ((bf16[128,8,128]{2,1,0:T(8,128)(2,1)}), bf16[128,8,128]{2,1,0:T(8,128)(2,1)S(1)}, u32[]{:S(2)}, u32[]{:S(2)}) async-start(bf16[128,8,128]{2,1,0:T(8,128)(2,1)} %shard_map.221.refs_15_), calls=%async_computation.1 | async-start | bytes 524288 | tf_op jit(solution)/shard_map/all_to_all | solution.py:598
  91.8 0.0 collective-permute-done.9.refs_3_
  91.8 0.0 collective-permute-done.10.refs_4_
  91.8 15.3 %shard_map.222 = (bf16[256,4096]{1,0:T(8,128)(2,1)}, bf16[256,4096]{1,0:T(8,128)(2,1)}, f32[128,256]{1,0:T(8,128)}) custom-call(s32[3]{0:T(128)} %pad_add_fusion.refs_0_, bf16[128,4096]{1,0:T(8,128)(2,1)} %get-tuple-element.72.refs_1_, bf16[128,4096]{1,0:T(8,128)(2,1)} %get-tuple-element.73.refs_2_, bf16[128,4096]{1,0:T(8,128)(2,1)} %collective-permute-done.9.refs_3_, ...), custom_call_target="tpu_custom_call" | custom-call | flops 2000000000 | bytes 10000000 | tf_op jit(solution)/shard_map/pallas_call | solution.py:455
  107.1 2.3 %all-to-all-done.1.refs_7_.refs_8_ = bf16[128,8,128]{2,1,0:T(8,128)(2,1)S(1)} async-done(((bf16[128,8,128]{2,1,0:T(8,128)(2,1)}), bf16[128,8,128]{2,1,0:T(8,128)(2,1)S(1)}, u32[]{:S(2)}, u32[]{:S(2)}) %all-to-all-start.1) | async-done | bytes 262176 | tf_op jit(solution)/shard_map/all_to_all | solution.py:598
  109.4 0.7 copy-done
  110.1 12.2 %shard_map.223 = (bf16[128,8192]{1,0:T(8,128)(2,1)}, bf16[128,8192]{1,0:T(8,128)(2,1)}, bf16[128,8192]{1,0:T(8,128)(2,1)}, bf16[128,8192]{1,0:T(8,128)(2,1)}, bf...) custom-call(s32[3]{0:T(128)} %pad_add_fusion.refs_0_, bf16[128,4096]{1,0:T(8,128)(2,1)} %get-tuple-element.69.refs_1_, ...), custom_call_target="tpu_custom_call" | custom-call | flops 2000000000 | bytes 10000000 | tf_op jit(solution)/shard_map/pallas_call | solution.py:455
  122.3 0.0 collective-permute-done.7.refs_3_
  122.3 0.0 copy-start.5
  122.4 0.0 collective-permute-done.8.refs_4_
  122.4 1.0 copy-done.5
  123.3 15.4 %shard_map.224 = (bf16[256,4096]{1,0:T(8,128)(2,1)}, bf16[256,4096]{1,0:T(8,128)(2,1)}, f32[128,256]{1,0:T(8,128)}) custom-call(s32[3]{0:T(128)} %pad_add_fusion.refs_0_, bf16[128,4096]{1,0:T(8,128)(2,1)} %get-tuple-element.67.refs_1_, bf16[128,4096]{1,0:T(8,128)(2,1)} %get-tuple-element.68.refs_2_, bf16[128,4096]{1,0:T(8,128)(2,1)} %copy-done.5, ...), custom_call_target="tpu_custom_call" | custom-call | flops 2000000000 | bytes 10000000 | tf_op jit(solution)/shard_map/pallas_call | solution.py:455
  138.8 2.4 %shard_map.225 = f32[128,4,128]{2,1,0:T(4,128)} custom-call(s32[3]{0:T(128)} %pad_add_fusion.refs_0_, f32[128,256]{1,0:T(8,128)} %get-tuple-element.85.refs_1_, f32[128,256]{1,0:T(8,128)} %get-tuple-element.86.refs_2_), custom_call_target="tpu_custom_call" | custom-call | flops 100000000 | bytes 500000 | tf_op jit(solution)/shard_map/pallas_call | solution.py:455
  141.1 7.7 %all-to-all-start.2 = ((f32[128,4,128]{2,1,0:T(4,128)}), f32[128,4,128]{2,1,0:T(4,128)S(1)}, u32[]{:S(2)}, u32[]{:S(2)}) async-start(f32[128,4,128]{2,1,0:T(4,128)} %shard_map.225), calls=%async_computation.2 | async-start | bytes 524288 | tf_op jit(solution)/shard_map/all_to_all | solution.py:623
  148.8 0.0 copy-done.9
  148.8 4.8 %collective-permute-start.11 = (bf16[24,4096]{1,0:T(8,128)(2,1)S(1)}, bf16[24,4096]{1,0:T(8,128)(2,1)S(1)}, u32[]{:S(2)}, u32[]{:S(2)}) collective-permute-start(bf16[24,4096]{1,0:T(8,128)(2,1)S(1)} %copy-done.9), channel_id=1, source_target_pairs={{1,0},{2,1},{3,2},{4,3},{5,4},{6,5},{7,6},{8,7},{9,8},{10,9},{11,1... | collective-permute-start | bytes 589832 | tf_op jit(solution)/shard_map/ppermute | solution.py:362
  153.6 6.5 %all-to-all-done.2.refs_19_ = f32[128,4,128]{2,1,0:T(4,128)S(1)} async-done(((f32[128,4,128]{2,1,0:T(4,128)}), f32[128,4,128]{2,1,0:T(4,128)S(1)}, u32[]{:S(2)}, u32[]{:S(2)}) %all-to-all-start.2) | async-done | bytes 262176 | tf_op jit(solution)/shard_map/all_to_all | solution.py:623
  160.1 0.7 copy-done.1
  160.8 12.2 %shard_map.226 = (bf16[128,8192]{1,0:T(8,128)(2,1)}, bf16[128,8192]{1,0:T(8,128)(2,1)}, bf16[128,8192]{1,0:T(8,128)(2,1)}, bf16[128,8192]{1,0:T(8,128)(2,1)}, bf...) custom-call(s32[3]{0:T(128)} %pad_add_fusion.refs_0_, ...), custom_call_target="tpu_custom_call", output_to_operand_aliasing={{0}: (15, {}), {1}: (16, {}), {2}: (17, {}), {3}: (18, {})} | custom-call | flops 2000000000 | bytes 10000000 | tf_op jit(solution)/shard_map/pallas_call | solution.py:455
  173.0 3.3 %collective-permute-start.12 = (bf16[24,4096]{1,0:T(8,128)(2,1)}, bf16[24,4096]{1,0:T(8,128)(2,1)S(1)}, u32[]{:S(2)}, u32[]{:S(2)}) collective-permute-start(bf16[24,4096]{1,0:T(8,128)(2,1)} %get-tuple-element.90), channel_id=1, source_target_pairs={{1,0},{2,1},{3,2},{4,3},{5,4},{6,5},{7,6},{8,7},{9,8},{10,9},{11,1... | collective-permute-start | bytes 589832 | tf_op jit(solution)/shard_map/ppermute | solution.py:362
  176.3 1.1 reduce_sum.9
  177.4 11.3 %all_to_all.21 = f32[32,4,128]{2,1,0:T(4,128)S(1)} all-to-all(f32[32,4,128]{2,1,0:T(4,128)S(1)} %broadcast_in_dim.2), channel_id=1, replica_groups=mesh['ctx'=32,'own'=4] {'ctx'}, dimensions={0} | all-to-all | bytes 131072 | tf_op jit(solution)/shard_map/all_to_all | solution.py:627
  188.7 0.0 collective-permute-done.11.refs_3_
  188.7 0.0 collective-permute-done.12.refs_4_
  188.8 0.0 copy-start.8
  188.8 0.7 copy-done.7
  189.4 0.0 copy-done.8
  189.5 4.2 %shard_map.227 = (bf16[128,8192]{1,0:T(8,128)(2,1)}, bf16[128,8192]{1,0:T(8,128)(2,1)}, bf16[128,8192]{1,0:T(8,128)(2,1)}) custom-call(s32[3]{0:T(128)} %pad_add_fusion.refs_0_, f32[24,4096]{1,0:T(8,128)} %get-tuple-element.77.refs_15_.refs_1_, f32[24,4096]{1,0:T(8,128)} %get-tuple-element.88.refs_2_, ...), custom_call_target="tpu_custom_call", output_to_operand_aliasing={{0}: (7, {}), {1}: (8, {}), {2}: (9, {})} | custom-call | flops 200000000 | bytes 1000000 | tf_op jit(solution)/shard_map/pallas_call | solution.py:455
  193.7 0.6 copy.39
  (6 shorter events, 0.0 us)
Async XLA Ops:
  2.6 18.3 %collective-permute-start = (bf16[24,8192]{1,0:T(8,128)(2,1)}, bf16[24,8192]{1,0:T(8,128)(2,1)S(1)}, u32[]{:S(2)}, u32[]{:S(2)}) collective-permute-start(bf16[24,8192]{1,0:T(8,128)(2,1)} %get-tuple-element.51), channel_id=1, source_target_pairs={{0,1},{1,2},{2,3},{3,4},{4,5},{5,6},{6,7},{7,8},{8,9},{9,10},{10,1... | collective-permute-start | bytes 1179656 | tf_op jit(solution)/shard_map/ppermute | solution.py:362
  6.6 6.7 %collective-permute-start.3 = (f32[24,128]{1,0:T(8,128)}, f32[24,128]{1,0:T(8,128)S(1)}, u32[]{:S(2)}, u32[]{:S(2)}) collective-permute-start(f32[24,128]{1,0:T(8,128)} %get-tuple-element.52), channel_id=1, source_target_pairs={{0,3},{1,0},{2,1},{3,2},{4,7},{5,4},{6,5},{7,6},{8,11},{9,8},{10,9... | collective-permute-start | bytes 36872 | tf_op jit(solution)/shard_map/ppermute | solution.py:373
  10.0 7.9 %collective-permute-start.2 = (f32[24,128]{1,0:T(8,128)}, f32[24,128]{1,0:T(8,128)S(1)}, u32[]{:S(2)}, u32[]{:S(2)}) collective-permute-start(f32[24,128]{1,0:T(8,128)} %get-tuple-element.52), channel_id=1, source_target_pairs={{0,2},{1,3},{2,0},{3,1},{4,6},{5,7},{6,4},{7,5},{8,10},{9,11},{10,... | collective-permute-start | bytes 36872 | tf_op jit(solution)/shard_map/ppermute | solution.py:373
  10.0 9.6 %collective-permute-start.1 = (f32[24,128]{1,0:T(8,128)}, f32[24,128]{1,0:T(8,128)S(1)}, u32[]{:S(2)}, u32[]{:S(2)}) collective-permute-start(f32[24,128]{1,0:T(8,128)} %get-tuple-element.52), channel_id=1, source_target_pairs={{0,1},{1,2},{2,3},{3,0},{4,5},{5,6},{6,7},{7,4},{8,9},{9,10},{10,1... | collective-permute-start | bytes 36872 | tf_op jit(solution)/shard_map/ppermute | solution.py:373
  10.6 21.7 %collective-permute-start.6 = (f32[384,128]{1,0:T(8,128)}, f32[384,128]{1,0:T(8,128)S(1)}, u32[]{:S(2)}, u32[]{:S(2)}) collective-permute-start(f32[384,128]{1,0:T(8,128)} %get-tuple-element.63), channel_id=1, source_target_pairs={{0,3},{1,0},{2,1},{3,2},{4,7},{5,4},{6,5},{7,6},{8,11},{9,8},{10,9... | collective-permute-start | bytes 589832 | tf_op jit(solution)/shard_map/ppermute | solution.py:373
  13.3 19.0 %collective-permute-start.5 = (f32[384,128]{1,0:T(8,128)}, f32[384,128]{1,0:T(8,128)S(1)}, u32[]{:S(2)}, u32[]{:S(2)}) collective-permute-start(f32[384,128]{1,0:T(8,128)} %get-tuple-element.63), channel_id=1, source_target_pairs={{0,2},{1,3},{2,0},{3,1},{4,6},{5,7},{6,4},{7,5},{8,10},{9,11},{10,... | collective-permute-start | bytes 589832 | tf_op jit(solution)/shard_map/ppermute | solution.py:373
  17.9 14.4 %collective-permute-start.4 = (f32[384,128]{1,0:T(8,128)}, f32[384,128]{1,0:T(8,128)S(1)}, u32[]{:S(2)}, u32[]{:S(2)}) collective-permute-start(f32[384,128]{1,0:T(8,128)} %get-tuple-element.63), channel_id=1, source_target_pairs={{0,1},{1,2},{2,3},{3,0},{4,5},{5,6},{6,7},{7,4},{8,9},{9,10},{10,1... | collective-permute-start | bytes 589832 | tf_op jit(solution)/shard_map/ppermute | solution.py:373
  20.9 0.7 copy-start.2
  32.3 59.5 %collective-permute-start.9 = (bf16[128,4096]{1,0:T(8,128)(2,1)}, bf16[128,4096]{1,0:T(8,128)(2,1)}, u32[]{:S(2)}, u32[]{:S(2)}) collective-permute-start(bf16[128,4096]{1,0:T(8,128)(2,1)} %get-tuple-element.72.refs_1_), channel_id=1, source_target_pairs={{0,1},{1,2},{2,3},{3,4},{4,5},{5,6},{6,7},{7,8},{8,9},{9,10},{10,1... | collective-permute-start | bytes 3145736 | tf_op jit(solution)/shard_map/ppermute | solution.py:362
  34.3 57.6 %collective-permute-start.10 = (bf16[128,4096]{1,0:T(8,128)(2,1)}, bf16[128,4096]{1,0:T(8,128)(2,1)}, u32[]{:S(2)}, u32[]{:S(2)}) collective-permute-start(bf16[128,4096]{1,0:T(8,128)(2,1)} %get-tuple-element.73.refs_2_), channel_id=1, source_target_pairs={{1,0},{2,1},{3,2},{4,3},{5,4},{6,5},{7,6},{8,7},{9,8},{10,9},{11,1... | collective-permute-start | bytes 3145736 | tf_op jit(solution)/shard_map/ppermute | solution.py:362
  40.3 10.9 %copy-start.6 = (f32[384,128]{1,0:T(8,128)S(1)}, f32[384,128]{1,0:T(8,128)}, u32[]{:S(2)}) copy-start(f32[384,128]{1,0:T(8,128)} %get-tuple-element.63) | copy-start | bytes 589828
  51.2 25.6 %copy-start.3 = (bf16[128,4096]{1,0:T(8,128)(2,1)S(1)}, bf16[128,4096]{1,0:T(8,128)(2,1)}, u32[]{:S(2)}) copy-start(bf16[128,4096]{1,0:T(8,128)(2,1)} %get-tuple-element.67.refs_1_) | copy-start | bytes 3145732
  51.2 27.8 %copy-start.4 = (bf16[128,4096]{1,0:T(8,128)(2,1)S(1)}, bf16[128,4096]{1,0:T(8,128)(2,1)}, u32[]{:S(2)}) copy-start(bf16[128,4096]{1,0:T(8,128)(2,1)} %get-tuple-element.68.refs_2_) | copy-start | bytes 3145732
  76.8 45.5 %collective-permute-start.7 = (bf16[128,4096]{1,0:T(8,128)(2,1)S(1)}, bf16[128,4096]{1,0:T(8,128)(2,1)S(1)}, u32[]{:S(2)}, u32[]{:S(2)}) collective-permute-start(bf16[128,4096]{1,0:T(8,128)(2,1)S(1)} %copy-done.3), channel_id=1, source_target_pairs={{0,1},{1,2},{2,3},{3,4},{4,5},{5,6},{6,7},{7,8},{8,9},{9,10},{10,1... | collective-permute-start | bytes 3145736 | tf_op jit(solution)/shard_map/ppermute | solution.py:362
  79.1 43.3 %collective-permute-start.8 = (bf16[128,4096]{1,0:T(8,128)(2,1)S(1)}, bf16[128,4096]{1,0:T(8,128)(2,1)}, u32[]{:S(2)}, u32[]{:S(2)}) collective-permute-start(bf16[128,4096]{1,0:T(8,128)(2,1)S(1)} %copy-done.4), channel_id=1, source_target_pairs={{1,0},{2,1},{3,2},{4,3},{5,4},{6,5},{7,6},{8,7},{9,8},{10,9},{11,1... | collective-permute-start | bytes 3145736 | tf_op jit(solution)/shard_map/ppermute | solution.py:362
  86.3 23.1 %all-to-all-start.1 = ((bf16[128,8,128]{2,1,0:T(8,128)(2,1)}), bf16[128,8,128]{2,1,0:T(8,128)(2,1)S(1)}, u32[]{:S(2)}, u32[]{:S(2)}) async-start(bf16[128,8,128]{2,1,0:T(8,128)(2,1)} %shard_map.221.refs_15_), calls=%async_computation.1 | async-start | bytes 524288 | tf_op jit(solution)/shard_map/all_to_all | solution.py:598
  109.4 0.7 copy-start
  122.3 1.0 copy-start.5
  123.3 25.4 %copy-start.9 = (bf16[24,4096]{1,0:T(8,128)(2,1)S(1)}, bf16[24,4096]{1,0:T(8,128)(2,1)}, u32[]{:S(2)}) copy-start(bf16[24,4096]{1,0:T(8,128)(2,1)} %get-tuple-element.89) | copy-start | bytes 589828
  141.1 19.0 %all-to-all-start.2 = ((f32[128,4,128]{2,1,0:T(4,128)}), f32[128,4,128]{2,1,0:T(4,128)S(1)}, u32[]{:S(2)}, u32[]{:S(2)}) async-start(f32[128,4,128]{2,1,0:T(4,128)} %shard_map.225), calls=%async_computation.2 | async-start | bytes 524288 | tf_op jit(solution)/shard_map/all_to_all | solution.py:623
  148.8 39.9 %collective-permute-start.11 = (bf16[24,4096]{1,0:T(8,128)(2,1)S(1)}, bf16[24,4096]{1,0:T(8,128)(2,1)S(1)}, u32[]{:S(2)}, u32[]{:S(2)}) collective-permute-start(bf16[24,4096]{1,0:T(8,128)(2,1)S(1)} %copy-done.9), channel_id=1, source_target_pairs={{1,0},{2,1},{3,2},{4,3},{5,4},{6,5},{7,6},{8,7},{9,8},{10,9},{11,1... | collective-permute-start | bytes 589832 | tf_op jit(solution)/shard_map/ppermute | solution.py:362
  160.1 0.7 copy-start.1
  173.0 15.7 %collective-permute-start.12 = (bf16[24,4096]{1,0:T(8,128)(2,1)}, bf16[24,4096]{1,0:T(8,128)(2,1)S(1)}, u32[]{:S(2)}, u32[]{:S(2)}) collective-permute-start(bf16[24,4096]{1,0:T(8,128)(2,1)} %get-tuple-element.90), channel_id=1, source_target_pairs={{1,0},{2,1},{3,2},{4,3},{5,4},{6,5},{7,6},{8,7},{9,8},{10,9},{11,1... | collective-permute-start | bytes 589832 | tf_op jit(solution)/shard_map/ppermute | solution.py:362
  188.7 0.7 copy-start.7
  188.8 0.7 copy-start.8

commit v3 on v2

--- a/solution.py
+++ b/solution.py
@@ -101,9 +101,10 @@
     return terms
 
 
-def pack_kernel(q, k, v, short, rate, resid, ltaps, rim, small, big):
-    for at, src in enumerate((q, k, v)):
-        rim[8 * at : 8 * at + 8] = src[...]
+def pack_kernel(q, k, v, short, rate, resid, ltaps, small, big, *rims):
+    for chunk, rim in enumerate(rims):
+        for at, src in enumerate((q, k, v)):
+            rim[8 * at : 8 * at + 8] = src[:, rim.shape[1] * chunk : rim.shape[1] * (chunk + 1)]
     small[...] = jnp.zeros_like(small)
     for at in range(3):
         small[7 * at : 7 * at + 7] = short[at]
@@ -206,8 +207,9 @@
 def mid_kernel(
     me, prod, gconv, before, after, rates, resids, ltaps,
     t_own, t_before, t_after, t_taps, t_head, t_inv3, spread,
-    yout, zout, tgrad, xx, own, prv, cur, nxt, tre, hre, cs, tsp, acc, coef,
+    *rest,
 ):
+    (yout, zout, tgrad, xx, own, prv, cur, nxt, tre, hre, cs, tsp, acc, coef) = rest[-14:]
     rows = prod.shape[0]
     quarter = pl.program_id(0) % (128 * CPG // BLOCK)
 
@@ -263,7 +265,10 @@
 
     @pl.when(quarter == 128 * CPG // BLOCK - 1)
     def _():
-        tgrad[...] = dot(t_inv3[...], stack3(acc[...]))
+        made = dot(t_inv3[...], stack3(acc[...]))
+        share = tgrad.shape[2]
+        for at in range(tgrad.shape[0]):
+            tgrad[at, 0] = made[share * at : share * at + share]
 
 
 def back_kernel(
@@ -324,12 +329,12 @@
 def tail_kernel(me, *refs):
     lasts, rims, taps = refs[:CHUNKS], refs[CHUNKS : 2 * CHUNKS], refs[2 * CHUNKS : 3 * CHUNKS]
     gq, gk, gv, ext = refs[3 * CHUNKS + 3 :]
-    pid = pl.program_id(0)
+    piece = pl.program_id(0) // (pl.num_programs(0) // CHUNKS)
     ext[:, 0:8] = jnp.zeros((3, 8, 128), F32)
     for chunk in range(CHUNKS):
         last, rim, tap = lasts[chunk], rims[chunk], taps[chunk]
 
-        @pl.when(pid == chunk)
+        @pl.when(piece == chunk)
         def _():
             def tile(n, _):
                 cols = pl.ds(pl.multiple_of(n * 128, 128), 128)
@@ -342,18 +347,6 @@
                 return 0
 
             lax.fori_loop(0, last.shape[1] // 128, tile, 0)
-
-
-def fold_kernel(me, *refs):
-    out = refs[-1]
-    share = out.shape[1]
-    owners = sum(part.shape[1] for part in refs[:-1]) // 128
-    for at in range(refs[0].shape[0] // share):
-        for own in range(owners):
-            chunk, part = divmod(own, owners // CHUNKS)
-            out[owners * at + own] = refs[chunk][
-                share * at : share * at + share, 128 * part : 128 * part + 128
-            ]
 
 
 def shift(value, steps):
@@ -395,27 +388,30 @@
     whole = lambda shape: pl.BlockSpec(shape, lambda i, *m: (0,) * len(shape))
     edge = pl.BlockSpec((8, width), lambda i: (rows // 8 - 1, 0))
 
-    rims, short, poles = pl.pallas_call(
+    short, poles, *rims = pl.pallas_call(
         pack_kernel,
         out_shape=(
-            jax.ShapeDtypeStruct((24, width), BF16),
             jax.ShapeDtypeStruct((24, 128), F32),
             jax.ShapeDtypeStruct((384, 128), F32),
-        ),
+        )
+        + (jax.ShapeDtypeStruct((24, per), BF16),) * CHUNKS,
         grid=(1,),
         in_specs=[edge] * 3
         + [whole(short_taps.shape), whole(decay_rate.shape), whole(residues.shape), whole(long_taps.shape)],
         out_specs=(
-            whole((24, width)),
             whole((24, 128)),
             whole((384, 128)),
-        ),
+        )
+        + (whole((24, per)),) * CHUNKS,
         compiler_params=params_of(60 << 20),
         name="pack",
     )(query, key, value, short_taps, decay_rate, residues, long_taps)
+    rims[0] = shift(rims[0], 1)
     short_all = gather_own(short)
-    rims = shift(rims, 1)
     poles_parts = ring_own(poles)
+    for chunk in range(1, CHUNKS):
+        edge_rows, _ = lax.optimization_barrier((rims[chunk], short_all))
+        rims[chunk] = shift(edge_rows, 1)
 
     def slot(me_ref, chunk):
         return (me_ref[0] - chunk + owners) % owners
@@ -475,8 +471,8 @@
         return call(
             front_kernel, 2_000_000_000, (steps,),
             [wide(chunk)] * 4
-            + [pl.BlockSpec((24, BLOCK), lambda i, m: (0, chunk * steps + i)), shorts(chunk), moment_spec, spread_spec],
-            (query, key, value, grad_out, rims, short_all, moment, spread),
+            + [pl.BlockSpec((24, BLOCK), lambda i, m: (0, i)), shorts(chunk), moment_spec, spread_spec],
+            (query, key, value, grad_out, rims[chunk], short_all, moment, spread),
             (part,) * 5
             + (jax.ShapeDtypeStruct((32, per), F32), jax.ShapeDtypeStruct((24, per), F32)),
             (here,) * 5
@@ -510,9 +506,11 @@
     )
     arrived = lax.all_to_all(states, AXES, 0, 0, tiled=True)
     for chunk in range(1, CHUNKS):
-        exchange(chunk, arrived)
-
-    def mid(chunk, after):
+        exchange(chunk, states)
+    ctxs = lax.axis_size("ctx")
+    share = rows // ctxs
+
+    def mid(chunk, pieces, after):
         consts = [tab(name) for name in ("own", "before", "after", "taps", "head", "inverse3")]
         spec32 = pltpu.VMEM((2 * rows, BLOCK), F32)
         spec16 = pltpu.VMEM((2 * rows, BLOCK), BF16)
@@ -525,13 +523,21 @@
                 pl.BlockSpec((1, 128, 128), lambda i, m: (owned(chunk, i, m), 2, 0)),
             ]
             + [spec for _, spec in consts]
-            + [spread_spec],
+            + [spread_spec]
+            + [pl.BlockSpec(memory_space=pl.ANY)] * len(pieces),
             [fronts[chunk][3], fronts[chunk][4], behinds[chunk], aheads[chunk]]
             + [poles_all] * 3
             + [c for c, _ in consts]
-            + [spread],
-            (spectrum,) * 2 + (jax.ShapeDtypeStruct((128, per // CPG), F32),),
-            (bins,) * 2 + (pl.BlockSpec((128, 128), lambda i, m: (0, i // quarters)),),
+            + [spread]
+            + pieces,
+            (spectrum,) * 2 + (jax.ShapeDtypeStruct((ctxs, owners, share, 128), F32),),
+            (bins,) * 2
+            + (
+                pl.BlockSpec(
+                    (ctxs, 1, share, 128),
+                    lambda i, m: (0, chunk * (owners // CHUNKS) + i // quarters, 0, 0),
+                ),
+            ),
             [spec16]
             + [spec32] * 6
             + [
@@ -540,7 +546,8 @@
                 pltpu.VMEM((2 * rows, 128), F32),
                 pltpu.VMEM((16, BLOCK), F32),
             ],
-            after=after,
+            {8 + len(consts) + 1: 2} if pieces else {},
+            after,
         )
 
     def back(chunk, ys, zs, outs, after):
@@ -579,6 +586,7 @@
             after,
         )
 
+    mids = [mid(0, [], [])]
     scanned = call(
         scan_kernel, 200_000_000, (1,),
         [
@@ -594,6 +602,7 @@
         jax.ShapeDtypeStruct(arrived.shape, BF16),
         whole(arrived.shape),
         [],
+        after=[mids[0][2]],
     )
     carried = lax.all_to_all(scanned, AXES, 0, 0, tiled=True)
 
@@ -605,34 +614,30 @@
         lasts.append(made[5])
         return made[:4]
 
-    mids = []
+    for chunk in range(1, CHUNKS):
+        mids.append(mid(chunk, [mids[-1][2]], [scanned]))
+    landed = lax.all_to_all(mids[-1][2].reshape(ctxs * owners, share, 128), AXES, 0, 0, tiled=True)
     for chunk in range(CHUNKS):
-        mids.append(mid(chunk, [lasts[-1]] if lasts else [scanned]))
-        if chunk < CHUNKS - 1:
-            outs = finish(chunk, [])
-    ctxs = lax.axis_size("ctx")
-    share = rows // ctxs
-    pieces = call(
-        fold_kernel, 100_000_000, (1,),
-        [whole((rows, per // CPG))] * CHUNKS,
-        [m[2] for m in mids],
-        jax.ShapeDtypeStruct((ctxs * owners, share, 128), F32),
-        whole((ctxs * owners, share, 128)),
-        [],
-    )
-    landed = lax.all_to_all(pieces, AXES, 0, 0, tiled=True)
-    outs = finish(CHUNKS - 1, [landed])
+        outs = finish(chunk, [])
     tokens = rows * ctxs * owners
     total = landed.sum(axis=0) * (1.0 / math.sqrt(tokens * CPG))
     every = lax.all_to_all(
         jnp.broadcast_to(total[None], (ctxs, share, 128)), "ctx", 0, 0, tiled=True
     )
 
-    strip = pl.BlockSpec((8, per), lambda i, m: (rows // 8 - 1, i))
+    cuts = 2
+    strip = pl.BlockSpec((8, per // cuts), lambda i, m: (rows // 8 - 1, i))
+    bands = [
+        pl.BlockSpec(
+            (24, per // cuts),
+            lambda i, m, chunk=chunk: (0, jnp.clip(i - cuts * chunk, 0, cuts - 1)),
+        )
+        for chunk in range(CHUNKS)
+    ]
     anyspec = pl.BlockSpec(memory_space=pl.ANY)
     grads = call(
-        tail_kernel, 200_000_000, (CHUNKS,),
-        [whole((24, per))] * (3 * CHUNKS) + [anyspec] * 3,
+        tail_kernel, 200_000_000, (CHUNKS * cuts,),
+        bands * 3 + [anyspec] * 3,
         (*lasts, *edges, *[f[6] for f in fronts], *outs[1:4]),
         (full,) * 3,
         (strip,) * 3,

time: 196 us -> 185 us (0.944)
  starting transfers between devices: 47.9 us -> 70.2 us
  blocking collectives: 32.2 us -> 14.6 us
  waiting for transfers between devices: 13.3 us -> 0.56 us
    all_to_all x1 -> x0, blocking collectives: 20.9 us -> none  [shards(): arrived = lax.all_to_all(states, AXES, 0, 0, tiled=True)]
    all_to_all x1 -> x2, starting transfers between devices: 7.66 us -> 21.8 us  [the longest x1 12.1 us: shards(): arrived = lax.all_to_all(states, AXES, 0, 0, tiled=True)]
    all_to_all x1 -> x2, waiting for transfers between devices: 6.48 us -> 0.52 us  [the longest x1 0.52 us: shards(): arrived = lax.all_to_all(states, AXES, 0, 0, tiled=True)]
    all_to_all x1, starting transfers between devices: 5.55 us -> 10.7 us  [shards(): carried = lax.all_to_all(scanned, AXES, 0, 0, tiled=True)]
    ppermute x6, waiting for transfers between devices: 4.5 us -> 0.02 us  [ring_own(): lax.ppermute(value, 'own', [(at, (at + hop) % count) for at in range(coun...]
    all_to_all x1, blocking collectives: 11.3 us -> 14.6 us  [shards(): lax.all_to_all(jnp.broadcast_to(total[None], (ctxs, share, 128)), 'ctx',...]
    all_to_all x1, waiting for transfers between devices: 2.26 us -> 0.01 us  [shards(): carried = lax.all_to_all(scanned, AXES, 0, 0, tiled=True)]
    ppermute x7 -> x8, starting transfers between devices: 26.9 us -> 28.6 us  [shift(): lax.ppermute(value, AXES, [(at, at + steps) for at in range(first, last)])]
  transfers between devices with their start and end apart: 15 -> 17, of which waited for: 4 -> 1; matrix products, arithmetic and copies ran while one was open for 2% -> 2% of each run, Pallas kernels for 35% -> 45%
where the time goes in v3:
time: 185 us; the launch traced here: 184 us
  Pallas kernels  89.9 us (49%)
  starting transfers between devices  70.2 us (38%)
  blocking collectives  14.6 us (8%)
  local copies, waits for them, and re-layouts  4.44 us (2%)
  other arithmetic  3.05 us (2%)
    pallas_call x9, Pallas kernels, call(): pl.pallas_call(body, out_shape=out_shape, grid_spec=pltpu.PrefetchScalarG...  88 us
    ppermute x8, starting transfers between devices, shift(): lax.ppermute(value, AXES, [(at, at + steps) for at in range(first, last)])  28.6 us
    all_to_all x1, blocking collectives, shards(): lax.all_to_all(jnp.broadcast_to(total[None], (ctxs, share, 128)), 'ctx',...  14.6 us
    all_to_all x1, starting transfers between devices, shards(): arrived = lax.all_to_all(states, AXES, 0, 0, tiled=True)  12.1 us
    all_to_all x1, starting transfers between devices, shards(): carried = lax.all_to_all(scanned, AXES, 0, 0, tiled=True)  10.7 us
    all_to_all x1, starting transfers between devices, shards(): lax.all_to_all(mids[-1][2].reshape(ctxs * owners, share, 128), AXES, 0, 0...  9.77 us
    ppermute x6, starting transfers between devices, ring_own(): lax.ppermute(value, 'own', [(at, (at + hop) % count) for at in range(coun...  9.1 us
    unnamed x23, local copies, waits for them, and re-layouts  4.43 us
  transfers between devices with their start and end apart: 17, of which 1 were waited for; matrix products, arithmetic and copies ran while one was open for 2% of the time, Pallas kernels for 45%

profile of v3, /device:TPU:1, one launch (start us, length us, event | category | flops | bytes accessed | tf_op | source)
XLA Modules:
  0.0 183.7 jit_solution(4193786997304740846)
XLA Ops:
  0.6 1.9 %pack.1 = (f32[24,128]{1,0:T(8,128)}, f32[384,128]{1,0:T(8,128)}, bf16[24,4096]{1,0:T(8,128)(2,1)}, bf16[24,4096]{1,0:T(8,128)(2,1)}) custom-call(bf16[128,8192]{1,0:T(8,128)(2,1)} %refs_1_.3, bf16[128,8192]{1,0:T(8,128)(2,1)} %refs_2_.3, bf16[128,8192]{1,0:T(8,128)(2,1)} %refs_3_.3, f32[3,7,128]{2,1,0:T(8,128)} %short.1, f32[8,2048]{1,0:T(8,128)} %rate.1, ...), custom_call_target="tpu_custom_call" | custom-call | tf_op jit(solution)/shard_map/pack/pallas_call | solution.py:391
  2.6 3.6 %collective-permute-start.2 = (f32[24,128]{1,0:T(8,128)}, f32[24,128]{1,0:T(8,128)S(1)}, u32[]{:S(2)}, u32[]{:S(2)}) collective-permute-start(f32[24,128]{1,0:T(8,128)} %get-tuple-element.54), channel_id=1, source_target_pairs={{0,3},{1,0},{2,1},{3,2},{4,7},{5,4},{6,5},{7,6},{8,11},{9,8},{10,9... | collective-permute-start | bytes 36872 | tf_op jit(solution)/shard_map/ppermute | solution.py:366
  6.1 0.3 collective-permute-start.1
  6.5 0.7 collective-permute-start
  7.2 3.5 %collective-permute-start.4 = (bf16[24,4096]{1,0:T(8,128)(2,1)}, bf16[24,4096]{1,0:T(8,128)(2,1)S(1)}, u32[]{:S(2)}, u32[]{:S(2)}) collective-permute-start(bf16[24,4096]{1,0:T(8,128)(2,1)} %get-tuple-element.56), channel_id=1, source_target_pairs={{0,1},{1,2},{2,3},{3,4},{4,5},{5,6},{6,7},{7,8},{8,9},{9,10},{10,1... | collective-permute-start | bytes 589832 | tf_op jit(solution)/shard_map/ppermute | solution.py:355
  10.7 3.9 %collective-permute-start.7 = (f32[384,128]{1,0:T(8,128)}, f32[384,128]{1,0:T(8,128)S(1)}, u32[]{:S(2)}, u32[]{:S(2)}) collective-permute-start(f32[384,128]{1,0:T(8,128)} %get-tuple-element.67), channel_id=1, source_target_pairs={{0,3},{1,0},{2,1},{3,2},{4,7},{5,4},{6,5},{7,6},{8,11},{9,8},{10,9... | collective-permute-start | bytes 589832 | tf_op jit(solution)/shard_map/ppermute | solution.py:366
  14.6 0.6 pad_add_fusion.refs_0_
  15.2 0.0 collective-permute-done.2
  15.2 0.0 collective-permute-start.6
  15.2 0.0 collective-permute-done.1
  15.2 0.6 collective-permute-start.5
  15.8 0.0 collective-permute-done
  15.8 1.3 pad_maximum_fusion.1.refs_6_
  17.1 4.1 %collective-permute-start.3 = (bf16[24,4096]{1,0:T(8,128)(2,1)}, bf16[24,4096]{1,0:T(8,128)(2,1)S(1)}, u32[]{:S(2)}, u32[]{:S(2)}) collective-permute-start(bf16[24,4096]{1,0:T(8,128)(2,1)} %get-tuple-element.55), channel_id=1, source_target_pairs={{0,1},{1,2},{2,3},{3,4},{4,5},{5,6},{6,7},{7,8},{8,9},{9,10},{10,1... | collective-permute-start | bytes 589832 | tf_op jit(solution)/shard_map/ppermute | solution.py:355
  21.2 0.0 collective-permute-done.4.refs_5_
  21.2 0.0 copy-start.6
  21.2 0.7 copy-done.6
  21.9 10.7 %shard_map.218 = (bf16[128,4096]{1,0:T(8,128)(2,1)}, bf16[128,4096]{1,0:T(8,128)(2,1)}, bf16[128,4096]{1,0:T(8,128)(2,1)}, bf16[128,4096]{1,0:T(8,128)(2,1)}, bf...) custom-call(s32[3]{0:T(128)} %pad_add_fusion.refs_0_, bf16[128,8192]{1,0:T(8,128)(2,1)} %refs_1_.3, ...), custom_call_target="tpu_custom_call" | custom-call | flops 2000000000 | bytes 10000000 | tf_op jit(solution)/shard_map/pallas_call | solution.py:451
  32.6 0.0 collective-permute-done.7
  32.6 0.0 collective-permute-done.6
  32.6 0.0 collective-permute-done.5
  32.6 1.9 %collective-permute-start.10 = (bf16[128,4096]{1,0:T(8,128)(2,1)}, bf16[128,4096]{1,0:T(8,128)(2,1)}, u32[]{:S(2)}, u32[]{:S(2)}) collective-permute-start(bf16[128,4096]{1,0:T(8,128)(2,1)} %get-tuple-element.73.refs_1_), channel_id=1, source_target_pairs={{0,1},{1,2},{2,3},{3,4},{4,5},{5,6},{6,7},{7,8},{8,9},{9,10},{10,1... | collective-permute-start | bytes 3145736 | tf_op jit(solution)/shard_map/ppermute | solution.py:355
  34.5 4.9 %collective-permute-start.11 = (bf16[128,4096]{1,0:T(8,128)(2,1)}, bf16[128,4096]{1,0:T(8,128)(2,1)}, u32[]{:S(2)}, u32[]{:S(2)}) collective-permute-start(bf16[128,4096]{1,0:T(8,128)(2,1)} %get-tuple-element.74.refs_2_), channel_id=1, source_target_pairs={{1,0},{2,1},{3,2},{4,3},{5,4},{6,5},{7,6},{8,7},{9,8},{10,9},{11,1... | collective-permute-start | bytes 3145736 | tf_op jit(solution)/shard_map/ppermute | solution.py:355
  39.4 0.0 copy-done.5
  39.4 0.9 pad_maximum_fusion.refs_3_.refs_5_.refs_6_.refs_7_.refs_2_.refs_10_.refs_11_
  40.3 0.0 collective-permute-done.3.refs_5_
  40.4 0.7 copy-done.7
  41.0 10.7 %shard_map.219 = (bf16[128,4096]{1,0:T(8,128)(2,1)}, bf16[128,4096]{1,0:T(8,128)(2,1)}, bf16[128,4096]{1,0:T(8,128)(2,1)}, bf16[128,4096]{1,0:T(8,128)(2,1)}, bf...) custom-call(s32[3]{0:T(128)} %pad_add_fusion.refs_0_, bf16[128,8192]{1,0:T(8,128)(2,1)} %refs_1_.3, ...), custom_call_target="tpu_custom_call" | custom-call | flops 2000000000 | bytes 10000000 | tf_op jit(solution)/shard_map/pallas_call | solution.py:451
  51.7 0.0 copy-start.1
  51.8 0.0 copy-start.2
  51.8 3.9 %shard_map.220 = bf16[128,8,128]{2,1,0:T(8,128)(2,1)} custom-call(s32[3]{0:T(128)} %pad_add_fusion.refs_0_, f32[32,4096]{1,0:T(8,128)} %get-tuple-element.57.refs_9_.refs_1_, f32[32,4096]{1,0:T(8,128)} %get-tuple-element.63.refs_2_, f32[4,384,128]{2,1,0:T(8,128)} %pad_maximum_fusion.refs_3_.refs_5_.refs_6_.refs_7_.refs_2_.refs_10_.refs_11_), custom_call_target="tpu_custom_call" | custom-call | flops 200000000 | bytes 1000000 | tf_op jit(solution)/shard_map/pallas_call | solution.py:451
  55.6 0.0 copy-done.1
  55.6 1.9 %collective-permute-start.8 = (bf16[128,4096]{1,0:T(8,128)(2,1)S(1)}, bf16[128,4096]{1,0:T(8,128)(2,1)S(1)}, u32[]{:S(2)}, u32[]{:S(2)}) collective-permute-start(bf16[128,4096]{1,0:T(8,128)(2,1)S(1)} %copy-done.1), channel_id=1, source_target_pairs={{0,1},{1,2},{2,3},{3,4},{4,5},{5,6},{6,7},{7,8},{8,9},{9,10},{10,1... | collective-permute-start | bytes 3145736 | tf_op jit(solution)/shard_map/ppermute | solution.py:355
  57.6 0.0 copy-done.2
  57.6 4.9 %collective-permute-start.9 = (bf16[128,4096]{1,0:T(8,128)(2,1)S(1)}, bf16[128,4096]{1,0:T(8,128)(2,1)}, u32[]{:S(2)}, u32[]{:S(2)}) collective-permute-start(bf16[128,4096]{1,0:T(8,128)(2,1)S(1)} %copy-done.2), channel_id=1, source_target_pairs={{1,0},{2,1},{3,2},{4,3},{5,4},{6,5},{7,6},{8,7},{9,8},{10,9},{11,1... | collective-permute-start | bytes 3145736 | tf_op jit(solution)/shard_map/ppermute | solution.py:355
  62.4 12.1 %all-to-all-start = ((bf16[128,8,128]{2,1,0:T(8,128)(2,1)}), bf16[128,8,128]{2,1,0:T(8,128)(2,1)S(1)}, u32[]{:S(2)}, u32[]{:S(2)}) async-start(bf16[128,8,128]{2,1,0:T(8,128)(2,1)} %shard_map.220), calls=%async_computation | async-start | bytes 524288 | tf_op jit(solution)/shard_map/all_to_all | solution.py:507
  74.5 0.0 collective-permute-done.10.refs_3_
  74.5 0.0 collective-permute-done.11.refs_4_
  74.5 15.3 %shard_map.221 = (bf16[256,4096]{1,0:T(8,128)(2,1)}, bf16[256,4096]{1,0:T(8,128)(2,1)}, f32[32,4,4,128]{3,2,1,0:T(4,128)}) custom-call(s32[3]{0:T(128)} %pad_add_fusion.refs_0_, bf16[128,4096]{1,0:T(8,128)(2,1)} %get-tuple-element.73.refs_1_, bf16[128,4096]{1,0:T(8,128)(2,1)} %get-tuple-element.74.refs_2_, ...), custom_call_target="tpu_custom_call" | custom-call | flops 2000000000 | bytes 10000000 | tf_op jit(solution)/shard_map/pallas_call | solution.py:451
  89.8 0.5 all-to-all-done.refs_1_
  90.3 0.7 copy-done.4
  91.0 2.6 %shard_map.222.refs_16_ = bf16[128,8,128]{2,1,0:T(8,128)(2,1)} custom-call(s32[3]{0:T(128)} %pad_add_fusion.refs_0_, bf16[128,8,128]{2,1,0:T(8,128)(2,1)} %copy-done.4, f32[4,384,128]{2,1,0:T(8,128)} %pad_maximum_fusion.refs_3_.refs_5_.refs_6_.refs_7_.refs_2_.refs_10_.refs_11_, f32[32,4,4,128]{3,2,1,0:T(4,128)} %get-tuple-element.75.refs_3_.refs_15_), custom_call_target="tpu_custom_call" | custom-call | flops 200000000 | bytes 1000000 | tf_op jit(solution)/shard_map/pallas_call | solution.py:451
  93.7 10.7 %all-to-all-start.1 = ((bf16[128,8,128]{2,1,0:T(8,128)(2,1)}), bf16[128,8,128]{2,1,0:T(8,128)(2,1)S(1)}, u32[]{:S(2)}, u32[]{:S(2)}) async-start(bf16[128,8,128]{2,1,0:T(8,128)(2,1)} %shard_map.222.refs_16_), calls=%async_computation.1 | async-start | bytes 524288 | tf_op jit(solution)/shard_map/all_to_all | solution.py:607
  104.3 0.0 collective-permute-done.8.refs_3_
  104.4 0.0 copy-start.3
  104.4 0.0 collective-permute-done.9.refs_4_
  104.4 0.9 copy-done.3
  105.3 15.3 %shard_map.223 = (bf16[256,4096]{1,0:T(8,128)(2,1)}, bf16[256,4096]{1,0:T(8,128)(2,1)}, f32[32,4,4,128]{3,2,1,0:T(4,128)}) custom-call(s32[3]{0:T(128)} %pad_add_fusion.refs_0_, bf16[128,4096]{1,0:T(8,128)(2,1)} %get-tuple-element.71.refs_1_, bf16[128,4096]{1,0:T(8,128)(2,1)} %get-tuple-element.72.refs_2_, ...), custom_call_target="tpu_custom_call", output_to_operand_aliasing={{2}: (15, {})} | custom-call | flops 2000000000 | bytes 10000000 | tf_op jit(solution)/shard_map/pallas_call | solution.py:451
  120.6 0.0 all-to-all-done.1.refs_7_.refs_8_
  120.7 9.8 %all-to-all-start.2 = ((f32[128,4,128]{2,1,0:T(4,128)}), f32[128,4,128]{2,1,0:T(4,128)S(1)}, u32[]{:S(2)}, u32[]{:S(2)}) async-start(f32[128,4,128]{2,1,0:T(4,128)} %bitcast.13), calls=%async_computation.2 | async-start | bytes 524288 | tf_op jit(solution)/shard_map/all_to_all | solution.py:619
  130.4 12.2 %shard_map.224 = (bf16[128,8192]{1,0:T(8,128)(2,1)}, bf16[128,8192]{1,0:T(8,128)(2,1)}, bf16[128,8192]{1,0:T(8,128)(2,1)}, bf16[128,8192]{1,0:T(8,128)(2,1)}, bf...) custom-call(s32[3]{0:T(128)} %pad_add_fusion.refs_0_, bf16[128,4096]{1,0:T(8,128)(2,1)} %get-tuple-element.79.refs_1_, ...), custom_call_target="tpu_custom_call" | custom-call | flops 2000000000 | bytes 10000000 | tf_op jit(solution)/shard_map/pallas_call | solution.py:451
  142.7 12.3 %shard_map.225 = (bf16[128,8192]{1,0:T(8,128)(2,1)}, bf16[128,8192]{1,0:T(8,128)(2,1)}, bf16[128,8192]{1,0:T(8,128)(2,1)}, bf16[128,8192]{1,0:T(8,128)(2,1)}, bf...) custom-call(s32[3]{0:T(128)} %pad_add_fusion.refs_0_, ...), custom_call_target="tpu_custom_call", output_to_operand_aliasing={{0}: (15, {}), {1}: (16, {}), {2}: (17, {}), {3}: (18, {})} | custom-call | flops 2000000000 | bytes 10000000 | tf_op jit(solution)/shard_map/pallas_call | solution.py:451
  155.0 4.8 %collective-permute-start.13 = (bf16[24,4096]{1,0:T(8,128)(2,1)}, bf16[24,4096]{1,0:T(8,128)(2,1)S(1)}, u32[]{:S(2)}, u32[]{:S(2)}) collective-permute-start(bf16[24,4096]{1,0:T(8,128)(2,1)} %get-tuple-element.93), channel_id=1, source_target_pairs={{1,0},{2,1},{3,2},{4,3},{5,4},{6,5},{7,6},{8,7},{9,8},{10,9},{11,1... | collective-permute-start | bytes 589832 | tf_op jit(solution)/shard_map/ppermute | solution.py:355
  159.8 0.0 copy-done.10
  159.8 2.7 %collective-permute-start.12 = (bf16[24,4096]{1,0:T(8,128)(2,1)S(1)}, bf16[24,4096]{1,0:T(8,128)(2,1)S(1)}, u32[]{:S(2)}, u32[]{:S(2)}) collective-permute-start(bf16[24,4096]{1,0:T(8,128)(2,1)S(1)} %copy-done.10), channel_id=1, source_target_pairs={{1,0},{2,1},{3,2},{4,3},{5,4},{6,5},{7,6},{8,7},{9,8},{10,9},{11,1... | collective-permute-start | bytes 589832 | tf_op jit(solution)/shard_map/ppermute | solution.py:355
  162.6 0.0 all-to-all-done.2
  162.6 0.1 reduce_sum.9
  162.8 14.6 %all_to_all.20 = f32[32,4,128]{2,1,0:T(4,128)S(1)} all-to-all(f32[32,4,128]{2,1,0:T(4,128)S(1)} %broadcast_in_dim.2), channel_id=1, replica_groups=mesh['ctx'=32,'own'=4] {'ctx'}, dimensions={0} | all-to-all | bytes 131072 | tf_op jit(solution)/shard_map/all_to_all | solution.py:624
  177.4 0.0 collective-permute-done.13.refs_4_
  177.4 0.0 collective-permute-done.12.refs_3_
  177.4 0.7 copy-done.8
  178.1 0.1 copy-done.9
  178.2 5.0 %shard_map.226 = (bf16[128,8192]{1,0:T(8,128)(2,1)}, bf16[128,8192]{1,0:T(8,128)(2,1)}, bf16[128,8192]{1,0:T(8,128)(2,1)}) custom-call(s32[3]{0:T(128)} %pad_add_fusion.refs_0_, f32[24,4096]{1,0:T(8,128)} %get-tuple-element.90.refs_1_, f32[24,4096]{1,0:T(8,128)} %get-tuple-element.91.refs_2_, ...), custom_call_target="tpu_custom_call", output_to_operand_aliasing={{0}: (7, {}), {1}: (8, {}), {2}: (9, {})} | custom-call | flops 200000000 | bytes 1000000 | tf_op jit(solution)/shard_map/pallas_call | solution.py:451
  183.1 0.6 copy.41
  (10 shorter events, 0.0 us)
Async XLA Ops:
  2.6 12.6 %collective-permute-start.2 = (f32[24,128]{1,0:T(8,128)}, f32[24,128]{1,0:T(8,128)S(1)}, u32[]{:S(2)}, u32[]{:S(2)}) collective-permute-start(f32[24,128]{1,0:T(8,128)} %get-tuple-element.54), channel_id=1, source_target_pairs={{0,3},{1,0},{2,1},{3,2},{4,7},{5,4},{6,5},{7,6},{8,11},{9,8},{10,9... | collective-permute-start | bytes 36872 | tf_op jit(solution)/shard_map/ppermute | solution.py:366
  6.1 9.1 %collective-permute-start.1 = (f32[24,128]{1,0:T(8,128)}, f32[24,128]{1,0:T(8,128)S(1)}, u32[]{:S(2)}, u32[]{:S(2)}) collective-permute-start(f32[24,128]{1,0:T(8,128)} %get-tuple-element.54), channel_id=1, source_target_pairs={{0,2},{1,3},{2,0},{3,1},{4,6},{5,7},{6,4},{7,5},{8,10},{9,11},{10,... | collective-permute-start | bytes 36872 | tf_op jit(solution)/shard_map/ppermute | solution.py:366
  6.5 9.3 %collective-permute-start = (f32[24,128]{1,0:T(8,128)}, f32[24,128]{1,0:T(8,128)S(1)}, u32[]{:S(2)}, u32[]{:S(2)}) collective-permute-start(f32[24,128]{1,0:T(8,128)} %get-tuple-element.54), channel_id=1, source_target_pairs={{0,1},{1,2},{2,3},{3,0},{4,5},{5,6},{6,7},{7,4},{8,9},{9,10},{10,1... | collective-permute-start | bytes 36872 | tf_op jit(solution)/shard_map/ppermute | solution.py:366
  7.2 14.1 %collective-permute-start.4 = (bf16[24,4096]{1,0:T(8,128)(2,1)}, bf16[24,4096]{1,0:T(8,128)(2,1)S(1)}, u32[]{:S(2)}, u32[]{:S(2)}) collective-permute-start(bf16[24,4096]{1,0:T(8,128)(2,1)} %get-tuple-element.56), channel_id=1, source_target_pairs={{0,1},{1,2},{2,3},{3,4},{4,5},{5,6},{6,7},{7,8},{8,9},{9,10},{10,1... | collective-permute-start | bytes 589832 | tf_op jit(solution)/shard_map/ppermute | solution.py:355
  10.7 21.9 %collective-permute-start.7 = (f32[384,128]{1,0:T(8,128)}, f32[384,128]{1,0:T(8,128)S(1)}, u32[]{:S(2)}, u32[]{:S(2)}) collective-permute-start(f32[384,128]{1,0:T(8,128)} %get-tuple-element.67), channel_id=1, source_target_pairs={{0,3},{1,0},{2,1},{3,2},{4,7},{5,4},{6,5},{7,6},{8,11},{9,8},{10,9... | collective-permute-start | bytes 589832 | tf_op jit(solution)/shard_map/ppermute | solution.py:366
  15.2 17.4 %collective-permute-start.6 = (f32[384,128]{1,0:T(8,128)}, f32[384,128]{1,0:T(8,128)S(1)}, u32[]{:S(2)}, u32[]{:S(2)}) collective-permute-start(f32[384,128]{1,0:T(8,128)} %get-tuple-element.67), channel_id=1, source_target_pairs={{0,2},{1,3},{2,0},{3,1},{4,6},{5,7},{6,4},{7,5},{8,10},{9,11},{10,... | collective-permute-start | bytes 589832 | tf_op jit(solution)/shard_map/ppermute | solution.py:366
  15.2 17.4 %collective-permute-start.5 = (f32[384,128]{1,0:T(8,128)}, f32[384,128]{1,0:T(8,128)S(1)}, u32[]{:S(2)}, u32[]{:S(2)}) collective-permute-start(f32[384,128]{1,0:T(8,128)} %get-tuple-element.67), channel_id=1, source_target_pairs={{0,1},{1,2},{2,3},{3,0},{4,5},{5,6},{6,7},{7,4},{8,9},{9,10},{10,1... | collective-permute-start | bytes 589832 | tf_op jit(solution)/shard_map/ppermute | solution.py:366
  17.1 22.3 %copy-start.5 = (f32[384,128]{1,0:T(8,128)S(1)}, f32[384,128]{1,0:T(8,128)}, u32[]{:S(2)}) copy-start(f32[384,128]{1,0:T(8,128)} %get-tuple-element.67) | copy-start | bytes 589828
  17.1 23.2 %collective-permute-start.3 = (bf16[24,4096]{1,0:T(8,128)(2,1)}, bf16[24,4096]{1,0:T(8,128)(2,1)S(1)}, u32[]{:S(2)}, u32[]{:S(2)}) collective-permute-start(bf16[24,4096]{1,0:T(8,128)(2,1)} %get-tuple-element.55), channel_id=1, source_target_pairs={{0,1},{1,2},{2,3},{3,4},{4,5},{5,6},{6,7},{7,8},{8,9},{9,10},{10,1... | collective-permute-start | bytes 589832 | tf_op jit(solution)/shard_map/ppermute | solution.py:355
  21.2 0.7 copy-start.6
  32.6 41.9 %collective-permute-start.10 = (bf16[128,4096]{1,0:T(8,128)(2,1)}, bf16[128,4096]{1,0:T(8,128)(2,1)}, u32[]{:S(2)}, u32[]{:S(2)}) collective-permute-start(bf16[128,4096]{1,0:T(8,128)(2,1)} %get-tuple-element.73.refs_1_), channel_id=1, source_target_pairs={{0,1},{1,2},{2,3},{3,4},{4,5},{5,6},{6,7},{7,8},{8,9},{9,10},{10,1... | collective-permute-start | bytes 3145736 | tf_op jit(solution)/shard_map/ppermute | solution.py:355
  34.5 40.0 %collective-permute-start.11 = (bf16[128,4096]{1,0:T(8,128)(2,1)}, bf16[128,4096]{1,0:T(8,128)(2,1)}, u32[]{:S(2)}, u32[]{:S(2)}) collective-permute-start(bf16[128,4096]{1,0:T(8,128)(2,1)} %get-tuple-element.74.refs_2_), channel_id=1, source_target_pairs={{1,0},{2,1},{3,2},{4,3},{5,4},{6,5},{7,6},{8,7},{9,8},{10,9},{11,1... | collective-permute-start | bytes 3145736 | tf_op jit(solution)/shard_map/ppermute | solution.py:355
  40.4 0.7 copy-start.7
  51.7 3.9 %copy-start.1 = (bf16[128,4096]{1,0:T(8,128)(2,1)S(1)}, bf16[128,4096]{1,0:T(8,128)(2,1)}, u32[]{:S(2)}) copy-start(bf16[128,4096]{1,0:T(8,128)(2,1)} %get-tuple-element.71.refs_1_) | copy-start | bytes 3145732
  51.8 5.8 %copy-start.2 = (bf16[128,4096]{1,0:T(8,128)(2,1)S(1)}, bf16[128,4096]{1,0:T(8,128)(2,1)}, u32[]{:S(2)}) copy-start(bf16[128,4096]{1,0:T(8,128)(2,1)} %get-tuple-element.72.refs_2_) | copy-start | bytes 3145732
  55.6 48.7 %collective-permute-start.8 = (bf16[128,4096]{1,0:T(8,128)(2,1)S(1)}, bf16[128,4096]{1,0:T(8,128)(2,1)S(1)}, u32[]{:S(2)}, u32[]{:S(2)}) collective-permute-start(bf16[128,4096]{1,0:T(8,128)(2,1)S(1)} %copy-done.1), channel_id=1, source_target_pairs={{0,1},{1,2},{2,3},{3,4},{4,5},{5,6},{6,7},{7,8},{8,9},{9,10},{10,1... | collective-permute-start | bytes 3145736 | tf_op jit(solution)/shard_map/ppermute | solution.py:355
  57.6 46.8 %collective-permute-start.9 = (bf16[128,4096]{1,0:T(8,128)(2,1)S(1)}, bf16[128,4096]{1,0:T(8,128)(2,1)}, u32[]{:S(2)}, u32[]{:S(2)}) collective-permute-start(bf16[128,4096]{1,0:T(8,128)(2,1)S(1)} %copy-done.2), channel_id=1, source_target_pairs={{1,0},{2,1},{3,2},{4,3},{5,4},{6,5},{7,6},{8,7},{9,8},{10,9},{11,1... | collective-permute-start | bytes 3145736 | tf_op jit(solution)/shard_map/ppermute | solution.py:355
  62.4 27.9 %all-to-all-start = ((bf16[128,8,128]{2,1,0:T(8,128)(2,1)}), bf16[128,8,128]{2,1,0:T(8,128)(2,1)S(1)}, u32[]{:S(2)}, u32[]{:S(2)}) async-start(bf16[128,8,128]{2,1,0:T(8,128)(2,1)} %shard_map.220), calls=%async_computation | async-start | bytes 524288 | tf_op jit(solution)/shard_map/all_to_all | solution.py:507
  90.3 0.7 copy-start.4
  93.7 27.0 %all-to-all-start.1 = ((bf16[128,8,128]{2,1,0:T(8,128)(2,1)}), bf16[128,8,128]{2,1,0:T(8,128)(2,1)S(1)}, u32[]{:S(2)}, u32[]{:S(2)}) async-start(bf16[128,8,128]{2,1,0:T(8,128)(2,1)} %shard_map.222.refs_16_), calls=%async_computation.1 | async-start | bytes 524288 | tf_op jit(solution)/shard_map/all_to_all | solution.py:607
  104.4 1.0 copy-start.3
  120.7 9.8 %copy-start = (bf16[128,8,128]{2,1,0:T(8,128)(2,1)}, bf16[128,8,128]{2,1,0:T(8,128)(2,1)S(1)}, u32[]{:S(2)}) copy-start(bf16[128,8,128]{2,1,0:T(8,128)(2,1)S(1)} %all-to-all-done.1.refs_7_.refs_8_) | copy-start | bytes 786436
  120.7 41.9 %all-to-all-start.2 = ((f32[128,4,128]{2,1,0:T(4,128)}), f32[128,4,128]{2,1,0:T(4,128)S(1)}, u32[]{:S(2)}, u32[]{:S(2)}) async-start(f32[128,4,128]{2,1,0:T(4,128)} %bitcast.13), calls=%async_computation.2 | async-start | bytes 524288 | tf_op jit(solution)/shard_map/all_to_all | solution.py:619
  142.7 17.2 %copy-start.10 = (bf16[24,4096]{1,0:T(8,128)(2,1)S(1)}, bf16[24,4096]{1,0:T(8,128)(2,1)}, u32[]{:S(2)}) copy-start(bf16[24,4096]{1,0:T(8,128)(2,1)} %get-tuple-element.92) | copy-start | bytes 589828
  155.0 22.4 %collective-permute-start.13 = (bf16[24,4096]{1,0:T(8,128)(2,1)}, bf16[24,4096]{1,0:T(8,128)(2,1)S(1)}, u32[]{:S(2)}, u32[]{:S(2)}) collective-permute-start(bf16[24,4096]{1,0:T(8,128)(2,1)} %get-tuple-element.93), channel_id=1, source_target_pairs={{1,0},{2,1},{3,2},{4,3},{5,4},{6,5},{7,6},{8,7},{9,8},{10,9},{11,1... | collective-permute-start | bytes 589832 | tf_op jit(solution)/shard_map/ppermute | solution.py:355
  159.8 17.5 %collective-permute-start.12 = (bf16[24,4096]{1,0:T(8,128)(2,1)S(1)}, bf16[24,4096]{1,0:T(8,128)(2,1)S(1)}, u32[]{:S(2)}, u32[]{:S(2)}) collective-permute-start(bf16[24,4096]{1,0:T(8,128)(2,1)S(1)} %copy-done.10), channel_id=1, source_target_pairs={{1,0},{2,1},{3,2},{4,3},{5,4},{6,5},{7,6},{8,7},{9,8},{10,9},{11,1... | collective-permute-start | bytes 589832 | tf_op jit(solution)/shard_map/ppermute | solution.py:355
  177.4 0.7 copy-start.8
  177.4 0.8 copy-start.9

commit v4 on v3

--- a/solution.py
+++ b/solution.py
@@ -1,3 +1,4 @@
+import functools
 import math
 
 import jax
@@ -116,9 +117,12 @@
 
 
 def front_kernel(
-    me, q, k, v, g, rim, short, moment, spread,
-    qf, kf, vf, prod, gconv, mom, taps, xq, xk, xv,
+    me, q, k, v, g, rim, short, moment, spread, *rest, pieces=0
 ):
+    moms, rates = rest[: max(pieces - 1, 0)], rest[max(pieces - 1, 0) : max(2 * pieces - 1, 0)]
+    outs = rest[len(moms) + len(rates) :]
+    qf, kf, vf, prod, gconv, mom, taps = outs[:7]
+    xq, xk, xv = outs[-3:]
     rows = q.shape[0]
     taps[...] = spread_taps(short[0], spread[...])
     lanes = range(BLOCK // 128)
@@ -151,32 +155,18 @@
     p, c = prod[...], gconv[...]
     mom[0:16] = dot(moment[0:16, :], jnp.concatenate([p, p], axis=0))
     mom[16:32] = dot(moment[16:32, :], jnp.concatenate([c, c], axis=0))
-
-
-def state_kernel(me, *refs):
-    moms, rates, out = refs[:CHUNKS], refs[CHUNKS], refs[CHUNKS + 1]
-    owners = rates.shape[0]
-    per = out.shape[0] // (2 * owners)
-    for own in range(owners):
-        chunk, part = divmod(own, owners // CHUNKS)
-        mom = moms[chunk]
-        slot = (me[0] - own + owners) % owners
-
-        def tile(n, _):
-            eight = pl.ds(pl.multiple_of(n * 8, 8), 8)
-            cols = pl.ds(pl.multiple_of((part * per + n) * 128, 128), 128)
-            terms = chebyshev(rates[slot, eight, :])
-            mine = mom[:, cols]
+    for piece in range(pieces):
+        source, states = (*moms, mom)[piece], outs[7]
+        for lane in lanes:
+            mine = source[:, 128 * lane : 128 * lane + 128]
+            terms = chebyshev(rates[piece][0, 8 * lane : 8 * lane + 8, :])
             ahead = terms[0] * mine[0:1]
             back = terms[0] * mine[16:17]
             for at in range(1, TERMS):
                 ahead = ahead + terms[at] * mine[at : at + 1]
                 back = back + terms[at] * mine[16 + at : 17 + at]
-            out[own * per + n] = ahead.astype(BF16)
-            out[(owners + own) * per + n] = back.astype(BF16)
-            return 0
-
-        lax.fori_loop(0, per, tile, 0, unroll=4)
+            states[0, piece, lane] = ahead.astype(BF16)
+            states[1, piece, lane] = back.astype(BF16)
 
 
 def scan_kernel(me, states, rates, out):
@@ -224,41 +214,43 @@
     one_hot = spread[...]
     xx[0:128] = one_hot
     xx[128:256] = one_hot
-    tre[...] = dot(tsp[...], xx[...])
-    for src, table, dst in (
-        (prod, t_own, own), (before, t_before, prv), (gconv, t_own, cur), (after, t_after, nxt),
-    ):
-        value = src[...]
-        xx[0:rows] = value
-        xx[rows:] = value
-        dst[...] = dot(table[...], xx[...])
     for lane in range(BLOCK // 128):
         cols = slice(128 * lane, 128 * lane + 128)
         eight = slice(8 * lane, 8 * lane + 8)
         weight = modal_weight(rates[0, eight, :], resids[0, eight, :])
         for n, term in enumerate(chebyshev(rates[0, eight, :])):
             coef[n : n + 1, cols] = jnp.sum(term * weight, axis=0, keepdims=True)
-    hre[...] = dot(t_head[...], stack3(coef[...]))
-
-    def bins(r, _):
-        base = pl.multiple_of(r * 16, 16)
-        re = pl.ds(base, 16)
-        im = pl.ds(rows + base, 16)
-        for lane in range(BLOCK // 128):
-            cols = slice(128 * lane, 128 * lane + 128)
-            tr, ti, hr, hi = tre[re, cols], tre[im, cols], hre[re, cols], hre[im, cols]
-            pr, pi, cr, ci = own[re, cols], own[im, cols], cur[re, cols], cur[im, cols]
-            wr, wi = pr + prv[re, cols], pi + prv[im, cols]
-            ar, ai = cr + nxt[re, cols], ci + nxt[im, cols]
-            yout[re, cols] = (wr * tr - wi * ti + (pr * hr - pi * hi)).astype(BF16)
-            yout[im, cols] = (wr * ti + wi * tr + (pr * hi + pi * hr)).astype(BF16)
-            zout[re, cols] = (ar * tr + ai * ti + (cr * hr + ci * hi)).astype(BF16)
-            zout[im, cols] = (ai * tr - ar * ti + (ci * hr - cr * hi)).astype(BF16)
-            cs[re, cols] = (cr * wr + ci * wi).astype(BF16)
-            cs[im, cols] = (ci * wr - cr * wi).astype(BF16)
-        return 0
-
-    lax.fori_loop(0, rows // 16, bins, 0)
+
+    def transforms(half):
+        wide = slice(256 * half, 256 * half + 256)
+        tre[:, wide] = dot(tsp[...], xx[:, wide])
+        for src, table, dst in (
+            (prod, t_own, own), (before, t_before, prv), (gconv, t_own, cur), (after, t_after, nxt),
+        ):
+            value = src[:, wide]
+            dst[:, wide] = dot(table[...], jnp.concatenate([value, value], axis=0))
+        hre[:, wide] = dot(t_head[...], stack3(coef[:, wide]))
+
+    def bins(base, lane):
+        re = slice(base, base + 16)
+        im = slice(rows + base, rows + base + 16)
+        cols = slice(128 * lane, 128 * lane + 128)
+        tr, ti, hr, hi = tre[re, cols], tre[im, cols], hre[re, cols], hre[im, cols]
+        pr, pi, cr, ci = own[re, cols], own[im, cols], cur[re, cols], cur[im, cols]
+        wr, wi = pr + prv[re, cols], pi + prv[im, cols]
+        ar, ai = cr + nxt[re, cols], ci + nxt[im, cols]
+        yout[re, cols] = (wr * tr - wi * ti + (pr * hr - pi * hi)).astype(BF16)
+        yout[im, cols] = (wr * ti + wi * tr + (pr * hi + pi * hr)).astype(BF16)
+        zout[re, cols] = (ar * tr + ai * ti + (cr * hr + ci * hi)).astype(BF16)
+        zout[im, cols] = (ai * tr - ar * ti + (ci * hr - cr * hi)).astype(BF16)
+        cs[re, cols] = (cr * wr + ci * wi).astype(BF16)
+        cs[im, cols] = (ci * wr - cr * wi).astype(BF16)
+
+    for half in range(BLOCK // 256):
+        transforms(half)
+        for lane in (2 * half, 2 * half + 1):
+            for base in range(0, rows, 16):
+                bins(base, lane)
     acc[...] += lax.dot_general(
         cs[...], spread[...], (((1,), (1,)), ((), ())), preferred_element_type=F32
     )
@@ -346,7 +338,7 @@
                     dst[:, cols] = total.astype(BF16)
                 return 0
 
-            lax.fori_loop(0, last.shape[1] // 128, tile, 0)
+            lax.fori_loop(0, last.shape[1] // 128, tile, 0, unroll=4)
 
 
 def shift(value, steps):
@@ -468,26 +460,31 @@
 
     def front(chunk, after):
         moment, moment_spec = tab("moment")
+        final = chunk == CHUNKS - 1
+        mom_spec = pl.BlockSpec((32, BLOCK), lambda i, m: (0, i))
+        in_specs = [wide(chunk)] * 4 + [
+            pl.BlockSpec((24, BLOCK), lambda i, m: (0, i)), shorts(chunk), moment_spec, spread_spec,
+        ]
+        operands = [query, key, value, grad_out, rims[chunk], short_all, moment, spread]
+        out_shape = (part,) * 5 + (
+            jax.ShapeDtypeStruct((32, per), F32), jax.ShapeDtypeStruct((24, per), F32),
+        )
+        out_specs = (here,) * 5 + (mom_spec, pl.BlockSpec((24, BLOCK), lambda i, m: (0, i)))
+        if final:
+            in_specs += [mom_spec] * chunk + [poles_at(c, 0) for c in range(CHUNKS)]
+            operands += [f[5] for f in fronts] + [poles_all] * CHUNKS
+            out_shape += (jax.ShapeDtypeStruct((2, CHUNKS, per // 128, 8, 128), BF16),)
+            out_specs += (
+                pl.BlockSpec((2, CHUNKS, group, 8, 128), lambda i, m: (0, 0, i, 0, 0)),
+            )
         return call(
-            front_kernel, 2_000_000_000, (steps,),
-            [wide(chunk)] * 4
-            + [pl.BlockSpec((24, BLOCK), lambda i, m: (0, i)), shorts(chunk), moment_spec, spread_spec],
-            (query, key, value, grad_out, rims[chunk], short_all, moment, spread),
-            (part,) * 5
-            + (jax.ShapeDtypeStruct((32, per), F32), jax.ShapeDtypeStruct((24, per), F32)),
-            (here,) * 5
-            + (
-                pl.BlockSpec((32, BLOCK), lambda i, m: (0, i)),
-                pl.BlockSpec((24, BLOCK), lambda i, m: (0, i)),
-            ),
+            functools.partial(front_kernel, pieces=CHUNKS if final else 0),
+            2_000_000_000, (steps,), in_specs, operands, out_shape, out_specs,
             [pltpu.VMEM((group, rows + 8, 128), F32)] * 3,
             after=after,
         )
 
     fronts, behinds, aheads = [], [], []
-    for chunk in range(CHUNKS):
-        made = front(chunk, [fronts[-1][5]] if fronts else [])
-        fronts.append(made)
 
     def exchange(chunk, after):
         prod, gconv, after = lax.optimization_barrier((fronts[chunk][3], fronts[chunk][4], after))
@@ -495,15 +492,11 @@
         aheads.append(shift(gconv, -1))
         return after
 
+    fronts.append(front(0, []))
     poles_all = jnp.stack(exchange(0, tuple(poles_parts)))
-    states = call(
-        state_kernel, 200_000_000, (1,),
-        [whole((32, per))] * CHUNKS + [pl.BlockSpec((owners, 128, 128), lambda i, m: (0, 0, 0))],
-        [f[5] for f in fronts] + [poles_all],
-        jax.ShapeDtypeStruct((2 * half, 8, 128), BF16),
-        whole((2 * half, 8, 128)),
-        [],
-    )
+    for chunk in range(1, CHUNKS):
+        fronts.append(front(chunk, [fronts[-1][5]]))
+    states = fronts[-1][7].reshape(2 * half, 8, 128)
     arrived = lax.all_to_all(states, AXES, 0, 0, tiled=True)
     for chunk in range(1, CHUNKS):
         exchange(chunk, states)
@@ -625,7 +618,7 @@
         jnp.broadcast_to(total[None], (ctxs, share, 128)), "ctx", 0, 0, tiled=True
     )
 
-    cuts = 2
+    cuts = 1
     strip = pl.BlockSpec((8, per // cuts), lambda i, m: (rows // 8 - 1, i))
     bands = [
         pl.BlockSpec(

time: 185 us -> 181 us (0.978)
  Pallas kernels: 89.9 us -> 80 us
  waiting for transfers between devices: 0.56 us -> 5.33 us
  local copies, waits for them, and re-layouts: 4.44 us -> 6.32 us
    pallas_call x9 -> x8, Pallas kernels: 88 us -> 78.1 us  [call(): pl.pallas_call(body, out_shape=out_shape, grid_spec=pltpu.PrefetchScalarG...]
    all_to_all x1, waiting for transfers between devices: 0.52 us -> 5.29 us  [shards(): arrived = lax.all_to_all(states, AXES, 0, 0, tiled=True)]
    unnamed x23, local copies, waits for them, and re-layouts: 4.43 us -> 6.31 us
  transfers between devices with their start and end apart: 17 -> 17, of which waited for: 1 -> 1; matrix products, arithmetic and copies ran while one was open for 2% -> 2% of each run, Pallas kernels for 45% -> 41%
where the time goes in v4:
time: 181 us; the launch traced here: 180 us
  Pallas kernels  80 us (44%)
  starting transfers between devices  69.4 us (38%)
  blocking collectives  14.6 us (8%)
  local copies, waits for them, and re-layouts  6.32 us (3%)
  waiting for transfers between devices  5.33 us (3%)
  other arithmetic  3.08 us (2%)
    pallas_call x8, Pallas kernels, call(): pl.pallas_call(body, out_shape=out_shape, grid_spec=pltpu.PrefetchScalarG...  78.1 us
    ppermute x8, starting transfers between devices, shift(): lax.ppermute(value, AXES, [(at, at + steps) for at in range(first, last)])  28.6 us
    all_to_all x1, blocking collectives, shards(): lax.all_to_all(jnp.broadcast_to(total[None], (ctxs, share, 128)), 'ctx',...  14.6 us
    all_to_all x1, starting transfers between devices, shards(): arrived = lax.all_to_all(states, AXES, 0, 0, tiled=True)  12 us
    all_to_all x1, starting transfers between devices, shards(): carried = lax.all_to_all(scanned, AXES, 0, 0, tiled=True)  9.86 us
    all_to_all x1, starting transfers between devices, shards(): lax.all_to_all(mids[-1][2].reshape(ctxs * owners, share, 128), AXES, 0, 0...  9.76 us
    ppermute x6, starting transfers between devices, ring_own(): lax.ppermute(value, 'own', [(at, (at + hop) % count) for at in range(coun...  9.1 us
    unnamed x23, local copies, waits for them, and re-layouts  6.31 us
  transfers between devices with their start and end apart: 17, of which 1 were waited for; matrix products, arithmetic and copies ran while one was open for 2% of the time, Pallas kernels for 41%

profile of v4, /device:TPU:1, one launch (start us, length us, event | category | flops | bytes accessed | tf_op | source)
XLA Modules:
  0.0 179.7 jit_solution(8471556472401186233)
XLA Ops:
  0.6 1.9 %pack.1 = (f32[24,128]{1,0:T(8,128)}, f32[384,128]{1,0:T(8,128)}, bf16[24,4096]{1,0:T(8,128)(2,1)}, bf16[24,4096]{1,0:T(8,128)(2,1)}) custom-call(bf16[128,8192]{1,0:T(8,128)(2,1)} %refs_1_.3, bf16[128,8192]{1,0:T(8,128)(2,1)} %refs_2_.3, bf16[128,8192]{1,0:T(8,128)(2,1)} %refs_3_.3, f32[3,7,128]{2,1,0:T(8,128)} %short.1, f32[8,2048]{1,0:T(8,128)} %rate.1, ...), custom_call_target="tpu_custom_call" | custom-call | tf_op jit(solution)/shard_map/pack/pallas_call | solution.py:383
  2.6 3.6 %collective-permute-start.2 = (f32[24,128]{1,0:T(8,128)}, f32[24,128]{1,0:T(8,128)S(1)}, u32[]{:S(2)}, u32[]{:S(2)}) collective-permute-start(f32[24,128]{1,0:T(8,128)} %get-tuple-element.54), channel_id=1, source_target_pairs={{0,3},{1,0},{2,1},{3,2},{4,7},{5,4},{6,5},{7,6},{8,11},{9,8},{10,9... | collective-permute-start | bytes 36872 | tf_op jit(solution)/shard_map/ppermute | solution.py:358
  6.1 0.3 collective-permute-start.1
  6.5 0.7 collective-permute-start
  7.2 3.5 %collective-permute-start.4 = (bf16[24,4096]{1,0:T(8,128)(2,1)}, bf16[24,4096]{1,0:T(8,128)(2,1)S(1)}, u32[]{:S(2)}, u32[]{:S(2)}) collective-permute-start(bf16[24,4096]{1,0:T(8,128)(2,1)} %get-tuple-element.56), channel_id=1, source_target_pairs={{0,1},{1,2},{2,3},{3,4},{4,5},{5,6},{6,7},{7,8},{8,9},{9,10},{10,1... | collective-permute-start | bytes 589832 | tf_op jit(solution)/shard_map/ppermute | solution.py:347
  10.7 3.9 %collective-permute-start.7 = (f32[384,128]{1,0:T(8,128)}, f32[384,128]{1,0:T(8,128)S(1)}, u32[]{:S(2)}, u32[]{:S(2)}) collective-permute-start(f32[384,128]{1,0:T(8,128)} %get-tuple-element.61), channel_id=1, source_target_pairs={{0,3},{1,0},{2,1},{3,2},{4,7},{5,4},{6,5},{7,6},{8,11},{9,8},{10,9... | collective-permute-start | bytes 589832 | tf_op jit(solution)/shard_map/ppermute | solution.py:358
  14.6 0.6 pad_add_fusion.refs_0_
  15.2 0.0 collective-permute-done.2
  15.2 0.0 collective-permute-start.6
  15.2 0.0 collective-permute-done.1
  15.2 0.6 collective-permute-start.5
  15.8 0.0 collective-permute-done
  15.8 1.3 pad_maximum_fusion.1.refs_6_
  17.2 4.1 %collective-permute-start.3 = (bf16[24,4096]{1,0:T(8,128)(2,1)}, bf16[24,4096]{1,0:T(8,128)(2,1)S(1)}, u32[]{:S(2)}, u32[]{:S(2)}) collective-permute-start(bf16[24,4096]{1,0:T(8,128)(2,1)} %get-tuple-element.55), channel_id=1, source_target_pairs={{0,1},{1,2},{2,3},{3,4},{4,5},{5,6},{6,7},{7,8},{8,9},{9,10},{10,1... | collective-permute-start | bytes 589832 | tf_op jit(solution)/shard_map/ppermute | solution.py:347
  21.2 0.0 collective-permute-done.4.refs_5_
  21.2 0.0 copy-start.6
  21.3 0.7 copy-done.6
  21.9 10.7 %shard_map.218 = (bf16[128,4096]{1,0:T(8,128)(2,1)}, bf16[128,4096]{1,0:T(8,128)(2,1)}, bf16[128,4096]{1,0:T(8,128)(2,1)}, bf16[128,4096]{1,0:T(8,128)(2,1)}, bf...) custom-call(s32[3]{0:T(128)} %pad_add_fusion.refs_0_, bf16[128,8192]{1,0:T(8,128)(2,1)} %refs_1_.3, ...), custom_call_target="tpu_custom_call" | custom-call | flops 2000000000 | bytes 10000000 | tf_op jit(solution)/shard_map/pallas_call | solution.py:443
  32.6 0.0 collective-permute-done.7
  32.6 0.0 collective-permute-done.6
  32.6 0.0 collective-permute-done.5
  32.6 1.9 %collective-permute-start.10 = (bf16[128,4096]{1,0:T(8,128)(2,1)}, bf16[128,4096]{1,0:T(8,128)(2,1)S(1)}, u32[]{:S(2)}, u32[]{:S(2)}) collective-permute-start(bf16[128,4096]{1,0:T(8,128)(2,1)} %get-tuple-element.73.refs_1_), channel_id=1, source_target_pairs={{0,1},{1,2},{2,3},{3,4},{4,5},{5,6},{6,7},{7,8},{8,9},{9,10},{10,1... | collective-permute-start | bytes 3145736 | tf_op jit(solution)/shard_map/ppermute | solution.py:347
  34.5 4.9 %collective-permute-start.11 = (bf16[128,4096]{1,0:T(8,128)(2,1)}, bf16[128,4096]{1,0:T(8,128)(2,1)}, u32[]{:S(2)}, u32[]{:S(2)}) collective-permute-start(bf16[128,4096]{1,0:T(8,128)(2,1)} %get-tuple-element.74.refs_2_), channel_id=1, source_target_pairs={{1,0},{2,1},{3,2},{4,3},{5,4},{6,5},{7,6},{8,7},{9,8},{10,9},{11,1... | collective-permute-start | bytes 3145736 | tf_op jit(solution)/shard_map/ppermute | solution.py:347
  39.4 0.0 copy-done.5
  39.4 1.0 pad_maximum_fusion.refs_10_.refs_11_.refs_5_.refs_6_.refs_7_.refs_2_
  40.4 0.0 collective-permute-done.3.refs_5_
  40.4 0.7 copy-done.7
  41.1 11.2 %shard_map.219 = (bf16[128,4096]{1,0:T(8,128)(2,1)}, bf16[128,4096]{1,0:T(8,128)(2,1)}, bf16[128,4096]{1,0:T(8,128)(2,1)}, bf16[128,4096]{1,0:T(8,128)(2,1)}, bf...) custom-call(s32[3]{0:T(128)} %pad_add_fusion.refs_0_, ...), custom_call_target="tpu_custom_call" | custom-call | flops 2000000000 | bytes 10000000 | tf_op jit(solution)/shard_map/pallas_call | solution.py:443
  52.2 1.9 %collective-permute-start.8 = (bf16[128,4096]{1,0:T(8,128)(2,1)}, bf16[128,4096]{1,0:T(8,128)(2,1)S(1)}, u32[]{:S(2)}, u32[]{:S(2)}) collective-permute-start(bf16[128,4096]{1,0:T(8,128)(2,1)} %get-tuple-element.71.refs_1_), channel_id=1, source_target_pairs={{0,1},{1,2},{2,3},{3,4},{4,5},{5,6},{6,7},{7,8},{8,9},{9,10},{10,1... | collective-permute-start | bytes 3145736 | tf_op jit(solution)/shard_map/ppermute | solution.py:347
  54.2 4.9 %collective-permute-start.9 = (bf16[128,4096]{1,0:T(8,128)(2,1)}, bf16[128,4096]{1,0:T(8,128)(2,1)S(1)}, u32[]{:S(2)}, u32[]{:S(2)}) collective-permute-start(bf16[128,4096]{1,0:T(8,128)(2,1)} %get-tuple-element.72.refs_2_), channel_id=1, source_target_pairs={{1,0},{2,1},{3,2},{4,3},{5,4},{6,5},{7,6},{8,7},{9,8},{10,9},{11,1... | collective-permute-start | bytes 3145736 | tf_op jit(solution)/shard_map/ppermute | solution.py:347
  59.0 12.0 %all-to-all-start = ((bf16[128,8,128]{2,1,0:T(8,128)(2,1)}), bf16[128,8,128]{2,1,0:T(8,128)(2,1)S(1)}, u32[]{:S(2)}, u32[]{:S(2)}) async-start(bf16[128,8,128]{2,1,0:T(8,128)(2,1)} %bitcast.15), calls=%async_computation | async-start | bytes 524288 | tf_op jit(solution)/shard_map/all_to_all | solution.py:500
  71.1 0.0 collective-permute-done.10.refs_3_
  71.1 0.0 copy-start.2
  71.1 0.0 collective-permute-done.11.refs_4_
  71.1 0.9 copy-done.2
  72.0 12.6 %shard_map.220 = (bf16[256,4096]{1,0:T(8,128)(2,1)}, bf16[256,4096]{1,0:T(8,128)(2,1)}, f32[32,4,4,128]{3,2,1,0:T(4,128)}) custom-call(s32[3]{0:T(128)} %pad_add_fusion.refs_0_, bf16[128,4096]{1,0:T(8,128)(2,1)} %get-tuple-element.73.refs_1_, bf16[128,4096]{1,0:T(8,128)(2,1)} %get-tuple-element.74.refs_2_, bf16[128,4096]{1,0:T(8,128)(2,1)} %copy-done.2, ...), custom_call_target="tpu_custom_call" | custom-call | flops 2000000000 | bytes 10000000 | tf_op jit(solution)/shard_map/pallas_call | solution.py:443
  84.6 5.3 %all-to-all-done.refs_1_ = bf16[128,8,128]{2,1,0:T(8,128)(2,1)S(1)} async-done(((bf16[128,8,128]{2,1,0:T(8,128)(2,1)}), bf16[128,8,128]{2,1,0:T(8,128)(2,1)S(1)}, u32[]{:S(2)}, u32[]{:S(2)}) %all-to-all-start) | async-done | bytes 262176 | tf_op jit(solution)/shard_map/all_to_all | solution.py:500
  89.9 0.7 copy-done.4
  90.6 2.6 %shard_map.221.refs_16_ = bf16[128,8,128]{2,1,0:T(8,128)(2,1)} custom-call(s32[3]{0:T(128)} %pad_add_fusion.refs_0_, bf16[128,8,128]{2,1,0:T(8,128)(2,1)} %copy-done.4, f32[4,384,128]{2,1,0:T(8,128)} %pad_maximum_fusion.refs_10_.refs_11_.refs_5_.refs_6_.refs_7_.refs_2_, f32[32,4,4,128]{3,2,1,0:T(4,128)} %get-tuple-element.75.refs_3_.refs_15_), custom_call_target="tpu_custom_call" | custom-call | flops 200000000 | bytes 1000000 | tf_op jit(solution)/shard_map/pallas_call | solution.py:443
  93.2 9.9 %all-to-all-start.1 = ((bf16[128,8,128]{2,1,0:T(8,128)(2,1)}), bf16[128,8,128]{2,1,0:T(8,128)(2,1)S(1)}, u32[]{:S(2)}, u32[]{:S(2)}) async-start(bf16[128,8,128]{2,1,0:T(8,128)(2,1)} %shard_map.221.refs_16_), calls=%async_computation.1 | async-start | bytes 524288 | tf_op jit(solution)/shard_map/all_to_all | solution.py:600
  103.1 0.0 collective-permute-done.8.refs_3_
  103.1 0.0 copy-start.1
  103.1 0.0 collective-permute-done.9.refs_4_
  103.1 0.9 copy-done.1
  104.1 1.0 copy-done.3
  105.1 12.6 %shard_map.222 = (bf16[256,4096]{1,0:T(8,128)(2,1)}, bf16[256,4096]{1,0:T(8,128)(2,1)}, f32[32,4,4,128]{3,2,1,0:T(4,128)}) custom-call(s32[3]{0:T(128)} %pad_add_fusion.refs_0_, bf16[128,4096]{1,0:T(8,128)(2,1)} %get-tuple-element.71.refs_1_, bf16[128,4096]{1,0:T(8,128)(2,1)} %get-tuple-element.72.refs_2_, ...), custom_call_target="tpu_custom_call", output_to_operand_aliasing={{2}: (15, {})} | custom-call | flops 2000000000 | bytes 10000000 | tf_op jit(solution)/shard_map/pallas_call | solution.py:443
  117.7 0.0 all-to-all-done.1.refs_7_.refs_8_
  117.7 0.0 copy-start
  117.7 9.8 %all-to-all-start.2 = ((f32[128,4,128]{2,1,0:T(4,128)}), f32[128,4,128]{2,1,0:T(4,128)S(1)}, u32[]{:S(2)}, u32[]{:S(2)}) async-start(f32[128,4,128]{2,1,0:T(4,128)} %bitcast.14), calls=%async_computation.2 | async-start | bytes 524288 | tf_op jit(solution)/shard_map/all_to_all | solution.py:612
  127.4 0.0 copy-done
  127.5 12.2 %shard_map.223 = (bf16[128,8192]{1,0:T(8,128)(2,1)}, bf16[128,8192]{1,0:T(8,128)(2,1)}, bf16[128,8192]{1,0:T(8,128)(2,1)}, bf16[128,8192]{1,0:T(8,128)(2,1)}, bf...) custom-call(s32[3]{0:T(128)} %pad_add_fusion.refs_0_, bf16[128,4096]{1,0:T(8,128)(2,1)} %get-tuple-element.79.refs_1_, ...), custom_call_target="tpu_custom_call" | custom-call | flops 2000000000 | bytes 10000000 | tf_op jit(solution)/shard_map/pallas_call | solution.py:443
  139.7 12.4 %shard_map.224 = (bf16[128,8192]{1,0:T(8,128)(2,1)}, bf16[128,8192]{1,0:T(8,128)(2,1)}, bf16[128,8192]{1,0:T(8,128)(2,1)}, bf16[128,8192]{1,0:T(8,128)(2,1)}, bf...) custom-call(s32[3]{0:T(128)} %pad_add_fusion.refs_0_, ...), custom_call_target="tpu_custom_call", output_to_operand_aliasing={{0}: (15, {}), {1}: (16, {}), {2}: (17, {}), {3}: (18, {})} | custom-call | flops 2000000000 | bytes 10000000 | tf_op jit(solution)/shard_map/pallas_call | solution.py:443
  152.1 4.8 %collective-permute-start.13 = (bf16[24,4096]{1,0:T(8,128)(2,1)}, bf16[24,4096]{1,0:T(8,128)(2,1)S(1)}, u32[]{:S(2)}, u32[]{:S(2)}) collective-permute-start(bf16[24,4096]{1,0:T(8,128)(2,1)} %get-tuple-element.93), channel_id=1, source_target_pairs={{1,0},{2,1},{3,2},{4,3},{5,4},{6,5},{7,6},{8,7},{9,8},{10,9},{11,1... | collective-permute-start | bytes 589832 | tf_op jit(solution)/shard_map/ppermute | solution.py:347
  156.9 2.7 %collective-permute-start.12 = (bf16[24,4096]{1,0:T(8,128)(2,1)S(1)}, bf16[24,4096]{1,0:T(8,128)(2,1)S(1)}, u32[]{:S(2)}, u32[]{:S(2)}) collective-permute-start(bf16[24,4096]{1,0:T(8,128)(2,1)S(1)} %copy-done.10), channel_id=1, source_target_pairs={{1,0},{2,1},{3,2},{4,3},{5,4},{6,5},{7,6},{8,7},{9,8},{10,9},{11,1... | collective-permute-start | bytes 589832 | tf_op jit(solution)/shard_map/ppermute | solution.py:347
  159.6 0.0 all-to-all-done.2
  159.6 0.1 reduce_sum.9
  159.8 14.6 %all_to_all.20 = f32[32,4,128]{2,1,0:T(4,128)S(1)} all-to-all(f32[32,4,128]{2,1,0:T(4,128)S(1)} %broadcast_in_dim.2), channel_id=1, replica_groups=mesh['ctx'=32,'own'=4] {'ctx'}, dimensions={0} | all-to-all | bytes 131072 | tf_op jit(solution)/shard_map/all_to_all | solution.py:617
  174.4 0.0 collective-permute-done.13.refs_4_
  174.4 0.0 collective-permute-done.12.refs_3_
  174.4 0.0 copy-start.9
  174.4 0.7 copy-done.8
  175.1 0.1 copy-done.9
  175.2 3.9 %shard_map.225 = (bf16[128,8192]{1,0:T(8,128)(2,1)}, bf16[128,8192]{1,0:T(8,128)(2,1)}, bf16[128,8192]{1,0:T(8,128)(2,1)}) custom-call(s32[3]{0:T(128)} %pad_add_fusion.refs_0_, f32[24,4096]{1,0:T(8,128)} %get-tuple-element.90.refs_1_, f32[24,4096]{1,0:T(8,128)} %get-tuple-element.91.refs_2_, ...), custom_call_target="tpu_custom_call", output_to_operand_aliasing={{0}: (7, {}), {1}: (8, {}), {2}: (9, {})} | custom-call | flops 200000000 | bytes 1000000 | tf_op jit(solution)/shard_map/pallas_call | solution.py:443
  179.1 0.6 copy.41
  (9 shorter events, 0.0 us)
Async XLA Ops:
  2.6 12.6 %collective-permute-start.2 = (f32[24,128]{1,0:T(8,128)}, f32[24,128]{1,0:T(8,128)S(1)}, u32[]{:S(2)}, u32[]{:S(2)}) collective-permute-start(f32[24,128]{1,0:T(8,128)} %get-tuple-element.54), channel_id=1, source_target_pairs={{0,3},{1,0},{2,1},{3,2},{4,7},{5,4},{6,5},{7,6},{8,11},{9,8},{10,9... | collective-permute-start | bytes 36872 | tf_op jit(solution)/shard_map/ppermute | solution.py:358
  6.1 9.1 %collective-permute-start.1 = (f32[24,128]{1,0:T(8,128)}, f32[24,128]{1,0:T(8,128)S(1)}, u32[]{:S(2)}, u32[]{:S(2)}) collective-permute-start(f32[24,128]{1,0:T(8,128)} %get-tuple-element.54), channel_id=1, source_target_pairs={{0,2},{1,3},{2,0},{3,1},{4,6},{5,7},{6,4},{7,5},{8,10},{9,11},{10,... | collective-permute-start | bytes 36872 | tf_op jit(solution)/shard_map/ppermute | solution.py:358
  6.5 9.4 %collective-permute-start = (f32[24,128]{1,0:T(8,128)}, f32[24,128]{1,0:T(8,128)S(1)}, u32[]{:S(2)}, u32[]{:S(2)}) collective-permute-start(f32[24,128]{1,0:T(8,128)} %get-tuple-element.54), channel_id=1, source_target_pairs={{0,1},{1,2},{2,3},{3,0},{4,5},{5,6},{6,7},{7,4},{8,9},{9,10},{10,1... | collective-permute-start | bytes 36872 | tf_op jit(solution)/shard_map/ppermute | solution.py:358
  7.2 14.1 %collective-permute-start.4 = (bf16[24,4096]{1,0:T(8,128)(2,1)}, bf16[24,4096]{1,0:T(8,128)(2,1)S(1)}, u32[]{:S(2)}, u32[]{:S(2)}) collective-permute-start(bf16[24,4096]{1,0:T(8,128)(2,1)} %get-tuple-element.56), channel_id=1, source_target_pairs={{0,1},{1,2},{2,3},{3,4},{4,5},{5,6},{6,7},{7,8},{8,9},{9,10},{10,1... | collective-permute-start | bytes 589832 | tf_op jit(solution)/shard_map/ppermute | solution.py:347
  10.7 21.9 %collective-permute-start.7 = (f32[384,128]{1,0:T(8,128)}, f32[384,128]{1,0:T(8,128)S(1)}, u32[]{:S(2)}, u32[]{:S(2)}) collective-permute-start(f32[384,128]{1,0:T(8,128)} %get-tuple-element.61), channel_id=1, source_target_pairs={{0,3},{1,0},{2,1},{3,2},{4,7},{5,4},{6,5},{7,6},{8,11},{9,8},{10,9... | collective-permute-start | bytes 589832 | tf_op jit(solution)/shard_map/ppermute | solution.py:358
  15.2 17.4 %collective-permute-start.6 = (f32[384,128]{1,0:T(8,128)}, f32[384,128]{1,0:T(8,128)S(1)}, u32[]{:S(2)}, u32[]{:S(2)}) collective-permute-start(f32[384,128]{1,0:T(8,128)} %get-tuple-element.61), channel_id=1, source_target_pairs={{0,2},{1,3},{2,0},{3,1},{4,6},{5,7},{6,4},{7,5},{8,10},{9,11},{10,... | collective-permute-start | bytes 589832 | tf_op jit(solution)/shard_map/ppermute | solution.py:358
  15.2 17.4 %collective-permute-start.5 = (f32[384,128]{1,0:T(8,128)}, f32[384,128]{1,0:T(8,128)S(1)}, u32[]{:S(2)}, u32[]{:S(2)}) collective-permute-start(f32[384,128]{1,0:T(8,128)} %get-tuple-element.61), channel_id=1, source_target_pairs={{0,1},{1,2},{2,3},{3,0},{4,5},{5,6},{6,7},{7,4},{8,9},{9,10},{10,1... | collective-permute-start | bytes 589832 | tf_op jit(solution)/shard_map/ppermute | solution.py:358
  17.2 22.2 %copy-start.5 = (f32[384,128]{1,0:T(8,128)S(1)}, f32[384,128]{1,0:T(8,128)}, u32[]{:S(2)}) copy-start(f32[384,128]{1,0:T(8,128)} %get-tuple-element.61) | copy-start | bytes 589828
  17.2 23.2 %collective-permute-start.3 = (bf16[24,4096]{1,0:T(8,128)(2,1)}, bf16[24,4096]{1,0:T(8,128)(2,1)S(1)}, u32[]{:S(2)}, u32[]{:S(2)}) collective-permute-start(bf16[24,4096]{1,0:T(8,128)(2,1)} %get-tuple-element.55), channel_id=1, source_target_pairs={{0,1},{1,2},{2,3},{3,4},{4,5},{5,6},{6,7},{7,8},{8,9},{9,10},{10,1... | collective-permute-start | bytes 589832 | tf_op jit(solution)/shard_map/ppermute | solution.py:347
  21.2 0.7 copy-start.6
  32.6 38.5 %collective-permute-start.10 = (bf16[128,4096]{1,0:T(8,128)(2,1)}, bf16[128,4096]{1,0:T(8,128)(2,1)S(1)}, u32[]{:S(2)}, u32[]{:S(2)}) collective-permute-start(bf16[128,4096]{1,0:T(8,128)(2,1)} %get-tuple-element.73.refs_1_), channel_id=1, source_target_pairs={{0,1},{1,2},{2,3},{3,4},{4,5},{5,6},{6,7},{7,8},{8,9},{9,10},{10,1... | collective-permute-start | bytes 3145736 | tf_op jit(solution)/shard_map/ppermute | solution.py:347
  34.5 36.5 %collective-permute-start.11 = (bf16[128,4096]{1,0:T(8,128)(2,1)}, bf16[128,4096]{1,0:T(8,128)(2,1)}, u32[]{:S(2)}, u32[]{:S(2)}) collective-permute-start(bf16[128,4096]{1,0:T(8,128)(2,1)} %get-tuple-element.74.refs_2_), channel_id=1, source_target_pairs={{1,0},{2,1},{3,2},{4,3},{5,4},{6,5},{7,6},{8,7},{9,8},{10,9},{11,1... | collective-permute-start | bytes 3145736 | tf_op jit(solution)/shard_map/ppermute | solution.py:347
  40.4 0.7 copy-start.7
  52.2 50.9 %collective-permute-start.8 = (bf16[128,4096]{1,0:T(8,128)(2,1)}, bf16[128,4096]{1,0:T(8,128)(2,1)S(1)}, u32[]{:S(2)}, u32[]{:S(2)}) collective-permute-start(bf16[128,4096]{1,0:T(8,128)(2,1)} %get-tuple-element.71.refs_1_), channel_id=1, source_target_pairs={{0,1},{1,2},{2,3},{3,4},{4,5},{5,6},{6,7},{7,8},{8,9},{9,10},{10,1... | collective-permute-start | bytes 3145736 | tf_op jit(solution)/shard_map/ppermute | solution.py:347
  54.2 48.9 %collective-permute-start.9 = (bf16[128,4096]{1,0:T(8,128)(2,1)}, bf16[128,4096]{1,0:T(8,128)(2,1)S(1)}, u32[]{:S(2)}, u32[]{:S(2)}) collective-permute-start(bf16[128,4096]{1,0:T(8,128)(2,1)} %get-tuple-element.72.refs_2_), channel_id=1, source_target_pairs={{1,0},{2,1},{3,2},{4,3},{5,4},{6,5},{7,6},{8,7},{9,8},{10,9},{11,1... | collective-permute-start | bytes 3145736 | tf_op jit(solution)/shard_map/ppermute | solution.py:347
  59.0 30.9 %all-to-all-start = ((bf16[128,8,128]{2,1,0:T(8,128)(2,1)}), bf16[128,8,128]{2,1,0:T(8,128)(2,1)S(1)}, u32[]{:S(2)}, u32[]{:S(2)}) async-start(bf16[128,8,128]{2,1,0:T(8,128)(2,1)} %bitcast.15), calls=%async_computation | async-start | bytes 524288 | tf_op jit(solution)/shard_map/all_to_all | solution.py:500
  71.1 1.0 copy-start.2
  89.9 0.7 copy-start.4
  93.2 24.4 %all-to-all-start.1 = ((bf16[128,8,128]{2,1,0:T(8,128)(2,1)}), bf16[128,8,128]{2,1,0:T(8,128)(2,1)S(1)}, u32[]{:S(2)}, u32[]{:S(2)}) async-start(bf16[128,8,128]{2,1,0:T(8,128)(2,1)} %shard_map.221.refs_16_), calls=%async_computation.1 | async-start | bytes 524288 | tf_op jit(solution)/shard_map/all_to_all | solution.py:600
  103.1 1.0 copy-start.1
  104.1 1.0 copy-start.3
  117.7 9.8 %copy-start = (bf16[128,8,128]{2,1,0:T(8,128)(2,1)}, bf16[128,8,128]{2,1,0:T(8,128)(2,1)S(1)}, u32[]{:S(2)}) copy-start(bf16[128,8,128]{2,1,0:T(8,128)(2,1)S(1)} %all-to-all-done.1.refs_7_.refs_8_) | copy-start | bytes 786436
  117.7 41.9 %all-to-all-start.2 = ((f32[128,4,128]{2,1,0:T(4,128)}), f32[128,4,128]{2,1,0:T(4,128)S(1)}, u32[]{:S(2)}, u32[]{:S(2)}) async-start(f32[128,4,128]{2,1,0:T(4,128)} %bitcast.14), calls=%async_computation.2 | async-start | bytes 524288 | tf_op jit(solution)/shard_map/all_to_all | solution.py:612
  139.7 17.2 %copy-start.10 = (bf16[24,4096]{1,0:T(8,128)(2,1)S(1)}, bf16[24,4096]{1,0:T(8,128)(2,1)}, u32[]{:S(2)}) copy-start(bf16[24,4096]{1,0:T(8,128)(2,1)} %get-tuple-element.92) | copy-start | bytes 589828
  152.1 22.4 %collective-permute-start.13 = (bf16[24,4096]{1,0:T(8,128)(2,1)}, bf16[24,4096]{1,0:T(8,128)(2,1)S(1)}, u32[]{:S(2)}, u32[]{:S(2)}) collective-permute-start(bf16[24,4096]{1,0:T(8,128)(2,1)} %get-tuple-element.93), channel_id=1, source_target_pairs={{1,0},{2,1},{3,2},{4,3},{5,4},{6,5},{7,6},{8,7},{9,8},{10,9},{11,1... | collective-permute-start | bytes 589832 | tf_op jit(solution)/shard_map/ppermute | solution.py:347
  156.9 17.5 %collective-permute-start.12 = (bf16[24,4096]{1,0:T(8,128)(2,1)S(1)}, bf16[24,4096]{1,0:T(8,128)(2,1)S(1)}, u32[]{:S(2)}, u32[]{:S(2)}) collective-permute-start(bf16[24,4096]{1,0:T(8,128)(2,1)S(1)} %copy-done.10), channel_id=1, source_target_pairs={{1,0},{2,1},{3,2},{4,3},{5,4},{6,5},{7,6},{8,7},{9,8},{10,9},{11,1... | collective-permute-start | bytes 589832 | tf_op jit(solution)/shard_map/ppermute | solution.py:347
  174.4 0.7 copy-start.8
  174.4 0.7 copy-start.9

commit v5 on v4

--- a/solution.py
+++ b/solution.py
@@ -283,8 +283,8 @@
     lg[...] = dot(t_inv[...], ys[...]) + dot(t_ahead[...], stack3(coef[0:16]))
     gp[...] = dot(t_inv[...], zs[...]) + dot(t_behind[...], stack3(coef[16:32]))
 
-    def rows_out(r, _):
-        here = pl.ds(pl.multiple_of(r * 16, 16), 16)
+    for base in range(0, rows, 16):
+        here = slice(base, base + 16)
         for lane in lanes:
             cols = slice(128 * lane, 128 * lane + 128)
             conv, grad = lg[here, cols], gp[here, cols]
@@ -292,9 +292,6 @@
             eq[lane, here] = (g[here, cols].astype(F32) * conv).astype(BF16).astype(F32)
             ek[lane, here] = (grad * vf[here, cols].astype(F32)).astype(BF16).astype(F32)
             ev[lane, here] = (grad * kf[here, cols].astype(F32)).astype(BF16).astype(F32)
-        return 0
-
-    lax.fori_loop(0, rows // 16, rows_out, 0)
     for at, src in enumerate((eq, ek, ev)):
         for lane in lanes:
             cols = slice(128 * lane, 128 * lane + 128)
@@ -318,27 +315,20 @@
     lax.fori_loop(0, rows // 32, finish, 0)
 
 
-def tail_kernel(me, *refs):
-    lasts, rims, taps = refs[:CHUNKS], refs[CHUNKS : 2 * CHUNKS], refs[2 * CHUNKS : 3 * CHUNKS]
-    gq, gk, gv, ext = refs[3 * CHUNKS + 3 :]
-    piece = pl.program_id(0) // (pl.num_programs(0) // CHUNKS)
+def tail_kernel(me, last, rim, tap, gq_in, gk_in, gv_in, gq, gk, gv, ext):
     ext[:, 0:8] = jnp.zeros((3, 8, 128), F32)
-    for chunk in range(CHUNKS):
-        last, rim, tap = lasts[chunk], rims[chunk], taps[chunk]
-
-        @pl.when(piece == chunk)
-        def _():
-            def tile(n, _):
-                cols = pl.ds(pl.multiple_of(n * 128, 128), 128)
-                for at, dst in enumerate((gq, gk, gv)):
-                    ext[at, 8:16] = rim[8 * at : 8 * at + 8, cols].astype(F32)
-                    total = last[8 * at : 8 * at + 8, cols]
-                    for j in range(1, 7):
-                        total = total + tap[7 * at + j : 7 * at + j + 1, cols] * ext[at, j : 8 + j]
-                    dst[:, cols] = total.astype(BF16)
-                return 0
-
-            lax.fori_loop(0, last.shape[1] // 128, tile, 0, unroll=4)
+
+    def tile(n, _):
+        cols = pl.ds(pl.multiple_of(n * 128, 128), 128)
+        for at, dst in enumerate((gq, gk, gv)):
+            ext[at, 8:16] = rim[8 * at : 8 * at + 8, cols].astype(F32)
+            total = last[8 * at : 8 * at + 8, cols]
+            for j in range(1, 7):
+                total = total + tap[7 * at + j : 7 * at + j + 1, cols] * ext[at, j : 8 + j]
+            dst[:, cols] = total.astype(BF16)
+        return 0
+
+    lax.fori_loop(0, last.shape[1] // 128, tile, 0, unroll=4)
 
 
 def shift(value, steps):
@@ -618,26 +608,20 @@
         jnp.broadcast_to(total[None], (ctxs, share, 128)), "ctx", 0, 0, tiled=True
     )
 
-    cuts = 1
-    strip = pl.BlockSpec((8, per // cuts), lambda i, m: (rows // 8 - 1, i))
-    bands = [
-        pl.BlockSpec(
-            (24, per // cuts),
-            lambda i, m, chunk=chunk: (0, jnp.clip(i - cuts * chunk, 0, cuts - 1)),
-        )
-        for chunk in range(CHUNKS)
-    ]
-    anyspec = pl.BlockSpec(memory_space=pl.ANY)
-    grads = call(
-        tail_kernel, 200_000_000, (CHUNKS * cuts,),
-        bands * 3 + [anyspec] * 3,
-        (*lasts, *edges, *[f[6] for f in fronts], *outs[1:4]),
-        (full,) * 3,
-        (strip,) * 3,
-        [pltpu.VMEM((3, 16, 128), F32)],
-        {3 * CHUNKS + 1: 0, 3 * CHUNKS + 2: 1, 3 * CHUNKS + 3: 2},
-    )
-    return (outs[0],) + tuple(grads) + (every.reshape(rows, 128),)
+    every = every.reshape(rows, 128)
+    grads = outs[1:4]
+    for chunk in range(CHUNKS):
+        grads = call(
+            tail_kernel, 200_000_000, (1,),
+            [whole((24, per))] * 3 + [pl.BlockSpec(memory_space=pl.ANY)] * 3,
+            (lasts[chunk], edges[chunk], fronts[chunk][6], *grads),
+            (full,) * 3,
+            (pl.BlockSpec((8, per), lambda i, m, chunk=chunk: (rows // 8 - 1, chunk)),) * 3,
+            [pltpu.VMEM((3, 16, 128), F32)],
+            {4: 0, 5: 1, 6: 2},
+            [every] if chunk == CHUNKS - 1 else [],
+        )
+    return (outs[0],) + tuple(grads) + (every,)
 
 
 def solution(mesh):

time: 181 us -> 183 us (1.011)
    pallas_call x8 -> x9, Pallas kernels: 78.1 us -> 79.1 us  [call(): pl.pallas_call(body, out_shape=out_shape, grid_spec=pltpu.PrefetchScalarG...]
    unnamed x23 -> x25, local copies, waits for them, and re-layouts: 6.31 us -> 6.92 us
  transfers between devices with their start and end apart: 17 -> 17, of which waited for: 1 -> 1; matrix products, arithmetic and copies ran while one was open for 2% -> 2% of each run, Pallas kernels for 41% -> 42%
where the time goes in v5:
time: 183 us; the launch traced here: 181 us
  Pallas kernels  81 us (44%)
  starting transfers between devices  69.4 us (38%)
  blocking collectives  14.7 us (8%)
  local copies, waits for them, and re-layouts  6.93 us (4%)
  waiting for transfers between devices  5.33 us (3%)
  other arithmetic  3.08 us (2%)
    pallas_call x9, Pallas kernels, call(): pl.pallas_call(body, out_shape=out_shape, grid_spec=pltpu.PrefetchScalarG...  79.1 us
    ppermute x8, starting transfers between devices, shift(): lax.ppermute(value, AXES, [(at, at + steps) for at in range(first, last)])  28.6 us
    all_to_all x1, blocking collectives, shards(): lax.all_to_all(jnp.broadcast_to(total[None], (ctxs, share, 128)), 'ctx',...  14.7 us
    all_to_all x1, starting transfers between devices, shards(): arrived = lax.all_to_all(states, AXES, 0, 0, tiled=True)  12 us
    all_to_all x1, starting transfers between devices, shards(): carried = lax.all_to_all(scanned, AXES, 0, 0, tiled=True)  9.86 us
    all_to_all x1, starting transfers between devices, shards(): lax.all_to_all(mids[-1][2].reshape(ctxs * owners, share, 128), AXES, 0, 0...  9.76 us
    ppermute x6, starting transfers between devices, ring_own(): lax.ppermute(value, 'own', [(at, (at + hop) % count) for at in range(coun...  9.1 us
    unnamed x25, local copies, waits for them, and re-layouts  6.92 us
  transfers between devices with their start and end apart: 17, of which 1 were waited for; matrix products, arithmetic and copies ran while one was open for 2% of the time, Pallas kernels for 42%

profile of v5, /device:TPU:1, one launch (start us, length us, event | category | flops | bytes accessed | tf_op | source)
XLA Modules:
  0.0 181.4 jit_solution(10341024977522270726)
XLA Ops:
  0.6 1.9 %pack.1 = (f32[24,128]{1,0:T(8,128)}, f32[384,128]{1,0:T(8,128)}, bf16[24,4096]{1,0:T(8,128)(2,1)}, bf16[24,4096]{1,0:T(8,128)(2,1)}) custom-call(bf16[128,8192]{1,0:T(8,128)(2,1)} %refs_1_.3, bf16[128,8192]{1,0:T(8,128)(2,1)} %refs_2_.3, bf16[128,8192]{1,0:T(8,128)(2,1)} %refs_3_.3, f32[3,7,128]{2,1,0:T(8,128)} %short.1, f32[8,2048]{1,0:T(8,128)} %rate.1, ...), custom_call_target="tpu_custom_call" | custom-call | tf_op jit(solution)/shard_map/pack/pallas_call | solution.py:373
  2.6 3.6 %collective-permute-start.2 = (f32[24,128]{1,0:T(8,128)}, f32[24,128]{1,0:T(8,128)S(1)}, u32[]{:S(2)}, u32[]{:S(2)}) collective-permute-start(f32[24,128]{1,0:T(8,128)} %get-tuple-element.57), channel_id=1, source_target_pairs={{0,3},{1,0},{2,1},{3,2},{4,7},{5,4},{6,5},{7,6},{8,11},{9,8},{10,9... | collective-permute-start | bytes 36872 | tf_op jit(solution)/shard_map/ppermute | solution.py:348
  6.1 0.3 collective-permute-start.1
  6.5 0.7 collective-permute-start
  7.2 3.5 %collective-permute-start.4 = (bf16[24,4096]{1,0:T(8,128)(2,1)}, bf16[24,4096]{1,0:T(8,128)(2,1)S(1)}, u32[]{:S(2)}, u32[]{:S(2)}) collective-permute-start(bf16[24,4096]{1,0:T(8,128)(2,1)} %get-tuple-element.59), channel_id=1, source_target_pairs={{0,1},{1,2},{2,3},{3,4},{4,5},{5,6},{6,7},{7,8},{8,9},{9,10},{10,1... | collective-permute-start | bytes 589832 | tf_op jit(solution)/shard_map/ppermute | solution.py:337
  10.7 3.9 %collective-permute-start.7 = (f32[384,128]{1,0:T(8,128)}, f32[384,128]{1,0:T(8,128)S(1)}, u32[]{:S(2)}, u32[]{:S(2)}) collective-permute-start(f32[384,128]{1,0:T(8,128)} %get-tuple-element.64), channel_id=1, source_target_pairs={{0,3},{1,0},{2,1},{3,2},{4,7},{5,4},{6,5},{7,6},{8,11},{9,8},{10,9... | collective-permute-start | bytes 589832 | tf_op jit(solution)/shard_map/ppermute | solution.py:348
  14.6 0.6 pad_add_fusion.refs_0_
  15.2 0.0 collective-permute-done.2
  15.2 0.0 collective-permute-start.6
  15.2 0.0 collective-permute-done.1
  15.2 0.6 collective-permute-start.5
  15.8 0.0 collective-permute-done
  15.8 1.3 pad_maximum_fusion.1.refs_6_
  17.2 4.1 %collective-permute-start.3 = (bf16[24,4096]{1,0:T(8,128)(2,1)}, bf16[24,4096]{1,0:T(8,128)(2,1)S(1)}, u32[]{:S(2)}, u32[]{:S(2)}) collective-permute-start(bf16[24,4096]{1,0:T(8,128)(2,1)} %get-tuple-element.58), channel_id=1, source_target_pairs={{0,1},{1,2},{2,3},{3,4},{4,5},{5,6},{6,7},{7,8},{8,9},{9,10},{10,1... | collective-permute-start | bytes 589832 | tf_op jit(solution)/shard_map/ppermute | solution.py:337
  21.2 0.0 collective-permute-done.4.refs_5_
  21.2 0.0 copy-start.7
  21.3 0.7 copy-done.7
  21.9 10.7 %shard_map.218 = (bf16[128,4096]{1,0:T(8,128)(2,1)}, bf16[128,4096]{1,0:T(8,128)(2,1)}, bf16[128,4096]{1,0:T(8,128)(2,1)}, bf16[128,4096]{1,0:T(8,128)(2,1)}, bf...) custom-call(s32[3]{0:T(128)} %pad_add_fusion.refs_0_, bf16[128,8192]{1,0:T(8,128)(2,1)} %refs_1_.3, ...), custom_call_target="tpu_custom_call" | custom-call | flops 2000000000 | bytes 10000000 | tf_op jit(solution)/shard_map/pallas_call | solution.py:433
  32.6 0.0 collective-permute-done.7
  32.6 0.0 collective-permute-done.6
  32.6 0.0 collective-permute-done.5
  32.6 1.9 %collective-permute-start.10 = (bf16[128,4096]{1,0:T(8,128)(2,1)}, bf16[128,4096]{1,0:T(8,128)(2,1)S(1)}, u32[]{:S(2)}, u32[]{:S(2)}) collective-permute-start(bf16[128,4096]{1,0:T(8,128)(2,1)} %get-tuple-element.76.refs_1_), channel_id=1, source_target_pairs={{0,1},{1,2},{2,3},{3,4},{4,5},{5,6},{6,7},{7,8},{8,9},{9,10},{10,1... | collective-permute-start | bytes 3145736 | tf_op jit(solution)/shard_map/ppermute | solution.py:337
  34.5 4.9 %collective-permute-start.11 = (bf16[128,4096]{1,0:T(8,128)(2,1)}, bf16[128,4096]{1,0:T(8,128)(2,1)}, u32[]{:S(2)}, u32[]{:S(2)}) collective-permute-start(bf16[128,4096]{1,0:T(8,128)(2,1)} %get-tuple-element.77.refs_2_), channel_id=1, source_target_pairs={{1,0},{2,1},{3,2},{4,3},{5,4},{6,5},{7,6},{8,7},{9,8},{10,9},{11,1... | collective-permute-start | bytes 3145736 | tf_op jit(solution)/shard_map/ppermute | solution.py:337
  39.4 0.0 copy-done.6
  39.4 1.0 pad_maximum_fusion.refs_10_.refs_11_.refs_5_.refs_6_.refs_7_.refs_2_
  40.4 0.0 collective-permute-done.3.refs_5_
  40.4 0.7 copy-done.8
  41.1 11.2 %shard_map.219 = (bf16[128,4096]{1,0:T(8,128)(2,1)}, bf16[128,4096]{1,0:T(8,128)(2,1)}, bf16[128,4096]{1,0:T(8,128)(2,1)}, bf16[128,4096]{1,0:T(8,128)(2,1)}, bf...) custom-call(s32[3]{0:T(128)} %pad_add_fusion.refs_0_, ...), custom_call_target="tpu_custom_call" | custom-call | flops 2000000000 | bytes 10000000 | tf_op jit(solution)/shard_map/pallas_call | solution.py:433
  52.2 1.9 %collective-permute-start.8 = (bf16[128,4096]{1,0:T(8,128)(2,1)}, bf16[128,4096]{1,0:T(8,128)(2,1)S(1)}, u32[]{:S(2)}, u32[]{:S(2)}) collective-permute-start(bf16[128,4096]{1,0:T(8,128)(2,1)} %get-tuple-element.74.refs_1_), channel_id=1, source_target_pairs={{0,1},{1,2},{2,3},{3,4},{4,5},{5,6},{6,7},{7,8},{8,9},{9,10},{10,1... | collective-permute-start | bytes 3145736 | tf_op jit(solution)/shard_map/ppermute | solution.py:337
  54.2 4.9 %collective-permute-start.9 = (bf16[128,4096]{1,0:T(8,128)(2,1)}, bf16[128,4096]{1,0:T(8,128)(2,1)S(1)}, u32[]{:S(2)}, u32[]{:S(2)}) collective-permute-start(bf16[128,4096]{1,0:T(8,128)(2,1)} %get-tuple-element.75.refs_2_), channel_id=1, source_target_pairs={{1,0},{2,1},{3,2},{4,3},{5,4},{6,5},{7,6},{8,7},{9,8},{10,9},{11,1... | collective-permute-start | bytes 3145736 | tf_op jit(solution)/shard_map/ppermute | solution.py:337
  59.0 12.0 %all-to-all-start = ((bf16[128,8,128]{2,1,0:T(8,128)(2,1)}), bf16[128,8,128]{2,1,0:T(8,128)(2,1)S(1)}, u32[]{:S(2)}, u32[]{:S(2)}) async-start(bf16[128,8,128]{2,1,0:T(8,128)(2,1)} %bitcast.17), calls=%async_computation | async-start | bytes 524288 | tf_op jit(solution)/shard_map/all_to_all | solution.py:490
  71.0 0.0 collective-permute-done.10.refs_3_
  71.1 0.0 copy-start.2
  71.1 0.0 collective-permute-done.11.refs_4_
  71.1 1.0 copy-done.2
  72.0 12.6 %shard_map.220 = (bf16[256,4096]{1,0:T(8,128)(2,1)}, bf16[256,4096]{1,0:T(8,128)(2,1)}, f32[32,4,4,128]{3,2,1,0:T(4,128)}) custom-call(s32[3]{0:T(128)} %pad_add_fusion.refs_0_, bf16[128,4096]{1,0:T(8,128)(2,1)} %get-tuple-element.76.refs_1_, bf16[128,4096]{1,0:T(8,128)(2,1)} %get-tuple-element.77.refs_2_, bf16[128,4096]{1,0:T(8,128)(2,1)} %copy-done.2, ...), custom_call_target="tpu_custom_call" | custom-call | flops 2000000000 | bytes 10000000 | tf_op jit(solution)/shard_map/pallas_call | solution.py:433
  84.6 5.3 %all-to-all-done.refs_1_ = bf16[128,8,128]{2,1,0:T(8,128)(2,1)S(1)} async-done(((bf16[128,8,128]{2,1,0:T(8,128)(2,1)}), bf16[128,8,128]{2,1,0:T(8,128)(2,1)S(1)}, u32[]{:S(2)}, u32[]{:S(2)}) %all-to-all-start) | async-done | bytes 262176 | tf_op jit(solution)/shard_map/all_to_all | solution.py:490
  89.9 0.7 copy-done.4
  90.6 2.6 %shard_map.221.refs_16_ = bf16[128,8,128]{2,1,0:T(8,128)(2,1)} custom-call(s32[3]{0:T(128)} %pad_add_fusion.refs_0_, bf16[128,8,128]{2,1,0:T(8,128)(2,1)} %copy-done.4, f32[4,384,128]{2,1,0:T(8,128)} %pad_maximum_fusion.refs_10_.refs_11_.refs_5_.refs_6_.refs_7_.refs_2_, f32[32,4,4,128]{3,2,1,0:T(4,128)} %get-tuple-element.78.refs_3_.refs_15_), custom_call_target="tpu_custom_call" | custom-call | flops 200000000 | bytes 1000000 | tf_op jit(solution)/shard_map/pallas_call | solution.py:433
  93.2 9.9 %all-to-all-start.1 = ((bf16[128,8,128]{2,1,0:T(8,128)(2,1)}), bf16[128,8,128]{2,1,0:T(8,128)(2,1)S(1)}, u32[]{:S(2)}, u32[]{:S(2)}) async-start(bf16[128,8,128]{2,1,0:T(8,128)(2,1)} %shard_map.221.refs_16_), calls=%async_computation.1 | async-start | bytes 524288 | tf_op jit(solution)/shard_map/all_to_all | solution.py:590
  103.1 0.0 collective-permute-done.8.refs_3_
  103.1 0.0 copy-start.1
  103.1 0.0 collective-permute-done.9.refs_4_
  103.1 0.9 copy-done.1
  104.1 1.0 copy-done.3
  105.1 12.6 %shard_map.222 = (bf16[256,4096]{1,0:T(8,128)(2,1)}, bf16[256,4096]{1,0:T(8,128)(2,1)}, f32[32,4,4,128]{3,2,1,0:T(4,128)}) custom-call(s32[3]{0:T(128)} %pad_add_fusion.refs_0_, bf16[128,4096]{1,0:T(8,128)(2,1)} %get-tuple-element.74.refs_1_, bf16[128,4096]{1,0:T(8,128)(2,1)} %get-tuple-element.75.refs_2_, ...), custom_call_target="tpu_custom_call", output_to_operand_aliasing={{2}: (15, {})} | custom-call | flops 2000000000 | bytes 10000000 | tf_op jit(solution)/shard_map/pallas_call | solution.py:433
  117.7 0.0 all-to-all-done.1.refs_7_.refs_8_
  117.7 9.8 %all-to-all-start.2 = ((f32[128,4,128]{2,1,0:T(4,128)}), f32[128,4,128]{2,1,0:T(4,128)S(1)}, u32[]{:S(2)}, u32[]{:S(2)}) async-start(f32[128,4,128]{2,1,0:T(4,128)} %bitcast.14), calls=%async_computation.2 | async-start | bytes 524288 | tf_op jit(solution)/shard_map/all_to_all | solution.py:602
  127.5 0.0 copy-done
  127.5 11.5 %shard_map.223 = (bf16[128,8192]{1,0:T(8,128)(2,1)}, bf16[128,8192]{1,0:T(8,128)(2,1)}, bf16[128,8192]{1,0:T(8,128)(2,1)}, bf16[128,8192]{1,0:T(8,128)(2,1)}, bf...) custom-call(s32[3]{0:T(128)} %pad_add_fusion.refs_0_, bf16[128,4096]{1,0:T(8,128)(2,1)} %get-tuple-element.82.refs_1_, ...), custom_call_target="tpu_custom_call" | custom-call | flops 2000000000 | bytes 10000000 | tf_op jit(solution)/shard_map/pallas_call | solution.py:433
  139.0 11.7 %shard_map.224 = (bf16[128,8192]{1,0:T(8,128)(2,1)}, bf16[128,8192]{1,0:T(8,128)(2,1)}, bf16[128,8192]{1,0:T(8,128)(2,1)}, bf16[128,8192]{1,0:T(8,128)(2,1)}, bf...) custom-call(s32[3]{0:T(128)} %pad_add_fusion.refs_0_, ...), custom_call_target="tpu_custom_call", output_to_operand_aliasing={{0}: (15, {}), {1}: (16, {}), {2}: (17, {}), {3}: (18, {})} | custom-call | flops 2000000000 | bytes 10000000 | tf_op jit(solution)/shard_map/pallas_call | solution.py:433
  150.7 4.8 %collective-permute-start.12 = (bf16[24,4096]{1,0:T(8,128)(2,1)}, bf16[24,4096]{1,0:T(8,128)(2,1)S(1)}, u32[]{:S(2)}, u32[]{:S(2)}) collective-permute-start(bf16[24,4096]{1,0:T(8,128)(2,1)} %get-tuple-element.94), channel_id=1, source_target_pairs={{1,0},{2,1},{3,2},{4,3},{5,4},{6,5},{7,6},{8,7},{9,8},{10,9},{11,1... | collective-permute-start | bytes 589832 | tf_op jit(solution)/shard_map/ppermute | solution.py:337
  155.5 2.7 %collective-permute-start.13 = (bf16[24,4096]{1,0:T(8,128)(2,1)S(1)}, bf16[24,4096]{1,0:T(8,128)(2,1)S(1)}, u32[]{:S(2)}, u32[]{:S(2)}) collective-permute-start(bf16[24,4096]{1,0:T(8,128)(2,1)S(1)} %copy-done.11), channel_id=1, source_target_pairs={{1,0},{2,1},{3,2},{4,3},{5,4},{6,5},{7,6},{8,7},{9,8},{10,9},{11,1... | collective-permute-start | bytes 589832 | tf_op jit(solution)/shard_map/ppermute | solution.py:337
  158.3 0.0 all-to-all-done.2
  158.3 0.1 reduce_sum.9
  158.4 14.7 %all_to_all.20 = f32[32,4,128]{2,1,0:T(4,128)} all-to-all(f32[32,4,128]{2,1,0:T(4,128)S(1)} %broadcast_in_dim.2), channel_id=1, replica_groups=mesh['ctx'=32,'own'=4] {'ctx'}, dimensions={0} | all-to-all | bytes 131072 | tf_op jit(solution)/shard_map/all_to_all | solution.py:607
  173.2 0.0 collective-permute-done.13.refs_2_
  173.2 0.7 copy-done.9
  173.9 3.0 %shard_map.225 = (bf16[128,8192]{1,0:T(8,128)(2,1)}, bf16[128,8192]{1,0:T(8,128)(2,1)}, bf16[128,8192]{1,0:T(8,128)(2,1)}) custom-call(s32[3]{0:T(128)} %pad_add_fusion.refs_0_, f32[24,4096]{1,0:T(8,128)} %get-tuple-element.95.refs_1_, bf16[24,4096]{1,0:T(8,128)(2,1)} %copy-done.9, ...), custom_call_target="tpu_custom_call", output_to_operand_aliasing={{0}: (4, {}), {1}: (5, {}), {2}: (6, {})} | custom-call | flops 200000000 | bytes 1000000 | tf_op jit(solution)/shard_map/pallas_call | solution.py:433
  176.9 0.0 collective-permute-done.12.refs_2_
  176.9 0.7 copy-done.10
  177.6 3.2 %shard_map.226 = (bf16[128,8192]{1,0:T(8,128)(2,1)}, bf16[128,8192]{1,0:T(8,128)(2,1)}, bf16[128,8192]{1,0:T(8,128)(2,1)}) custom-call(s32[3]{0:T(128)} %pad_add_fusion.refs_0_, f32[24,4096]{1,0:T(8,128)} %get-tuple-element.93.refs_1_, bf16[24,4096]{1,0:T(8,128)(2,1)} %copy-done.10, ...), custom_call_target="tpu_custom_call", output_to_operand_aliasing={{0}: (4, {}), {1}: (5, {}), {2}: (6, {})} | custom-call | flops 200000000 | bytes 1000000 | tf_op jit(solution)/shard_map/pallas_call | solution.py:433
  180.7 0.0 copy-done.5
  180.7 0.6 copy.47
  (12 shorter events, 0.0 us)
Async XLA Ops:
  2.6 12.6 %collective-permute-start.2 = (f32[24,128]{1,0:T(8,128)}, f32[24,128]{1,0:T(8,128)S(1)}, u32[]{:S(2)}, u32[]{:S(2)}) collective-permute-start(f32[24,128]{1,0:T(8,128)} %get-tuple-element.57), channel_id=1, source_target_pairs={{0,3},{1,0},{2,1},{3,2},{4,7},{5,4},{6,5},{7,6},{8,11},{9,8},{10,9... | collective-permute-start | bytes 36872 | tf_op jit(solution)/shard_map/ppermute | solution.py:348
  6.1 9.1 %collective-permute-start.1 = (f32[24,128]{1,0:T(8,128)}, f32[24,128]{1,0:T(8,128)S(1)}, u32[]{:S(2)}, u32[]{:S(2)}) collective-permute-start(f32[24,128]{1,0:T(8,128)} %get-tuple-element.57), channel_id=1, source_target_pairs={{0,2},{1,3},{2,0},{3,1},{4,6},{5,7},{6,4},{7,5},{8,10},{9,11},{10,... | collective-permute-start | bytes 36872 | tf_op jit(solution)/shard_map/ppermute | solution.py:348
  6.5 9.4 %collective-permute-start = (f32[24,128]{1,0:T(8,128)}, f32[24,128]{1,0:T(8,128)S(1)}, u32[]{:S(2)}, u32[]{:S(2)}) collective-permute-start(f32[24,128]{1,0:T(8,128)} %get-tuple-element.57), channel_id=1, source_target_pairs={{0,1},{1,2},{2,3},{3,0},{4,5},{5,6},{6,7},{7,4},{8,9},{9,10},{10,1... | collective-permute-start | bytes 36872 | tf_op jit(solution)/shard_map/ppermute | solution.py:348
  7.2 14.1 %collective-permute-start.4 = (bf16[24,4096]{1,0:T(8,128)(2,1)}, bf16[24,4096]{1,0:T(8,128)(2,1)S(1)}, u32[]{:S(2)}, u32[]{:S(2)}) collective-permute-start(bf16[24,4096]{1,0:T(8,128)(2,1)} %get-tuple-element.59), channel_id=1, source_target_pairs={{0,1},{1,2},{2,3},{3,4},{4,5},{5,6},{6,7},{7,8},{8,9},{9,10},{10,1... | collective-permute-start | bytes 589832 | tf_op jit(solution)/shard_map/ppermute | solution.py:337
  10.7 21.9 %collective-permute-start.7 = (f32[384,128]{1,0:T(8,128)}, f32[384,128]{1,0:T(8,128)S(1)}, u32[]{:S(2)}, u32[]{:S(2)}) collective-permute-start(f32[384,128]{1,0:T(8,128)} %get-tuple-element.64), channel_id=1, source_target_pairs={{0,3},{1,0},{2,1},{3,2},{4,7},{5,4},{6,5},{7,6},{8,11},{9,8},{10,9... | collective-permute-start | bytes 589832 | tf_op jit(solution)/shard_map/ppermute | solution.py:348
  15.2 17.4 %collective-permute-start.6 = (f32[384,128]{1,0:T(8,128)}, f32[384,128]{1,0:T(8,128)S(1)}, u32[]{:S(2)}, u32[]{:S(2)}) collective-permute-start(f32[384,128]{1,0:T(8,128)} %get-tuple-element.64), channel_id=1, source_target_pairs={{0,2},{1,3},{2,0},{3,1},{4,6},{5,7},{6,4},{7,5},{8,10},{9,11},{10,... | collective-permute-start | bytes 589832 | tf_op jit(solution)/shard_map/ppermute | solution.py:348
  15.2 17.4 %collective-permute-start.5 = (f32[384,128]{1,0:T(8,128)}, f32[384,128]{1,0:T(8,128)S(1)}, u32[]{:S(2)}, u32[]{:S(2)}) collective-permute-start(f32[384,128]{1,0:T(8,128)} %get-tuple-element.64), channel_id=1, source_target_pairs={{0,1},{1,2},{2,3},{3,0},{4,5},{5,6},{6,7},{7,4},{8,9},{9,10},{10,1... | collective-permute-start | bytes 589832 | tf_op jit(solution)/shard_map/ppermute | solution.py:348
  17.2 22.2 %copy-start.6 = (f32[384,128]{1,0:T(8,128)S(1)}, f32[384,128]{1,0:T(8,128)}, u32[]{:S(2)}) copy-start(f32[384,128]{1,0:T(8,128)} %get-tuple-element.64) | copy-start | bytes 589828
  17.2 23.2 %collective-permute-start.3 = (bf16[24,4096]{1,0:T(8,128)(2,1)}, bf16[24,4096]{1,0:T(8,128)(2,1)S(1)}, u32[]{:S(2)}, u32[]{:S(2)}) collective-permute-start(bf16[24,4096]{1,0:T(8,128)(2,1)} %get-tuple-element.58), channel_id=1, source_target_pairs={{0,1},{1,2},{2,3},{3,4},{4,5},{5,6},{6,7},{7,8},{8,9},{9,10},{10,1... | collective-permute-start | bytes 589832 | tf_op jit(solution)/shard_map/ppermute | solution.py:337
  21.2 0.7 copy-start.7
  32.6 38.4 %collective-permute-start.10 = (bf16[128,4096]{1,0:T(8,128)(2,1)}, bf16[128,4096]{1,0:T(8,128)(2,1)S(1)}, u32[]{:S(2)}, u32[]{:S(2)}) collective-permute-start(bf16[128,4096]{1,0:T(8,128)(2,1)} %get-tuple-element.76.refs_1_), channel_id=1, source_target_pairs={{0,1},{1,2},{2,3},{3,4},{4,5},{5,6},{6,7},{7,8},{8,9},{9,10},{10,1... | collective-permute-start | bytes 3145736 | tf_op jit(solution)/shard_map/ppermute | solution.py:337
  34.5 36.5 %collective-permute-start.11 = (bf16[128,4096]{1,0:T(8,128)(2,1)}, bf16[128,4096]{1,0:T(8,128)(2,1)}, u32[]{:S(2)}, u32[]{:S(2)}) collective-permute-start(bf16[128,4096]{1,0:T(8,128)(2,1)} %get-tuple-element.77.refs_2_), channel_id=1, source_target_pairs={{1,0},{2,1},{3,2},{4,3},{5,4},{6,5},{7,6},{8,7},{9,8},{10,9},{11,1... | collective-permute-start | bytes 3145736 | tf_op jit(solution)/shard_map/ppermute | solution.py:337
  40.4 0.7 copy-start.8
  52.2 50.9 %collective-permute-start.8 = (bf16[128,4096]{1,0:T(8,128)(2,1)}, bf16[128,4096]{1,0:T(8,128)(2,1)S(1)}, u32[]{:S(2)}, u32[]{:S(2)}) collective-permute-start(bf16[128,4096]{1,0:T(8,128)(2,1)} %get-tuple-element.74.refs_1_), channel_id=1, source_target_pairs={{0,1},{1,2},{2,3},{3,4},{4,5},{5,6},{6,7},{7,8},{8,9},{9,10},{10,1... | collective-permute-start | bytes 3145736 | tf_op jit(solution)/shard_map/ppermute | solution.py:337
  54.2 49.0 %collective-permute-start.9 = (bf16[128,4096]{1,0:T(8,128)(2,1)}, bf16[128,4096]{1,0:T(8,128)(2,1)S(1)}, u32[]{:S(2)}, u32[]{:S(2)}) collective-permute-start(bf16[128,4096]{1,0:T(8,128)(2,1)} %get-tuple-element.75.refs_2_), channel_id=1, source_target_pairs={{1,0},{2,1},{3,2},{4,3},{5,4},{6,5},{7,6},{8,7},{9,8},{10,9},{11,1... | collective-permute-start | bytes 3145736 | tf_op jit(solution)/shard_map/ppermute | solution.py:337
  59.0 30.9 %all-to-all-start = ((bf16[128,8,128]{2,1,0:T(8,128)(2,1)}), bf16[128,8,128]{2,1,0:T(8,128)(2,1)S(1)}, u32[]{:S(2)}, u32[]{:S(2)}) async-start(bf16[128,8,128]{2,1,0:T(8,128)(2,1)} %bitcast.17), calls=%async_computation | async-start | bytes 524288 | tf_op jit(solution)/shard_map/all_to_all | solution.py:490
  71.1 1.0 copy-start.2
  89.9 0.7 copy-start.4
  93.2 24.4 %all-to-all-start.1 = ((bf16[128,8,128]{2,1,0:T(8,128)(2,1)}), bf16[128,8,128]{2,1,0:T(8,128)(2,1)S(1)}, u32[]{:S(2)}, u32[]{:S(2)}) async-start(bf16[128,8,128]{2,1,0:T(8,128)(2,1)} %shard_map.221.refs_16_), calls=%async_computation.1 | async-start | bytes 524288 | tf_op jit(solution)/shard_map/all_to_all | solution.py:590
  103.1 1.0 copy-start.1
  104.1 1.0 copy-start.3
  117.7 9.8 %copy-start = (bf16[128,8,128]{2,1,0:T(8,128)(2,1)}, bf16[128,8,128]{2,1,0:T(8,128)(2,1)S(1)}, u32[]{:S(2)}) copy-start(bf16[128,8,128]{2,1,0:T(8,128)(2,1)S(1)} %all-to-all-done.1.refs_7_.refs_8_) | copy-start | bytes 786436
  117.7 40.6 %all-to-all-start.2 = ((f32[128,4,128]{2,1,0:T(4,128)}), f32[128,4,128]{2,1,0:T(4,128)S(1)}, u32[]{:S(2)}, u32[]{:S(2)}) async-start(f32[128,4,128]{2,1,0:T(4,128)} %bitcast.14), calls=%async_computation.2 | async-start | bytes 524288 | tf_op jit(solution)/shard_map/all_to_all | solution.py:602
  139.0 16.5 %copy-start.11 = (bf16[24,4096]{1,0:T(8,128)(2,1)S(1)}, bf16[24,4096]{1,0:T(8,128)(2,1)}, u32[]{:S(2)}) copy-start(bf16[24,4096]{1,0:T(8,128)(2,1)} %get-tuple-element.96) | copy-start | bytes 589828
  150.7 26.2 %collective-permute-start.12 = (bf16[24,4096]{1,0:T(8,128)(2,1)}, bf16[24,4096]{1,0:T(8,128)(2,1)S(1)}, u32[]{:S(2)}, u32[]{:S(2)}) collective-permute-start(bf16[24,4096]{1,0:T(8,128)(2,1)} %get-tuple-element.94), channel_id=1, source_target_pairs={{1,0},{2,1},{3,2},{4,3},{5,4},{6,5},{7,6},{8,7},{9,8},{10,9},{11,1... | collective-permute-start | bytes 589832 | tf_op jit(solution)/shard_map/ppermute | solution.py:337
  155.5 17.6 %collective-permute-start.13 = (bf16[24,4096]{1,0:T(8,128)(2,1)S(1)}, bf16[24,4096]{1,0:T(8,128)(2,1)S(1)}, u32[]{:S(2)}, u32[]{:S(2)}) collective-permute-start(bf16[24,4096]{1,0:T(8,128)(2,1)S(1)} %copy-done.11), channel_id=1, source_target_pairs={{1,0},{2,1},{3,2},{4,3},{5,4},{6,5},{7,6},{8,7},{9,8},{10,9},{11,1... | collective-permute-start | bytes 589832 | tf_op jit(solution)/shard_map/ppermute | solution.py:337
  173.2 0.7 copy-start.9
  176.9 0.7 copy-start.10
  177.6 3.2 %copy-start.5 = (f32[32,4,128]{2,1,0:T(4,128)S(1)}, f32[32,4,128]{2,1,0:T(4,128)}, u32[]{:S(2)}) copy-start(f32[32,4,128]{2,1,0:T(4,128)} %all_to_all.20) | copy-start | bytes 196612

commit v6 on v5

--- a/solution.py
+++ b/solution.py
@@ -388,12 +388,9 @@
         compiler_params=params_of(60 << 20),
         name="pack",
     )(query, key, value, short_taps, decay_rate, residues, long_taps)
-    rims[0] = shift(rims[0], 1)
+    rims = [shift(edge_rows, 1) for edge_rows in rims]
     short_all = gather_own(short)
     poles_parts = ring_own(poles)
-    for chunk in range(1, CHUNKS):
-        edge_rows, _ = lax.optimization_barrier((rims[chunk], short_all))
-        rims[chunk] = shift(edge_rows, 1)
 
     def slot(me_ref, chunk):
         return (me_ref[0] - chunk + owners) % owners

time: 183 us -> 183 us (level)
  no operation moved by 1% of the time
where the time goes in v6:
time: 183 us; the launch traced here: 181 us
  Pallas kernels  81 us (44%)
  starting transfers between devices  69.4 us (38%)
  blocking collectives  14.7 us (8%)
  local copies, waits for them, and re-layouts  6.94 us (4%)
  waiting for transfers between devices  5.19 us (3%)
  other arithmetic  3.08 us (2%)
    pallas_call x9, Pallas kernels, call(): pl.pallas_call(body, out_shape=out_shape, grid_spec=pltpu.PrefetchScalarG...  79.1 us
    ppermute x8, starting transfers between devices, shift(): lax.ppermute(value, AXES, [(at, at + steps) for at in range(first, last)])  28.5 us
    all_to_all x1, blocking collectives, shards(): lax.all_to_all(jnp.broadcast_to(total[None], (ctxs, share, 128)), 'ctx',...  14.7 us
    all_to_all x1, starting transfers between devices, shards(): arrived = lax.all_to_all(states, AXES, 0, 0, tiled=True)  12.2 us
    all_to_all x1, starting transfers between devices, shards(): carried = lax.all_to_all(scanned, AXES, 0, 0, tiled=True)  9.85 us
    all_to_all x1, starting transfers between devices, shards(): lax.all_to_all(mids[-1][2].reshape(ctxs * owners, share, 128), AXES, 0, 0...  9.77 us
    ppermute x6, starting transfers between devices, ring_own(): lax.ppermute(value, 'own', [(at, (at + hop) % count) for at in range(coun...  9.1 us
    unnamed x25, local copies, waits for them, and re-layouts  6.93 us
  transfers between devices with their start and end apart: 17, of which 1 were waited for; matrix products, arithmetic and copies ran while one was open for 2% of the time, Pallas kernels for 42%

profile of v6, /device:TPU:1, one launch (start us, length us, event | category | flops | bytes accessed | tf_op | source)
XLA Modules:
  0.0 181.2 jit_solution(1493642371064156479)
XLA Ops:
  0.6 1.9 %pack.1 = (f32[24,128]{1,0:T(8,128)}, f32[384,128]{1,0:T(8,128)}, bf16[24,4096]{1,0:T(8,128)(2,1)}, bf16[24,4096]{1,0:T(8,128)(2,1)}) custom-call(bf16[128,8192]{1,0:T(8,128)(2,1)} %refs_1_.3, bf16[128,8192]{1,0:T(8,128)(2,1)} %refs_2_.3, bf16[128,8192]{1,0:T(8,128)(2,1)} %refs_3_.3, f32[3,7,128]{2,1,0:T(8,128)} %short.1, f32[8,2048]{1,0:T(8,128)} %rate.1, ...), custom_call_target="tpu_custom_call" | custom-call | tf_op jit(solution)/shard_map/pack/pallas_call | solution.py:373
  2.6 3.6 %collective-permute-start.3 = (f32[24,128]{1,0:T(8,128)}, f32[24,128]{1,0:T(8,128)S(1)}, u32[]{:S(2)}, u32[]{:S(2)}) collective-permute-start(f32[24,128]{1,0:T(8,128)} %get-tuple-element.56), channel_id=1, source_target_pairs={{0,3},{1,0},{2,1},{3,2},{4,7},{5,4},{6,5},{7,6},{8,11},{9,8},{10,9... | collective-permute-start | bytes 36872 | tf_op jit(solution)/shard_map/ppermute | solution.py:348
  6.1 0.3 collective-permute-start.2
  6.5 0.7 collective-permute-start.1
  7.2 3.5 %collective-permute-start.4 = (bf16[24,4096]{1,0:T(8,128)(2,1)}, bf16[24,4096]{1,0:T(8,128)(2,1)S(1)}, u32[]{:S(2)}, u32[]{:S(2)}) collective-permute-start(bf16[24,4096]{1,0:T(8,128)(2,1)} %get-tuple-element.57), channel_id=1, source_target_pairs={{0,1},{1,2},{2,3},{3,4},{4,5},{5,6},{6,7},{7,8},{8,9},{9,10},{10,1... | collective-permute-start | bytes 589832 | tf_op jit(solution)/shard_map/ppermute | solution.py:337
  10.7 3.9 %collective-permute-start.7 = (f32[384,128]{1,0:T(8,128)}, f32[384,128]{1,0:T(8,128)S(1)}, u32[]{:S(2)}, u32[]{:S(2)}) collective-permute-start(f32[384,128]{1,0:T(8,128)} %get-tuple-element.62), channel_id=1, source_target_pairs={{0,3},{1,0},{2,1},{3,2},{4,7},{5,4},{6,5},{7,6},{8,11},{9,8},{10,9... | collective-permute-start | bytes 589832 | tf_op jit(solution)/shard_map/ppermute | solution.py:348
  14.6 0.6 pad_add_fusion.refs_0_
  15.2 0.0 collective-permute-done.3
  15.2 0.0 collective-permute-start.6
  15.2 0.0 collective-permute-done.2
  15.2 0.6 collective-permute-start.5
  15.8 0.0 collective-permute-done.1
  15.8 3.9 %collective-permute-start = (bf16[24,4096]{1,0:T(8,128)(2,1)}, bf16[24,4096]{1,0:T(8,128)(2,1)S(1)}, u32[]{:S(2)}, u32[]{:S(2)}) collective-permute-start(bf16[24,4096]{1,0:T(8,128)(2,1)} %get-tuple-element.55), channel_id=1, source_target_pairs={{0,1},{1,2},{2,3},{3,4},{4,5},{5,6},{6,7},{7,8},{8,9},{9,10},{10,1... | collective-permute-start | bytes 589832 | tf_op jit(solution)/shard_map/ppermute | solution.py:337
  19.8 1.3 pad_maximum_fusion.1.refs_6_
  21.1 0.0 collective-permute-done.4.refs_5_
  21.1 0.7 copy-done.7
  21.8 10.7 %shard_map.218 = (bf16[128,4096]{1,0:T(8,128)(2,1)}, bf16[128,4096]{1,0:T(8,128)(2,1)}, bf16[128,4096]{1,0:T(8,128)(2,1)}, bf16[128,4096]{1,0:T(8,128)(2,1)}, bf...) custom-call(s32[3]{0:T(128)} %pad_add_fusion.refs_0_, bf16[128,8192]{1,0:T(8,128)(2,1)} %refs_1_.3, ...), custom_call_target="tpu_custom_call" | custom-call | flops 2000000000 | bytes 10000000 | tf_op jit(solution)/shard_map/pallas_call | solution.py:430
  32.5 0.0 collective-permute-done.7
  32.5 0.0 collective-permute-done.6
  32.5 0.0 collective-permute-done.5
  32.5 1.9 %collective-permute-start.10 = (bf16[128,4096]{1,0:T(8,128)(2,1)}, bf16[128,4096]{1,0:T(8,128)(2,1)S(1)}, u32[]{:S(2)}, u32[]{:S(2)}) collective-permute-start(bf16[128,4096]{1,0:T(8,128)(2,1)} %get-tuple-element.74.refs_1_), channel_id=1, source_target_pairs={{0,1},{1,2},{2,3},{3,4},{4,5},{5,6},{6,7},{7,8},{8,9},{9,10},{10,1... | collective-permute-start | bytes 3145736 | tf_op jit(solution)/shard_map/ppermute | solution.py:337
  34.4 4.9 %collective-permute-start.11 = (bf16[128,4096]{1,0:T(8,128)(2,1)}, bf16[128,4096]{1,0:T(8,128)(2,1)}, u32[]{:S(2)}, u32[]{:S(2)}) collective-permute-start(bf16[128,4096]{1,0:T(8,128)(2,1)} %get-tuple-element.75.refs_2_), channel_id=1, source_target_pairs={{1,0},{2,1},{3,2},{4,3},{5,4},{6,5},{7,6},{8,7},{9,8},{10,9},{11,1... | collective-permute-start | bytes 3145736 | tf_op jit(solution)/shard_map/ppermute | solution.py:337
  39.3 0.0 copy-done.6
  39.3 1.0 pad_maximum_fusion.refs_10_.refs_11_.refs_5_.refs_6_.refs_7_.refs_2_
  40.2 0.0 collective-permute-done.refs_5_
  40.2 0.7 copy-done.8
  40.9 11.2 %shard_map.219 = (bf16[128,4096]{1,0:T(8,128)(2,1)}, bf16[128,4096]{1,0:T(8,128)(2,1)}, bf16[128,4096]{1,0:T(8,128)(2,1)}, bf16[128,4096]{1,0:T(8,128)(2,1)}, bf...) custom-call(s32[3]{0:T(128)} %pad_add_fusion.refs_0_, ...), custom_call_target="tpu_custom_call" | custom-call | flops 2000000000 | bytes 10000000 | tf_op jit(solution)/shard_map/pallas_call | solution.py:430
  52.1 1.9 %collective-permute-start.8 = (bf16[128,4096]{1,0:T(8,128)(2,1)}, bf16[128,4096]{1,0:T(8,128)(2,1)S(1)}, u32[]{:S(2)}, u32[]{:S(2)}) collective-permute-start(bf16[128,4096]{1,0:T(8,128)(2,1)} %get-tuple-element.72.refs_1_), channel_id=1, source_target_pairs={{0,1},{1,2},{2,3},{3,4},{4,5},{5,6},{6,7},{7,8},{8,9},{9,10},{10,1... | collective-permute-start | bytes 3145736 | tf_op jit(solution)/shard_map/ppermute | solution.py:337
  54.0 4.9 %collective-permute-start.9 = (bf16[128,4096]{1,0:T(8,128)(2,1)}, bf16[128,4096]{1,0:T(8,128)(2,1)S(1)}, u32[]{:S(2)}, u32[]{:S(2)}) collective-permute-start(bf16[128,4096]{1,0:T(8,128)(2,1)} %get-tuple-element.73.refs_2_), channel_id=1, source_target_pairs={{1,0},{2,1},{3,2},{4,3},{5,4},{6,5},{7,6},{8,7},{9,8},{10,9},{11,1... | collective-permute-start | bytes 3145736 | tf_op jit(solution)/shard_map/ppermute | solution.py:337
  58.9 12.2 %all-to-all-start = ((bf16[128,8,128]{2,1,0:T(8,128)(2,1)}), bf16[128,8,128]{2,1,0:T(8,128)(2,1)S(1)}, u32[]{:S(2)}, u32[]{:S(2)}) async-start(bf16[128,8,128]{2,1,0:T(8,128)(2,1)} %bitcast.17), calls=%async_computation | async-start | bytes 524288 | tf_op jit(solution)/shard_map/all_to_all | solution.py:487
  71.0 0.0 collective-permute-done.10.refs_3_
  71.1 0.0 copy-start.2
  71.1 0.0 collective-permute-done.11.refs_4_
  71.1 1.0 copy-done.2
  72.0 12.6 %shard_map.220 = (bf16[256,4096]{1,0:T(8,128)(2,1)}, bf16[256,4096]{1,0:T(8,128)(2,1)}, f32[32,4,4,128]{3,2,1,0:T(4,128)}) custom-call(s32[3]{0:T(128)} %pad_add_fusion.refs_0_, bf16[128,4096]{1,0:T(8,128)(2,1)} %get-tuple-element.74.refs_1_, bf16[128,4096]{1,0:T(8,128)(2,1)} %get-tuple-element.75.refs_2_, bf16[128,4096]{1,0:T(8,128)(2,1)} %copy-done.2, ...), custom_call_target="tpu_custom_call" | custom-call | flops 2000000000 | bytes 10000000 | tf_op jit(solution)/shard_map/pallas_call | solution.py:430
  84.6 5.2 %all-to-all-done.refs_1_ = bf16[128,8,128]{2,1,0:T(8,128)(2,1)S(1)} async-done(((bf16[128,8,128]{2,1,0:T(8,128)(2,1)}), bf16[128,8,128]{2,1,0:T(8,128)(2,1)S(1)}, u32[]{:S(2)}, u32[]{:S(2)}) %all-to-all-start) | async-done | bytes 262176 | tf_op jit(solution)/shard_map/all_to_all | solution.py:487
  89.8 0.7 copy-done.4
  90.5 2.6 %shard_map.221.refs_16_ = bf16[128,8,128]{2,1,0:T(8,128)(2,1)} custom-call(s32[3]{0:T(128)} %pad_add_fusion.refs_0_, bf16[128,8,128]{2,1,0:T(8,128)(2,1)} %copy-done.4, f32[4,384,128]{2,1,0:T(8,128)} %pad_maximum_fusion.refs_10_.refs_11_.refs_5_.refs_6_.refs_7_.refs_2_, f32[32,4,4,128]{3,2,1,0:T(4,128)} %get-tuple-element.76.refs_3_.refs_15_), custom_call_target="tpu_custom_call" | custom-call | flops 200000000 | bytes 1000000 | tf_op jit(solution)/shard_map/pallas_call | solution.py:430
  93.1 9.9 %all-to-all-start.1 = ((bf16[128,8,128]{2,1,0:T(8,128)(2,1)}), bf16[128,8,128]{2,1,0:T(8,128)(2,1)S(1)}, u32[]{:S(2)}, u32[]{:S(2)}) async-start(bf16[128,8,128]{2,1,0:T(8,128)(2,1)} %shard_map.221.refs_16_), calls=%async_computation.1 | async-start | bytes 524288 | tf_op jit(solution)/shard_map/all_to_all | solution.py:587
  103.0 0.0 collective-permute-done.8.refs_3_
  103.0 0.0 copy-start.1
  103.0 0.0 collective-permute-done.9.refs_4_
  103.0 0.9 copy-done.1
  104.0 1.0 copy-done.3
  104.9 12.6 %shard_map.222 = (bf16[256,4096]{1,0:T(8,128)(2,1)}, bf16[256,4096]{1,0:T(8,128)(2,1)}, f32[32,4,4,128]{3,2,1,0:T(4,128)}) custom-call(s32[3]{0:T(128)} %pad_add_fusion.refs_0_, bf16[128,4096]{1,0:T(8,128)(2,1)} %get-tuple-element.72.refs_1_, bf16[128,4096]{1,0:T(8,128)(2,1)} %get-tuple-element.73.refs_2_, ...), custom_call_target="tpu_custom_call", output_to_operand_aliasing={{2}: (15, {})} | custom-call | flops 2000000000 | bytes 10000000 | tf_op jit(solution)/shard_map/pallas_call | solution.py:430
  117.5 0.0 all-to-all-done.1.refs_7_.refs_8_
  117.6 0.0 copy-start
  117.6 9.8 %all-to-all-start.2 = ((f32[128,4,128]{2,1,0:T(4,128)}), f32[128,4,128]{2,1,0:T(4,128)S(1)}, u32[]{:S(2)}, u32[]{:S(2)}) async-start(f32[128,4,128]{2,1,0:T(4,128)} %bitcast.14), calls=%async_computation.2 | async-start | bytes 524288 | tf_op jit(solution)/shard_map/all_to_all | solution.py:599
  127.3 0.0 copy-done
  127.3 11.5 %shard_map.223 = (bf16[128,8192]{1,0:T(8,128)(2,1)}, bf16[128,8192]{1,0:T(8,128)(2,1)}, bf16[128,8192]{1,0:T(8,128)(2,1)}, bf16[128,8192]{1,0:T(8,128)(2,1)}, bf...) custom-call(s32[3]{0:T(128)} %pad_add_fusion.refs_0_, bf16[128,4096]{1,0:T(8,128)(2,1)} %get-tuple-element.80.refs_1_, ...), custom_call_target="tpu_custom_call" | custom-call | flops 2000000000 | bytes 10000000 | tf_op jit(solution)/shard_map/pallas_call | solution.py:430
  138.9 0.0 copy-start.11
  138.9 11.7 %shard_map.224 = (bf16[128,8192]{1,0:T(8,128)(2,1)}, bf16[128,8192]{1,0:T(8,128)(2,1)}, bf16[128,8192]{1,0:T(8,128)(2,1)}, bf16[128,8192]{1,0:T(8,128)(2,1)}, bf...) custom-call(s32[3]{0:T(128)} %pad_add_fusion.refs_0_, ...), custom_call_target="tpu_custom_call", output_to_operand_aliasing={{0}: (15, {}), {1}: (16, {}), {2}: (17, {}), {3}: (18, {})} | custom-call | flops 2000000000 | bytes 10000000 | tf_op jit(solution)/shard_map/pallas_call | solution.py:430
  150.6 4.8 %collective-permute-start.12 = (bf16[24,4096]{1,0:T(8,128)(2,1)}, bf16[24,4096]{1,0:T(8,128)(2,1)S(1)}, u32[]{:S(2)}, u32[]{:S(2)}) collective-permute-start(bf16[24,4096]{1,0:T(8,128)(2,1)} %get-tuple-element.92), channel_id=1, source_target_pairs={{1,0},{2,1},{3,2},{4,3},{5,4},{6,5},{7,6},{8,7},{9,8},{10,9},{11,1... | collective-permute-start | bytes 589832 | tf_op jit(solution)/shard_map/ppermute | solution.py:337
  155.4 2.7 %collective-permute-start.13 = (bf16[24,4096]{1,0:T(8,128)(2,1)S(1)}, bf16[24,4096]{1,0:T(8,128)(2,1)S(1)}, u32[]{:S(2)}, u32[]{:S(2)}) collective-permute-start(bf16[24,4096]{1,0:T(8,128)(2,1)S(1)} %copy-done.11), channel_id=1, source_target_pairs={{1,0},{2,1},{3,2},{4,3},{5,4},{6,5},{7,6},{8,7},{9,8},{10,9},{11,1... | collective-permute-start | bytes 589832 | tf_op jit(solution)/shard_map/ppermute | solution.py:337
  158.1 0.0 all-to-all-done.2
  158.1 0.1 reduce_sum.9
  158.3 14.7 %all_to_all.20 = f32[32,4,128]{2,1,0:T(4,128)} all-to-all(f32[32,4,128]{2,1,0:T(4,128)S(1)} %broadcast_in_dim.2), channel_id=1, replica_groups=mesh['ctx'=32,'own'=4] {'ctx'}, dimensions={0} | all-to-all | bytes 131072 | tf_op jit(solution)/shard_map/all_to_all | solution.py:604
  173.0 0.0 collective-permute-done.13.refs_2_
  173.1 0.7 copy-done.9
  173.7 3.0 %shard_map.225 = (bf16[128,8192]{1,0:T(8,128)(2,1)}, bf16[128,8192]{1,0:T(8,128)(2,1)}, bf16[128,8192]{1,0:T(8,128)(2,1)}) custom-call(s32[3]{0:T(128)} %pad_add_fusion.refs_0_, f32[24,4096]{1,0:T(8,128)} %get-tuple-element.93.refs_1_, bf16[24,4096]{1,0:T(8,128)(2,1)} %copy-done.9, ...), custom_call_target="tpu_custom_call", output_to_operand_aliasing={{0}: (4, {}), {1}: (5, {}), {2}: (6, {})} | custom-call | flops 200000000 | bytes 1000000 | tf_op jit(solution)/shard_map/pallas_call | solution.py:430
  176.7 0.0 collective-permute-done.12.refs_2_
  176.8 0.7 copy-done.10
  177.4 3.2 %shard_map.226 = (bf16[128,8192]{1,0:T(8,128)(2,1)}, bf16[128,8192]{1,0:T(8,128)(2,1)}, bf16[128,8192]{1,0:T(8,128)(2,1)}) custom-call(s32[3]{0:T(128)} %pad_add_fusion.refs_0_, f32[24,4096]{1,0:T(8,128)} %get-tuple-element.91.refs_1_, bf16[24,4096]{1,0:T(8,128)(2,1)} %copy-done.10, ...), custom_call_target="tpu_custom_call", output_to_operand_aliasing={{0}: (4, {}), {1}: (5, {}), {2}: (6, {})} | custom-call | flops 200000000 | bytes 1000000 | tf_op jit(solution)/shard_map/pallas_call | solution.py:430
  180.6 0.6 copy.47
  (12 shorter events, 0.0 us)
Async XLA Ops:
  2.6 12.6 %collective-permute-start.3 = (f32[24,128]{1,0:T(8,128)}, f32[24,128]{1,0:T(8,128)S(1)}, u32[]{:S(2)}, u32[]{:S(2)}) collective-permute-start(f32[24,128]{1,0:T(8,128)} %get-tuple-element.56), channel_id=1, source_target_pairs={{0,3},{1,0},{2,1},{3,2},{4,7},{5,4},{6,5},{7,6},{8,11},{9,8},{10,9... | collective-permute-start | bytes 36872 | tf_op jit(solution)/shard_map/ppermute | solution.py:348
  6.1 9.1 %collective-permute-start.2 = (f32[24,128]{1,0:T(8,128)}, f32[24,128]{1,0:T(8,128)S(1)}, u32[]{:S(2)}, u32[]{:S(2)}) collective-permute-start(f32[24,128]{1,0:T(8,128)} %get-tuple-element.56), channel_id=1, source_target_pairs={{0,2},{1,3},{2,0},{3,1},{4,6},{5,7},{6,4},{7,5},{8,10},{9,11},{10,... | collective-permute-start | bytes 36872 | tf_op jit(solution)/shard_map/ppermute | solution.py:348
  6.5 9.4 %collective-permute-start.1 = (f32[24,128]{1,0:T(8,128)}, f32[24,128]{1,0:T(8,128)S(1)}, u32[]{:S(2)}, u32[]{:S(2)}) collective-permute-start(f32[24,128]{1,0:T(8,128)} %get-tuple-element.56), channel_id=1, source_target_pairs={{0,1},{1,2},{2,3},{3,0},{4,5},{5,6},{6,7},{7,4},{8,9},{9,10},{10,1... | collective-permute-start | bytes 36872 | tf_op jit(solution)/shard_map/ppermute | solution.py:348
  7.2 14.0 %collective-permute-start.4 = (bf16[24,4096]{1,0:T(8,128)(2,1)}, bf16[24,4096]{1,0:T(8,128)(2,1)S(1)}, u32[]{:S(2)}, u32[]{:S(2)}) collective-permute-start(bf16[24,4096]{1,0:T(8,128)(2,1)} %get-tuple-element.57), channel_id=1, source_target_pairs={{0,1},{1,2},{2,3},{3,4},{4,5},{5,6},{6,7},{7,8},{8,9},{9,10},{10,1... | collective-permute-start | bytes 589832 | tf_op jit(solution)/shard_map/ppermute | solution.py:337
  10.7 21.8 %collective-permute-start.7 = (f32[384,128]{1,0:T(8,128)}, f32[384,128]{1,0:T(8,128)S(1)}, u32[]{:S(2)}, u32[]{:S(2)}) collective-permute-start(f32[384,128]{1,0:T(8,128)} %get-tuple-element.62), channel_id=1, source_target_pairs={{0,3},{1,0},{2,1},{3,2},{4,7},{5,4},{6,5},{7,6},{8,11},{9,8},{10,9... | collective-permute-start | bytes 589832 | tf_op jit(solution)/shard_map/ppermute | solution.py:348
  15.2 17.3 %collective-permute-start.6 = (f32[384,128]{1,0:T(8,128)}, f32[384,128]{1,0:T(8,128)S(1)}, u32[]{:S(2)}, u32[]{:S(2)}) collective-permute-start(f32[384,128]{1,0:T(8,128)} %get-tuple-element.62), channel_id=1, source_target_pairs={{0,2},{1,3},{2,0},{3,1},{4,6},{5,7},{6,4},{7,5},{8,10},{9,11},{10,... | collective-permute-start | bytes 589832 | tf_op jit(solution)/shard_map/ppermute | solution.py:348
  15.2 17.3 %collective-permute-start.5 = (f32[384,128]{1,0:T(8,128)}, f32[384,128]{1,0:T(8,128)S(1)}, u32[]{:S(2)}, u32[]{:S(2)}) collective-permute-start(f32[384,128]{1,0:T(8,128)} %get-tuple-element.62), channel_id=1, source_target_pairs={{0,1},{1,2},{2,3},{3,0},{4,5},{5,6},{6,7},{7,4},{8,9},{9,10},{10,1... | collective-permute-start | bytes 589832 | tf_op jit(solution)/shard_map/ppermute | solution.py:348
  15.8 24.4 %collective-permute-start = (bf16[24,4096]{1,0:T(8,128)(2,1)}, bf16[24,4096]{1,0:T(8,128)(2,1)S(1)}, u32[]{:S(2)}, u32[]{:S(2)}) collective-permute-start(bf16[24,4096]{1,0:T(8,128)(2,1)} %get-tuple-element.55), channel_id=1, source_target_pairs={{0,1},{1,2},{2,3},{3,4},{4,5},{5,6},{6,7},{7,8},{8,9},{9,10},{10,1... | collective-permute-start | bytes 589832 | tf_op jit(solution)/shard_map/ppermute | solution.py:337
  21.1 18.2 %copy-start.6 = (f32[384,128]{1,0:T(8,128)S(1)}, f32[384,128]{1,0:T(8,128)}, u32[]{:S(2)}) copy-start(f32[384,128]{1,0:T(8,128)} %get-tuple-element.62) | copy-start | bytes 589828
  21.1 0.7 copy-start.7
  32.5 38.6 %collective-permute-start.10 = (bf16[128,4096]{1,0:T(8,128)(2,1)}, bf16[128,4096]{1,0:T(8,128)(2,1)S(1)}, u32[]{:S(2)}, u32[]{:S(2)}) collective-permute-start(bf16[128,4096]{1,0:T(8,128)(2,1)} %get-tuple-element.74.refs_1_), channel_id=1, source_target_pairs={{0,1},{1,2},{2,3},{3,4},{4,5},{5,6},{6,7},{7,8},{8,9},{9,10},{10,1... | collective-permute-start | bytes 3145736 | tf_op jit(solution)/shard_map/ppermute | solution.py:337
  34.4 36.7 %collective-permute-start.11 = (bf16[128,4096]{1,0:T(8,128)(2,1)}, bf16[128,4096]{1,0:T(8,128)(2,1)}, u32[]{:S(2)}, u32[]{:S(2)}) collective-permute-start(bf16[128,4096]{1,0:T(8,128)(2,1)} %get-tuple-element.75.refs_2_), channel_id=1, source_target_pairs={{1,0},{2,1},{3,2},{4,3},{5,4},{6,5},{7,6},{8,7},{9,8},{10,9},{11,1... | collective-permute-start | bytes 3145736 | tf_op jit(solution)/shard_map/ppermute | solution.py:337
  40.2 0.7 copy-start.8
  52.1 50.9 %collective-permute-start.8 = (bf16[128,4096]{1,0:T(8,128)(2,1)}, bf16[128,4096]{1,0:T(8,128)(2,1)S(1)}, u32[]{:S(2)}, u32[]{:S(2)}) collective-permute-start(bf16[128,4096]{1,0:T(8,128)(2,1)} %get-tuple-element.72.refs_1_), channel_id=1, source_target_pairs={{0,1},{1,2},{2,3},{3,4},{4,5},{5,6},{6,7},{7,8},{8,9},{9,10},{10,1... | collective-permute-start | bytes 3145736 | tf_op jit(solution)/shard_map/ppermute | solution.py:337
  54.0 49.0 %collective-permute-start.9 = (bf16[128,4096]{1,0:T(8,128)(2,1)}, bf16[128,4096]{1,0:T(8,128)(2,1)S(1)}, u32[]{:S(2)}, u32[]{:S(2)}) collective-permute-start(bf16[128,4096]{1,0:T(8,128)(2,1)} %get-tuple-element.73.refs_2_), channel_id=1, source_target_pairs={{1,0},{2,1},{3,2},{4,3},{5,4},{6,5},{7,6},{8,7},{9,8},{10,9},{11,1... | collective-permute-start | bytes 3145736 | tf_op jit(solution)/shard_map/ppermute | solution.py:337
  58.9 30.9 %all-to-all-start = ((bf16[128,8,128]{2,1,0:T(8,128)(2,1)}), bf16[128,8,128]{2,1,0:T(8,128)(2,1)S(1)}, u32[]{:S(2)}, u32[]{:S(2)}) async-start(bf16[128,8,128]{2,1,0:T(8,128)(2,1)} %bitcast.17), calls=%async_computation | async-start | bytes 524288 | tf_op jit(solution)/shard_map/all_to_all | solution.py:487
  71.1 1.0 copy-start.2
  89.8 0.7 copy-start.4
  93.1 24.4 %all-to-all-start.1 = ((bf16[128,8,128]{2,1,0:T(8,128)(2,1)}), bf16[128,8,128]{2,1,0:T(8,128)(2,1)S(1)}, u32[]{:S(2)}, u32[]{:S(2)}) async-start(bf16[128,8,128]{2,1,0:T(8,128)(2,1)} %shard_map.221.refs_16_), calls=%async_computation.1 | async-start | bytes 524288 | tf_op jit(solution)/shard_map/all_to_all | solution.py:587
  103.0 1.0 copy-start.1
  104.0 1.0 copy-start.3
  117.6 9.8 %copy-start = (bf16[128,8,128]{2,1,0:T(8,128)(2,1)}, bf16[128,8,128]{2,1,0:T(8,128)(2,1)S(1)}, u32[]{:S(2)}) copy-start(bf16[128,8,128]{2,1,0:T(8,128)(2,1)S(1)} %all-to-all-done.1.refs_7_.refs_8_) | copy-start | bytes 786436
  117.6 40.6 %all-to-all-start.2 = ((f32[128,4,128]{2,1,0:T(4,128)}), f32[128,4,128]{2,1,0:T(4,128)S(1)}, u32[]{:S(2)}, u32[]{:S(2)}) async-start(f32[128,4,128]{2,1,0:T(4,128)} %bitcast.14), calls=%async_computation.2 | async-start | bytes 524288 | tf_op jit(solution)/shard_map/all_to_all | solution.py:599
  138.9 16.5 %copy-start.11 = (bf16[24,4096]{1,0:T(8,128)(2,1)S(1)}, bf16[24,4096]{1,0:T(8,128)(2,1)}, u32[]{:S(2)}) copy-start(bf16[24,4096]{1,0:T(8,128)(2,1)} %get-tuple-element.94) | copy-start | bytes 589828
  150.6 26.2 %collective-permute-start.12 = (bf16[24,4096]{1,0:T(8,128)(2,1)}, bf16[24,4096]{1,0:T(8,128)(2,1)S(1)}, u32[]{:S(2)}, u32[]{:S(2)}) collective-permute-start(bf16[24,4096]{1,0:T(8,128)(2,1)} %get-tuple-element.92), channel_id=1, source_target_pairs={{1,0},{2,1},{3,2},{4,3},{5,4},{6,5},{7,6},{8,7},{9,8},{10,9},{11,1... | collective-permute-start | bytes 589832 | tf_op jit(solution)/shard_map/ppermute | solution.py:337
  155.4 17.6 %collective-permute-start.13 = (bf16[24,4096]{1,0:T(8,128)(2,1)S(1)}, bf16[24,4096]{1,0:T(8,128)(2,1)S(1)}, u32[]{:S(2)}, u32[]{:S(2)}) collective-permute-start(bf16[24,4096]{1,0:T(8,128)(2,1)S(1)} %copy-done.11), channel_id=1, source_target_pairs={{1,0},{2,1},{3,2},{4,3},{5,4},{6,5},{7,6},{8,7},{9,8},{10,9},{11,1... | collective-permute-start | bytes 589832 | tf_op jit(solution)/shard_map/ppermute | solution.py:337
  173.1 0.7 copy-start.9
  176.8 0.7 copy-start.10
  177.4 3.2 %copy-start.5 = (f32[32,4,128]{2,1,0:T(4,128)S(1)}, f32[32,4,128]{2,1,0:T(4,128)}, u32[]{:S(2)}) copy-start(f32[32,4,128]{2,1,0:T(4,128)} %all_to_all.20) | copy-start | bytes 196612
